TPU v7x, 256 devices: a whole 4x4x8 slice. The times are simulated.
256 devices in a mesh: inl: 8 (over z_lo, core), xln: 8 (over x, z_hi), section: 4 (over y).
Axes of the slice: x: 4, y: 4, z: 8 (z_hi: 2, z_lo: 4; z = z_hi * 4 + z_lo), core: 2. Of those that a mesh axis runs over, the one named last changes fastest.
Arguments:
- skips: bfloat16 [4, 8192, 1024], P('section', ('inl', 'xln')), may hold values from -6 to 6
- deconv_weight: bfloat16 [4, 1024, 1024], P('section'), may hold values from -0.1875 to 0.1875
- norm_gain: float32 [4, 2, 128], P('section'), may hold values from 0.5 to 2
- conv_in: bfloat16 [4, 27, 128, 128], P('section'), may hold values from -0.109375 to 0.109375
- conv_out: bfloat16 [4, 27, 32, 128], P('section'), may hold values from -0.109375 to 0.109375
Outputs:
- features: bfloat16 [32, 32, 2048], P('section', 'inl', 'xln')
All inputs are finite; a program needn't handle non-finite values.
Results may differ from a plain program's by a relative error of at most 0.012.
Values may be sent and summed in bfloat16 or wider, within the bound.
A program may use at most 64 MiB of HBM per device.

v0:
```python
import jax
import jax.numpy as jnp
from jax import lax
from jax.sharding import PartitionSpec as P

PXD = 2
GZ = 8


epsilon = 1e-05


def with_halo(block, sides, width):
    for axis, dim in sides:
        count = lax.axis_size(axis)
        forward = [(i, i + 1) for i in range(count - 1)]
        backward = [(target, source) for source, target in forward]
        low = lax.ppermute(
            lax.slice_in_dim(block, block.shape[dim] - width, None, axis=dim), axis, forward
        )
        high = lax.ppermute(lax.slice_in_dim(block, 0, width, axis=dim), axis, backward)
        block = jnp.concatenate([low, block, high], axis=dim)
    return block


def normalize(values, scale):
    mean_square = jnp.mean(values * values, axis=-1, keepdims=True)
    return values * lax.rsqrt(mean_square + epsilon) * scale


def activate(upsampled, gains):
    width = gains.shape[1]
    shaped = upsampled.reshape(upsampled.shape[:-1] + (upsampled.shape[-1] // width, width))
    result = jax.nn.gelu(normalize(shaped, gains[0]), approximate=True).astype(jnp.bfloat16)
    return result.reshape(upsampled.shape)


def finish(inner, residual_part, gains):
    return jax.nn.gelu(
        normalize(inner, gains[1]) + residual_part.astype(jnp.float32), approximate=True
    ).astype(jnp.bfloat16)


def conv_taps(padded, kernel, out_x, out_y):
    depth = padded.shape[2]
    channels = padded.shape[3]
    deeper = jnp.pad(padded, ((0, 0), (0, 0), (1, 1), (0, 0)))
    total = jnp.zeros((out_x * out_y * depth, kernel.shape[2]), jnp.float32)
    for offset_x in range(3):
        for offset_y in range(3):
            for offset_z in range(3):
                window = deeper[
                    offset_x : offset_x + out_x,
                    offset_y : offset_y + out_y,
                    offset_z : offset_z + depth,
                ]
                total = total + jnp.dot(
                    window.reshape(-1, channels),
                    kernel[(offset_x * 3 + offset_y) * 3 + offset_z],
                    preferred_element_type=jnp.float32,
                )
    return total.reshape(out_x, out_y, depth, kernel.shape[2])


def conv_rows(padded, kernel_rows, out_x, out_y):
    depth = padded.shape[2]
    channels = padded.shape[3]
    deeper = jnp.pad(padded, ((0, 0), (0, 0), (1, 1), (0, 0)))
    total = jnp.zeros((kernel_rows.shape[1], out_x * out_y * depth), jnp.float32)
    for offset_x in range(3):
        for offset_y in range(3):
            for offset_z in range(3):
                window = deeper[
                    offset_x : offset_x + out_x,
                    offset_y : offset_y + out_y,
                    offset_z : offset_z + depth,
                ]
                total = total + lax.dot_general(
                    kernel_rows[(offset_x * 3 + offset_y) * 3 + offset_z],
                    window.reshape(-1, channels),
                    (((1,), (1,)), ((), ())),
                    preferred_element_type=jnp.float32,
                )
    return total.reshape(kernel_rows.shape[1], out_x, out_y * depth)


def local(skips, deconv_weight, norm_gain, conv_in, conv_out):
    inl_size = lax.axis_size("inl")
    tokens_here = skips[0]
    weight = deconv_weight[0]
    gains = norm_gain[0]
    channels = gains.shape[1]
    lines = tokens_here.shape[0] // (inl_size * PXD * GZ)
    cell_x = 2 * PXD
    cell_y = 2 * inl_size * lines
    cell_z = 2 * GZ
    ready = tokens_here.reshape(1, 1, lines, inl_size, PXD * GZ, tokens_here.shape[1])
    moved = lax.all_to_all(
        lax.all_to_all(ready, "inl", split_axis=3, concat_axis=0, tiled=True),
        "xln",
        split_axis=0,
        concat_axis=1,
        tiled=True,
    )
    upsampled = jnp.dot(
        moved.reshape(-1, tokens_here.shape[1]), weight, preferred_element_type=jnp.float32
    )
    brick = activate(upsampled, gains)
    field = (
        brick.reshape(cell_y // 2, PXD, GZ, 2, 2, 2, channels)
        .transpose(1, 3, 0, 4, 2, 5, 6)
        .reshape(cell_x, cell_y, cell_z, channels)
    )
    edged = with_halo(field, (("inl", 0), ("xln", 1)), 1)
    inner = conv_taps(edged, conv_in[0], cell_x, cell_y)
    merged = finish(inner, field, gains)
    padded = with_halo(merged, (("inl", 0), ("xln", 1)), 1)
    kernel_out = conv_out[0]
    return lax.psum_scatter(
        conv_rows(padded, kernel_out, cell_x, cell_y).astype(jnp.bfloat16),
        "section",
        scatter_dimension=0,
        tiled=True,
    )


def solution(mesh):
    return jax.shard_map(
        local,
        mesh=mesh,
        in_specs=(
            P("section", ("inl", "xln"), None),
            P("section", None, None),
            P("section", None, None),
            P("section", None, None, None),
            P("section", None, None, None),
        ),
        out_specs=P("section", "inl", "xln"),
        check_vma=False,
    )
```

profile of v0, /device:TPU:3, one launch (start us, length us, event | category | flops | bytes accessed | tf_op | source)
XLA Modules:
  0.0 154.8 jit_solution(16160873448347274510)
XLA Ops:
  6.5 15.4 %all_to_all.21 = bf16[1,1,1,8,16,1024]{5,4,2,1,0,3:T(8,128)(2,1)} all-to-all(bf16[1,1,1,8,16,1024]{5,4,2,1,0,3:T(8,128)(2,1)} %bitcast.403), channel_id=1, replica_groups=mesh['inl'=8,'xln'=8,'section'=4] {'inl'}, dimensions={3} | all-to-all | bytes 524288 | tf_op jit(solution)/shard_map/all_to_all | solution.py:99
  21.9 8.9 %all-to-all-start.1 = ((bf16[8,1,1,1,16,1024]{5,4,3,2,1,0:T(8,128)(2,1)}), bf16[8,1,1,1,16,1024]{5,4,3,2,1,0:T(8,128)(2,1)S(1)}, u32[]{:S(2)}, u32[]{:S(2)}) async-start(bf16[8,1,1,1,16,1024]{5,4,3,2,1,0:T(8,128)(2,1)} %bitcast.2), calls=%async_computation.1 | async-start | bytes 524288 | tf_op jit(solution)/shard_map/all_to_all | solution.py:98
  30.9 2.9 %copy.13 = bf16[1024,1024]{1,0:T(8,128)(2,1)S(1)} copy(bf16[1024,1024]{0,1:T(8,128)(2,1)} %bitcast.347) | data formatting | bytes 4194304 | tf_op jit(solution)/shard_map/dot_general | solution.py:105
  33.8 5.7 %all-to-all-done.1 = bf16[8,1,1,1,16,1024]{5,4,3,2,1,0:T(8,128)(2,1)S(1)} async-done(((bf16[8,1,1,1,16,1024]{5,4,3,2,1,0:T(8,128)(2,1)}), bf16[8,1,1,1,16,1024]{5,4,3,2,1,0:T(8,128)(2,1)S(1)}, u32[]{:S(2)}, u32[]{:S(2)}) %all-to-all-start.1) | async-done | bytes 262176 | tf_op jit(solution)/shard_map/all_to_all | solution.py:98
  39.5 0.9 multiply_reduce_fusion.1
  40.5 0.3 fusion.37
  40.8 0.3 copy.12
  41.0 6.8 %collective-permute-start = (bf16[1,16,16,128]{3,2,1,0:T(8,128)(2,1)S(1)}, bf16[1,16,16,128]{3,2,1,0:T(8,128)(2,1)S(1)}, u32[]{:S(2)}, u32[]{:S(2)}) collective-permute-start(bf16[1,16,16,128]{3,2,1,0:T(8,128)(2,1)S(1)} %get-tuple-element.67), channel_id=1, source_target_pairs={{0,32},{32,64},{64,96},{96,128},{128,160},{160,192},{192,224},{1,3... | collective-permute-start | bytes 196616 | tf_op jit(solution)/shard_map/ppermute | solution.py:18
  47.8 1.9 %collective-permute-start.1 = (bf16[1,16,16,128]{3,2,1,0:T(8,128)(2,1)S(1)}, bf16[1,16,16,128]{3,2,1,0:T(8,128)(2,1)S(1)}, u32[]{:S(2)}, u32[]{:S(2)}) collective-permute-start(bf16[1,16,16,128]{3,2,1,0:T(8,128)(2,1)S(1)} %get-tuple-element.68), channel_id=1, source_target_pairs={{32,0},{64,32},{96,64},{128,96},{160,128},{192,160},{224,192},{33,... | collective-permute-start | bytes 196616 | tf_op jit(solution)/shard_map/ppermute | solution.py:21
  49.8 3.9 %collective-permute-done.1 = bf16[1,16,16,128]{3,2,1,0:T(8,128)(2,1)S(1)} collective-permute-done((bf16[1,16,16,128]{3,2,1,0:T(8,128)(2,1)S(1)}, bf16[1,16,16,128]{3,2,1,0:T(8,128)(2,1)S(1)}, u32[]{:S(2)}, u32[]{:S(2)}) %collective-permute-start.1) | collective-permute-done | bytes 65568 | tf_op jit(solution)/shard_map/ppermute | solution.py:21
  53.7 2.2 %collective-permute-start.2 = (bf16[6,1,16,128]{3,2,1,0:T(8,128)(2,1)S(1)}, bf16[6,1,16,128]{3,2,1,0:T(8,128)(2,1)S(1)}, u32[]{:S(2)}, u32[]{:S(2)}) collective-permute-start(bf16[6,1,16,128]{3,2,1,0:T(8,128)(2,1)S(1)} %get-tuple-element.59), channel_id=1, source_target_pairs={{0,4},{4,8},{8,12},{12,16},{16,20},{20,24},{24,28},{1,5},{5,9},{9,... | collective-permute-start | bytes 73736 | tf_op jit(solution)/shard_map/ppermute | solution.py:18
  55.9 7.9 %collective-permute-start.3 = (bf16[6,1,16,128]{3,2,1,0:T(8,128)(2,1)S(1)}, bf16[6,1,16,128]{3,2,1,0:T(8,128)(2,1)S(1)}, u32[]{:S(2)}, u32[]{:S(2)}) collective-permute-start(bf16[6,1,16,128]{3,2,1,0:T(8,128)(2,1)S(1)} %get-tuple-element.60), channel_id=1, source_target_pairs={{4,0},{8,4},{12,8},{16,12},{20,16},{24,20},{28,24},{5,1},{9,5},{13... | collective-permute-start | bytes 73736 | tf_op jit(solution)/shard_map/ppermute | solution.py:21
  63.8 0.9 collective-permute-done.3
  64.7 0.4 fusion.25
  65.1 0.8 fusion.173
  65.9 0.4 copy-done
  67.0 0.3 fusion.176
  72.4 0.4 multiply_reduce_fusion
  72.8 0.3 fusion.45
  73.2 2.9 %collective-permute-start.4 = (bf16[1,16,16,128]{3,2,1,0:T(8,128)(2,1)S(1)}, bf16[1,16,16,128]{3,2,1,0:T(8,128)(2,1)S(1)}, u32[]{:S(2)}, u32[]{:S(2)}) collective-permute-start(bf16[1,16,16,128]{3,2,1,0:T(8,128)(2,1)S(1)} %get-tuple-element.63), channel_id=1, source_target_pairs={{0,32},{32,64},{64,96},{96,128},{128,160},{160,192},{192,224},{1,3... | collective-permute-start | bytes 196616 | tf_op jit(solution)/shard_map/ppermute | solution.py:18
  76.1 1.9 %collective-permute-start.5 = (bf16[1,16,16,128]{3,2,1,0:T(8,128)(2,1)S(1)}, bf16[1,16,16,128]{3,2,1,0:T(8,128)(2,1)S(1)}, u32[]{:S(2)}, u32[]{:S(2)}) collective-permute-start(bf16[1,16,16,128]{3,2,1,0:T(8,128)(2,1)S(1)} %get-tuple-element.64), channel_id=1, source_target_pairs={{32,0},{64,32},{96,64},{128,96},{160,128},{192,160},{224,192},{33,... | collective-permute-start | bytes 196616 | tf_op jit(solution)/shard_map/ppermute | solution.py:21
  78.1 3.6 %collective-permute-done.5 = bf16[1,16,16,128]{3,2,1,0:T(8,128)(2,1)S(1)} collective-permute-done((bf16[1,16,16,128]{3,2,1,0:T(8,128)(2,1)S(1)}, bf16[1,16,16,128]{3,2,1,0:T(8,128)(2,1)S(1)}, u32[]{:S(2)}, u32[]{:S(2)}) %collective-permute-start.5) | collective-permute-done | bytes 65568 | tf_op jit(solution)/shard_map/ppermute | solution.py:21
  81.7 7.9 %collective-permute-start.6 = (bf16[6,1,16,128]{3,2,1,0:T(8,128)(2,1)S(1)}, bf16[6,1,16,128]{3,2,1,0:T(8,128)(2,1)S(1)}, u32[]{:S(2)}, u32[]{:S(2)}) collective-permute-start(bf16[6,1,16,128]{3,2,1,0:T(8,128)(2,1)S(1)} %get-tuple-element.55), channel_id=1, source_target_pairs={{0,4},{4,8},{8,12},{12,16},{16,20},{20,24},{24,28},{1,5},{5,9},{9,... | collective-permute-start | bytes 73736 | tf_op jit(solution)/shard_map/ppermute | solution.py:18
  89.6 2.7 %collective-permute-start.7 = (bf16[6,1,16,128]{3,2,1,0:T(8,128)(2,1)S(1)}, bf16[6,1,16,128]{3,2,1,0:T(8,128)(2,1)S(1)}, u32[]{:S(2)}, u32[]{:S(2)}) collective-permute-start(bf16[6,1,16,128]{3,2,1,0:T(8,128)(2,1)S(1)} %get-tuple-element.56), channel_id=1, source_target_pairs={{4,0},{8,4},{12,8},{16,12},{20,16},{24,20},{28,24},{5,1},{9,5},{13... | collective-permute-start | bytes 73736 | tf_op jit(solution)/shard_map/ppermute | solution.py:21
  92.6 5.5 %collective-permute-done.7 = bf16[6,1,16,128]{3,2,1,0:T(8,128)(2,1)S(1)} collective-permute-done((bf16[6,1,16,128]{3,2,1,0:T(8,128)(2,1)S(1)}, bf16[6,1,16,128]{3,2,1,0:T(8,128)(2,1)S(1)}, u32[]{:S(2)}, u32[]{:S(2)}) %collective-permute-start.7) | collective-permute-done | bytes 24608 | tf_op jit(solution)/shard_map/ppermute | solution.py:21
  98.3 0.4 select_maximum_fusion
  98.7 0.8 fusion.172
  102.2 0.4 convolution_add_fusion.27
  105.1 0.7 convert_element_type.30
  105.8 0.6 dynamic-slice
  107.0 39.6 %all-reduce.5.cloned.1.call-done = bf16[32,4,256]{2,1,0:T(4,128)(2,1)} async-done(((bf16[32,4,256]{2,1,0:T(4,128)(2,1)}), bf16[32,4,256]{2,1,0:T(4,128)(2,1)}) %all-reduce.5.cloned.1.call-update) | async-done | bytes 65552
  146.6 1.3 constant_dynamic-slice_fusion
  (79 shorter events, 11.4 us)
Async XLA Ops:
  21.9 17.6 %all-to-all-start.1 = ((bf16[8,1,1,1,16,1024]{5,4,3,2,1,0:T(8,128)(2,1)}), bf16[8,1,1,1,16,1024]{5,4,3,2,1,0:T(8,128)(2,1)S(1)}, u32[]{:S(2)}, u32[]{:S(2)}) async-start(bf16[8,1,1,1,16,1024]{5,4,3,2,1,0:T(8,128)(2,1)} %bitcast.2), calls=%async_computation.1 | async-start | bytes 524288 | tf_op jit(solution)/shard_map/all_to_all | solution.py:98
  30.8 115.8 %all-reduce.5.cloned.1.call-start = ((), (), s32[]{:S(2)}) async-start(), calls=%async_computation.2 | async-start | bytes 131072
  30.9 2.9 %copy-start.2 = (f32[1,2,128]{2,1,0:T(2,128)S(1)}, f32[1,2,128]{2,1,0:T(2,128)}, u32[]{:S(2)}) copy-start(f32[1,2,128]{2,1,0:T(2,128)} %param.7) | copy-start | bytes 3076
  41.0 8.7 %collective-permute-start = (bf16[1,16,16,128]{3,2,1,0:T(8,128)(2,1)S(1)}, bf16[1,16,16,128]{3,2,1,0:T(8,128)(2,1)S(1)}, u32[]{:S(2)}, u32[]{:S(2)}) collective-permute-start(bf16[1,16,16,128]{3,2,1,0:T(8,128)(2,1)S(1)} %get-tuple-element.67), channel_id=1, source_target_pairs={{0,32},{32,64},{64,96},{96,128},{128,160},{160,192},{192,224},{1,3... | collective-permute-start | bytes 196616 | tf_op jit(solution)/shard_map/ppermute | solution.py:18
  47.8 5.8 %collective-permute-start.1 = (bf16[1,16,16,128]{3,2,1,0:T(8,128)(2,1)S(1)}, bf16[1,16,16,128]{3,2,1,0:T(8,128)(2,1)S(1)}, u32[]{:S(2)}, u32[]{:S(2)}) collective-permute-start(bf16[1,16,16,128]{3,2,1,0:T(8,128)(2,1)S(1)} %get-tuple-element.68), channel_id=1, source_target_pairs={{32,0},{64,32},{96,64},{128,96},{160,128},{192,160},{224,192},{33,... | collective-permute-start | bytes 196616 | tf_op jit(solution)/shard_map/ppermute | solution.py:21
  53.7 10.2 %collective-permute-start.2 = (bf16[6,1,16,128]{3,2,1,0:T(8,128)(2,1)S(1)}, bf16[6,1,16,128]{3,2,1,0:T(8,128)(2,1)S(1)}, u32[]{:S(2)}, u32[]{:S(2)}) collective-permute-start(bf16[6,1,16,128]{3,2,1,0:T(8,128)(2,1)S(1)} %get-tuple-element.59), channel_id=1, source_target_pairs={{0,4},{4,8},{8,12},{12,16},{16,20},{20,24},{24,28},{1,5},{5,9},{9,... | collective-permute-start | bytes 73736 | tf_op jit(solution)/shard_map/ppermute | solution.py:18
  55.9 8.8 %collective-permute-start.3 = (bf16[6,1,16,128]{3,2,1,0:T(8,128)(2,1)S(1)}, bf16[6,1,16,128]{3,2,1,0:T(8,128)(2,1)S(1)}, u32[]{:S(2)}, u32[]{:S(2)}) collective-permute-start(bf16[6,1,16,128]{3,2,1,0:T(8,128)(2,1)S(1)} %get-tuple-element.60), channel_id=1, source_target_pairs={{4,0},{8,4},{12,8},{16,12},{20,16},{24,20},{28,24},{5,1},{9,5},{13... | collective-permute-start | bytes 73736 | tf_op jit(solution)/shard_map/ppermute | solution.py:21
  65.1 1.2 copy-start
  72.8 19.6 %copy-start.1 = (bf16[1,27,32,128]{3,2,1,0:T(8,128)(2,1)S(1)}, bf16[1,27,32,128]{3,2,1,0:T(8,128)(2,1)}, u32[]{:S(2)}) copy-start(bf16[1,27,32,128]{3,2,1,0:T(8,128)(2,1)} %param.9) | copy-start | bytes 663556
  73.2 4.9 %collective-permute-start.4 = (bf16[1,16,16,128]{3,2,1,0:T(8,128)(2,1)S(1)}, bf16[1,16,16,128]{3,2,1,0:T(8,128)(2,1)S(1)}, u32[]{:S(2)}, u32[]{:S(2)}) collective-permute-start(bf16[1,16,16,128]{3,2,1,0:T(8,128)(2,1)S(1)} %get-tuple-element.63), channel_id=1, source_target_pairs={{0,32},{32,64},{64,96},{96,128},{128,160},{160,192},{192,224},{1,3... | collective-permute-start | bytes 196616 | tf_op jit(solution)/shard_map/ppermute | solution.py:18
  76.1 5.6 %collective-permute-start.5 = (bf16[1,16,16,128]{3,2,1,0:T(8,128)(2,1)S(1)}, bf16[1,16,16,128]{3,2,1,0:T(8,128)(2,1)S(1)}, u32[]{:S(2)}, u32[]{:S(2)}) collective-permute-start(bf16[1,16,16,128]{3,2,1,0:T(8,128)(2,1)S(1)} %get-tuple-element.64), channel_id=1, source_target_pairs={{32,0},{64,32},{96,64},{128,96},{160,128},{192,160},{224,192},{33,... | collective-permute-start | bytes 196616 | tf_op jit(solution)/shard_map/ppermute | solution.py:21
  81.7 10.9 %collective-permute-start.6 = (bf16[6,1,16,128]{3,2,1,0:T(8,128)(2,1)S(1)}, bf16[6,1,16,128]{3,2,1,0:T(8,128)(2,1)S(1)}, u32[]{:S(2)}, u32[]{:S(2)}) collective-permute-start(bf16[6,1,16,128]{3,2,1,0:T(8,128)(2,1)S(1)} %get-tuple-element.55), channel_id=1, source_target_pairs={{0,4},{4,8},{8,12},{12,16},{16,20},{20,24},{24,28},{1,5},{5,9},{9,... | collective-permute-start | bytes 73736 | tf_op jit(solution)/shard_map/ppermute | solution.py:18
  89.6 8.5 %collective-permute-start.7 = (bf16[6,1,16,128]{3,2,1,0:T(8,128)(2,1)S(1)}, bf16[6,1,16,128]{3,2,1,0:T(8,128)(2,1)S(1)}, u32[]{:S(2)}, u32[]{:S(2)}) collective-permute-start(bf16[6,1,16,128]{3,2,1,0:T(8,128)(2,1)S(1)} %get-tuple-element.56), channel_id=1, source_target_pairs={{4,0},{8,4},{12,8},{16,12},{20,16},{24,20},{28,24},{5,1},{9,5},{13... | collective-permute-start | bytes 73736 | tf_op jit(solution)/shard_map/ppermute | solution.py:21
  104.4 1.3 copy-start.3
Sparse Core Ops, SparseCore 0:
  105.9 40.7 all-reduce.4
where the time goes:
time: 157 us; the launch traced here: 155 us
  waiting for transfers between devices  59.3 us (38%)
  starting transfers between devices  43.2 us (28%)
  blocking collectives  15.4 us (10%)
  between operations  14.5 us (9%)
  matrix products  12.4 us (8%)
  local copies, waits for them, and re-layouts  8.35 us (5%)
  other arithmetic  1.59 us (1%)
    unnamed x2, waiting for transfers between devices  39.6 us
    ppermute x4, starting transfers between devices, with_halo(): lax.ppermute(lax.slice_in_dim(block, block.shape[dim] - width, None, axis...  19.8 us
    all_to_all x1, blocking collectives, local(): lax.all_to_all(ready, 'inl', split_axis=3, concat_axis=0, tiled=True)  15.4 us
    ppermute x4, starting transfers between devices, with_halo(): lax.ppermute(lax.slice_in_dim(block, 0, width, axis=dim), axis, backward)  14.5 us
    ppermute x4, waiting for transfers between devices, with_halo(): lax.ppermute(lax.slice_in_dim(block, 0, width, axis=dim), axis, backward)  13.9 us
    all_to_all x1, starting transfers between devices, local(): lax.all_to_all(lax.all_to_all(ready, 'inl', split_axis=3, concat_axis=0,...  8.93 us
    dot_general x27, matrix products, conv_taps(): jnp.dot(window.reshape(-1, channels), kernel[(offset_x * 3 + offset_y) *...  5.93 us
    all_to_all x1, waiting for transfers between devices, local(): lax.all_to_all(lax.all_to_all(ready, 'inl', split_axis=3, concat_axis=0,...  5.75 us
  transfers between devices with their start and end apart: 10, of which 6 were waited for; matrix products, arithmetic and copies ran while one was open for 2% of the time, Pallas kernels for 0%

commit v1 on v0

--- a/solution.py
+++ b/solution.py
@@ -1,7 +1,13 @@
+import functools
+
 import jax
 import jax.numpy as jnp
 from jax import lax
+from jax.experimental import pallas as pl
+from jax.experimental.pallas import tpu as pltpu
 from jax.sharding import PartitionSpec as P
+
+MESH = pl.DeviceIdType.MESH
 
 PXD = 2
 GZ = 8
@@ -84,6 +90,52 @@
     return total.reshape(kernel_rows.shape[1], out_x, out_y * depth)
 
 
+def reduce_scatter_kernel(count, parts_ref, out_ref, held, send_sem, recv_sem):
+    me = lax.axis_index("section")
+    barrier = pltpu.get_barrier_semaphore()
+    for step in range(1, count):
+        peer = lax.rem(me + step, count)
+        pl.semaphore_signal(barrier, inc=1, device_id={"section": peer}, device_id_type=MESH)
+    pl.semaphore_wait(barrier, count - 1)
+    sends = []
+    for step in range(1, count):
+        peer = lax.rem(me + step, count)
+        copy = pltpu.make_async_remote_copy(
+            src_ref=parts_ref.at[peer],
+            dst_ref=held.at[step],
+            send_sem=send_sem.at[step],
+            recv_sem=recv_sem.at[step],
+            device_id={"section": peer},
+            device_id_type=MESH,
+        )
+        copy.start()
+        sends.append(copy)
+    total = parts_ref[me]
+    for step in range(1, count):
+        sends[step - 1].wait_recv()
+        total = total + held[step]
+    for copy in sends:
+        copy.wait_send()
+    out_ref[...] = total.astype(out_ref.dtype)
+
+
+def reduce_scatter(parts):
+    count = lax.axis_size("section")
+    shaped = parts.reshape((count, parts.shape[0] // count) + parts.shape[1:])
+    return pl.pallas_call(
+        functools.partial(reduce_scatter_kernel, count),
+        out_shape=jax.ShapeDtypeStruct(shaped.shape[1:], jnp.bfloat16),
+        in_specs=[pl.BlockSpec(memory_space=pltpu.VMEM)],
+        out_specs=pl.BlockSpec(memory_space=pltpu.VMEM),
+        scratch_shapes=[
+            pltpu.VMEM(shaped.shape, jnp.float32),
+            pltpu.SemaphoreType.DMA((count,)),
+            pltpu.SemaphoreType.DMA((count,)),
+        ],
+        compiler_params=pltpu.CompilerParams(collective_id=0, has_side_effects=True),
+    )(shaped)
+
+
 def local(skips, deconv_weight, norm_gain, conv_in, conv_out):
     inl_size = lax.axis_size("inl")
     tokens_here = skips[0]
@@ -116,12 +168,7 @@
     merged = finish(inner, field, gains)
     padded = with_halo(merged, (("inl", 0), ("xln", 1)), 1)
     kernel_out = conv_out[0]
-    return lax.psum_scatter(
-        conv_rows(padded, kernel_out, cell_x, cell_y).astype(jnp.bfloat16),
-        "section",
-        scatter_dimension=0,
-        tiled=True,
-    )
+    return reduce_scatter(conv_rows(padded, kernel_out, cell_x, cell_y))
 
 
 def solution(mesh):

time: 157 us -> 110 us (0.70)
  the two profiles are of different devices: /device:TPU:3 before, /device:TPU:1 now
where the time goes in v1:
time: 110 us; the launch traced here: 109 us
  starting transfers between devices  34.8 us (32%)
  waiting for transfers between devices  28.8 us (26%)
  blocking collectives  16.2 us (15%)
  matrix products  12.3 us (11%)
  local copies, waits for them, and re-layouts  7.79 us (7%)
  Pallas kernels  7.32 us (7%)
  other arithmetic  1.6 us (1%)
    ppermute x4, waiting for transfers between devices, with_halo(): lax.ppermute(lax.slice_in_dim(block, 0, width, axis=dim), axis, backward)  21.6 us
    ppermute x4, starting transfers between devices, with_halo(): lax.ppermute(lax.slice_in_dim(block, block.shape[dim] - width, None, axis...  19.7 us
    all_to_all x1, blocking collectives, local(): lax.all_to_all(ready, 'inl', split_axis=3, concat_axis=0, tiled=True)  16.2 us
    all_to_all x1, starting transfers between devices, local(): lax.all_to_all(lax.all_to_all(ready, 'inl', split_axis=3, concat_axis=0,...  8.66 us
    pallas_call x1, Pallas kernels, reduce_scatter(): pl.pallas_call(functools.partial(reduce_scatter_kernel, count), out_shape...  7.32 us
    all_to_all x1, waiting for transfers between devices, local(): lax.all_to_all(lax.all_to_all(ready, 'inl', split_axis=3, concat_axis=0,...  7.24 us
    ppermute x4, starting transfers between devices, with_halo(): lax.ppermute(lax.slice_in_dim(block, 0, width, axis=dim), axis, backward)  6.43 us
    dot_general x27, matrix products, conv_taps(): jnp.dot(window.reshape(-1, channels), kernel[(offset_x * 3 + offset_y) *...  5.84 us
  transfers between devices with their start and end apart: 9, of which 5 were waited for; matrix products, arithmetic and copies ran while one was open for 3% of the time, Pallas kernels for 0%

profile of v1, /device:TPU:1, one launch (start us, length us, event | category | flops | bytes accessed | tf_op | source)
XLA Modules:
  0.0 109.4 jit_solution(15308489404495790255)
XLA Ops:
  0.0 16.2 %all_to_all.21 = bf16[1,1,1,8,16,1024]{5,4,2,1,0,3:T(8,128)(2,1)} all-to-all(bf16[1,1,1,8,16,1024]{5,4,2,1,0,3:T(8,128)(2,1)} %bitcast.400), channel_id=1, replica_groups=mesh['inl'=8,'xln'=8,'section'=4] {'inl'}, dimensions={3} | all-to-all | bytes 524288 | tf_op jit(solution)/shard_map/all_to_all | solution.py:151
  16.2 8.7 %all-to-all-start.1 = ((bf16[8,1,1,1,16,1024]{5,4,3,2,1,0:T(8,128)(2,1)}), bf16[8,1,1,1,16,1024]{5,4,3,2,1,0:T(8,128)(2,1)S(1)}, u32[]{:S(2)}, u32[]{:S(2)}) async-start(bf16[8,1,1,1,16,1024]{5,4,3,2,1,0:T(8,128)(2,1)} %bitcast.2), calls=%async_computation.1 | async-start | bytes 524288 | tf_op jit(solution)/shard_map/all_to_all | solution.py:150
  24.9 2.9 %copy.13 = bf16[1024,1024]{1,0:T(8,128)(2,1)S(1)} copy(bf16[1024,1024]{0,1:T(8,128)(2,1)} %bitcast.344) | data formatting | bytes 4194304 | tf_op jit(solution)/shard_map/dot_general | solution.py:157
  27.8 7.2 %all-to-all-done.1 = bf16[8,1,1,1,16,1024]{5,4,3,2,1,0:T(8,128)(2,1)S(1)} async-done(((bf16[8,1,1,1,16,1024]{5,4,3,2,1,0:T(8,128)(2,1)}), bf16[8,1,1,1,16,1024]{5,4,3,2,1,0:T(8,128)(2,1)S(1)}, u32[]{:S(2)}, u32[]{:S(2)}) %all-to-all-start.1) | async-done | bytes 262176 | tf_op jit(solution)/shard_map/all_to_all | solution.py:150
  35.0 0.9 multiply_reduce_fusion.1
  36.0 0.3 fusion.36
  36.3 0.3 copy.12
  36.6 6.8 %collective-permute-start = (bf16[1,16,16,128]{3,2,1,0:T(8,128)(2,1)S(1)}, bf16[1,16,16,128]{3,2,1,0:T(8,128)(2,1)S(1)}, u32[]{:S(2)}, u32[]{:S(2)}) collective-permute-start(bf16[1,16,16,128]{3,2,1,0:T(8,128)(2,1)S(1)} %get-tuple-element.67), channel_id=1, source_target_pairs={{0,32},{32,64},{64,96},{96,128},{128,160},{160,192},{192,224},{1,3... | collective-permute-start | bytes 196616 | tf_op jit(solution)/shard_map/ppermute | solution.py:24
  43.3 1.9 %collective-permute-start.1 = (bf16[1,16,16,128]{3,2,1,0:T(8,128)(2,1)S(1)}, bf16[1,16,16,128]{3,2,1,0:T(8,128)(2,1)S(1)}, u32[]{:S(2)}, u32[]{:S(2)}) collective-permute-start(bf16[1,16,16,128]{3,2,1,0:T(8,128)(2,1)S(1)} %get-tuple-element.68), channel_id=1, source_target_pairs={{32,0},{64,32},{96,64},{128,96},{160,128},{192,160},{224,192},{33,... | collective-permute-start | bytes 196616 | tf_op jit(solution)/shard_map/ppermute | solution.py:27
  45.3 3.9 %collective-permute-done.1 = bf16[1,16,16,128]{3,2,1,0:T(8,128)(2,1)S(1)} collective-permute-done((bf16[1,16,16,128]{3,2,1,0:T(8,128)(2,1)S(1)}, bf16[1,16,16,128]{3,2,1,0:T(8,128)(2,1)S(1)}, u32[]{:S(2)}, u32[]{:S(2)}) %collective-permute-start.1) | collective-permute-done | bytes 65568 | tf_op jit(solution)/shard_map/ppermute | solution.py:27
  49.2 1.9 %collective-permute-start.2 = (bf16[6,1,16,128]{3,2,1,0:T(8,128)(2,1)S(1)}, bf16[6,1,16,128]{3,2,1,0:T(8,128)(2,1)S(1)}, u32[]{:S(2)}, u32[]{:S(2)}) collective-permute-start(bf16[6,1,16,128]{3,2,1,0:T(8,128)(2,1)S(1)} %get-tuple-element.59), channel_id=1, source_target_pairs={{0,4},{4,8},{8,12},{12,16},{16,20},{20,24},{24,28},{1,5},{5,9},{9,... | collective-permute-start | bytes 73736 | tf_op jit(solution)/shard_map/ppermute | solution.py:24
  51.1 1.3 %collective-permute-start.3 = (bf16[6,1,16,128]{3,2,1,0:T(8,128)(2,1)S(1)}, bf16[6,1,16,128]{3,2,1,0:T(8,128)(2,1)S(1)}, u32[]{:S(2)}, u32[]{:S(2)}) collective-permute-start(bf16[6,1,16,128]{3,2,1,0:T(8,128)(2,1)S(1)} %get-tuple-element.60), channel_id=1, source_target_pairs={{4,0},{8,4},{12,8},{16,12},{20,16},{24,20},{28,24},{5,1},{9,5},{13... | collective-permute-start | bytes 73736 | tf_op jit(solution)/shard_map/ppermute | solution.py:27
  52.4 7.1 %collective-permute-done.3 = bf16[6,1,16,128]{3,2,1,0:T(8,128)(2,1)S(1)} collective-permute-done((bf16[6,1,16,128]{3,2,1,0:T(8,128)(2,1)S(1)}, bf16[6,1,16,128]{3,2,1,0:T(8,128)(2,1)S(1)}, u32[]{:S(2)}, u32[]{:S(2)}) %collective-permute-start.3) | collective-permute-done | bytes 24608 | tf_op jit(solution)/shard_map/ppermute | solution.py:27
  59.5 0.4 fusion.24
  59.9 0.8 fusion.172
  60.7 0.4 copy-done
  61.8 0.3 fusion.175
  62.8 0.2 fusion.1
  67.1 0.4 multiply_reduce_fusion
  67.6 0.3 fusion.44
  67.9 3.3 %collective-permute-start.4 = (bf16[1,16,16,128]{3,2,1,0:T(8,128)(2,1)S(1)}, bf16[1,16,16,128]{3,2,1,0:T(8,128)(2,1)S(1)}, u32[]{:S(2)}, u32[]{:S(2)}) collective-permute-start(bf16[1,16,16,128]{3,2,1,0:T(8,128)(2,1)S(1)} %get-tuple-element.63), channel_id=1, source_target_pairs={{0,32},{32,64},{64,96},{96,128},{128,160},{160,192},{192,224},{1,3... | collective-permute-start | bytes 196616 | tf_op jit(solution)/shard_map/ppermute | solution.py:24
  71.3 1.9 %collective-permute-start.5 = (bf16[1,16,16,128]{3,2,1,0:T(8,128)(2,1)S(1)}, bf16[1,16,16,128]{3,2,1,0:T(8,128)(2,1)S(1)}, u32[]{:S(2)}, u32[]{:S(2)}) collective-permute-start(bf16[1,16,16,128]{3,2,1,0:T(8,128)(2,1)S(1)} %get-tuple-element.64), channel_id=1, source_target_pairs={{32,0},{64,32},{96,64},{128,96},{160,128},{192,160},{224,192},{33,... | collective-permute-start | bytes 196616 | tf_op jit(solution)/shard_map/ppermute | solution.py:27
  73.2 3.6 %collective-permute-done.5 = bf16[1,16,16,128]{3,2,1,0:T(8,128)(2,1)S(1)} collective-permute-done((bf16[1,16,16,128]{3,2,1,0:T(8,128)(2,1)S(1)}, bf16[1,16,16,128]{3,2,1,0:T(8,128)(2,1)S(1)}, u32[]{:S(2)}, u32[]{:S(2)}) %collective-permute-start.5) | collective-permute-done | bytes 65568 | tf_op jit(solution)/shard_map/ppermute | solution.py:27
  76.9 7.8 %collective-permute-start.6 = (bf16[6,1,16,128]{3,2,1,0:T(8,128)(2,1)S(1)}, bf16[6,1,16,128]{3,2,1,0:T(8,128)(2,1)S(1)}, u32[]{:S(2)}, u32[]{:S(2)}) collective-permute-start(bf16[6,1,16,128]{3,2,1,0:T(8,128)(2,1)S(1)} %get-tuple-element.55), channel_id=1, source_target_pairs={{0,4},{4,8},{8,12},{12,16},{16,20},{20,24},{24,28},{1,5},{5,9},{9,... | collective-permute-start | bytes 73736 | tf_op jit(solution)/shard_map/ppermute | solution.py:24
  84.7 1.3 %collective-permute-start.7 = (bf16[6,1,16,128]{3,2,1,0:T(8,128)(2,1)S(1)}, bf16[6,1,16,128]{3,2,1,0:T(8,128)(2,1)S(1)}, u32[]{:S(2)}, u32[]{:S(2)}) collective-permute-start(bf16[6,1,16,128]{3,2,1,0:T(8,128)(2,1)S(1)} %get-tuple-element.56), channel_id=1, source_target_pairs={{4,0},{8,4},{12,8},{16,12},{20,16},{24,20},{28,24},{5,1},{9,5},{13... | collective-permute-start | bytes 73736 | tf_op jit(solution)/shard_map/ppermute | solution.py:27
  86.2 6.9 %collective-permute-done.7 = bf16[6,1,16,128]{3,2,1,0:T(8,128)(2,1)S(1)} collective-permute-done((bf16[6,1,16,128]{3,2,1,0:T(8,128)(2,1)S(1)}, bf16[6,1,16,128]{3,2,1,0:T(8,128)(2,1)S(1)}, u32[]{:S(2)}, u32[]{:S(2)}) %collective-permute-start.7) | collective-permute-done | bytes 24608 | tf_op jit(solution)/shard_map/ppermute | solution.py:27
  93.4 0.4 select_maximum_fusion
  93.7 0.8 fusion.171
  97.2 0.4 convolution_add_fusion.27
  100.1 0.7 reshape_reshape.7.parts_ref
  100.8 7.3 %shard_map.55 = bf16[8,4,256]{2,1,0:T(4,128)(2,1)} custom-call(f32[4,8,4,256]{3,2,1,0:T(4,128)} %reshape_reshape.7.parts_ref), custom_call_target="tpu_custom_call" | custom-call | tf_op jit(solution)/shard_map/pallas_call | solution.py:125
  108.1 1.3 %copy.15 = bf16[8,4,256]{2,1,0:T(4,128)(2,1)} copy(bf16[8,4,256]{2,1,0:T(4,128)(2,1)} %shard_map.55) | data formatting | bytes 32768
  (74 shorter events, 11.0 us)
Async XLA Ops:
  16.2 18.8 %all-to-all-start.1 = ((bf16[8,1,1,1,16,1024]{5,4,3,2,1,0:T(8,128)(2,1)}), bf16[8,1,1,1,16,1024]{5,4,3,2,1,0:T(8,128)(2,1)S(1)}, u32[]{:S(2)}, u32[]{:S(2)}) async-start(bf16[8,1,1,1,16,1024]{5,4,3,2,1,0:T(8,128)(2,1)} %bitcast.2), calls=%async_computation.1 | async-start | bytes 524288 | tf_op jit(solution)/shard_map/all_to_all | solution.py:150
  24.9 2.9 %copy-start.2 = (f32[1,2,128]{2,1,0:T(2,128)S(1)}, f32[1,2,128]{2,1,0:T(2,128)}, u32[]{:S(2)}) copy-start(f32[1,2,128]{2,1,0:T(2,128)} %param.7) | copy-start | bytes 3076
  36.6 8.7 %collective-permute-start = (bf16[1,16,16,128]{3,2,1,0:T(8,128)(2,1)S(1)}, bf16[1,16,16,128]{3,2,1,0:T(8,128)(2,1)S(1)}, u32[]{:S(2)}, u32[]{:S(2)}) collective-permute-start(bf16[1,16,16,128]{3,2,1,0:T(8,128)(2,1)S(1)} %get-tuple-element.67), channel_id=1, source_target_pairs={{0,32},{32,64},{64,96},{96,128},{128,160},{160,192},{192,224},{1,3... | collective-permute-start | bytes 196616 | tf_op jit(solution)/shard_map/ppermute | solution.py:24
  43.3 5.8 %collective-permute-start.1 = (bf16[1,16,16,128]{3,2,1,0:T(8,128)(2,1)S(1)}, bf16[1,16,16,128]{3,2,1,0:T(8,128)(2,1)S(1)}, u32[]{:S(2)}, u32[]{:S(2)}) collective-permute-start(bf16[1,16,16,128]{3,2,1,0:T(8,128)(2,1)S(1)} %get-tuple-element.68), channel_id=1, source_target_pairs={{32,0},{64,32},{96,64},{128,96},{160,128},{192,160},{224,192},{33,... | collective-permute-start | bytes 196616 | tf_op jit(solution)/shard_map/ppermute | solution.py:27
  49.2 3.2 %collective-permute-start.2 = (bf16[6,1,16,128]{3,2,1,0:T(8,128)(2,1)S(1)}, bf16[6,1,16,128]{3,2,1,0:T(8,128)(2,1)S(1)}, u32[]{:S(2)}, u32[]{:S(2)}) collective-permute-start(bf16[6,1,16,128]{3,2,1,0:T(8,128)(2,1)S(1)} %get-tuple-element.59), channel_id=1, source_target_pairs={{0,4},{4,8},{8,12},{12,16},{16,20},{20,24},{24,28},{1,5},{5,9},{9,... | collective-permute-start | bytes 73736 | tf_op jit(solution)/shard_map/ppermute | solution.py:24
  51.1 8.5 %collective-permute-start.3 = (bf16[6,1,16,128]{3,2,1,0:T(8,128)(2,1)S(1)}, bf16[6,1,16,128]{3,2,1,0:T(8,128)(2,1)S(1)}, u32[]{:S(2)}, u32[]{:S(2)}) collective-permute-start(bf16[6,1,16,128]{3,2,1,0:T(8,128)(2,1)S(1)} %get-tuple-element.60), channel_id=1, source_target_pairs={{4,0},{8,4},{12,8},{16,12},{20,16},{24,20},{28,24},{5,1},{9,5},{13... | collective-permute-start | bytes 73736 | tf_op jit(solution)/shard_map/ppermute | solution.py:27
  59.9 1.2 %copy-start = (bf16[1,27,128,128]{3,2,1,0:T(8,128)(2,1)S(1)}, bf16[1,27,128,128]{3,2,1,0:T(8,128)(2,1)}, u32[]{:S(2)}) copy-start(bf16[1,27,128,128]{3,2,1,0:T(8,128)(2,1)} %param.8) | copy-start | bytes 2654212
  67.6 18.4 %copy-start.1 = (bf16[1,27,32,128]{3,2,1,0:T(8,128)(2,1)S(1)}, bf16[1,27,32,128]{3,2,1,0:T(8,128)(2,1)}, u32[]{:S(2)}) copy-start(bf16[1,27,32,128]{3,2,1,0:T(8,128)(2,1)} %param.9) | copy-start | bytes 663556
  67.9 5.3 %collective-permute-start.4 = (bf16[1,16,16,128]{3,2,1,0:T(8,128)(2,1)S(1)}, bf16[1,16,16,128]{3,2,1,0:T(8,128)(2,1)S(1)}, u32[]{:S(2)}, u32[]{:S(2)}) collective-permute-start(bf16[1,16,16,128]{3,2,1,0:T(8,128)(2,1)S(1)} %get-tuple-element.63), channel_id=1, source_target_pairs={{0,32},{32,64},{64,96},{96,128},{128,160},{160,192},{192,224},{1,3... | collective-permute-start | bytes 196616 | tf_op jit(solution)/shard_map/ppermute | solution.py:24
  71.3 5.6 %collective-permute-start.5 = (bf16[1,16,16,128]{3,2,1,0:T(8,128)(2,1)S(1)}, bf16[1,16,16,128]{3,2,1,0:T(8,128)(2,1)S(1)}, u32[]{:S(2)}, u32[]{:S(2)}) collective-permute-start(bf16[1,16,16,128]{3,2,1,0:T(8,128)(2,1)S(1)} %get-tuple-element.64), channel_id=1, source_target_pairs={{32,0},{64,32},{96,64},{128,96},{160,128},{192,160},{224,192},{33,... | collective-permute-start | bytes 196616 | tf_op jit(solution)/shard_map/ppermute | solution.py:27
  76.9 9.3 %collective-permute-start.6 = (bf16[6,1,16,128]{3,2,1,0:T(8,128)(2,1)S(1)}, bf16[6,1,16,128]{3,2,1,0:T(8,128)(2,1)S(1)}, u32[]{:S(2)}, u32[]{:S(2)}) collective-permute-start(bf16[6,1,16,128]{3,2,1,0:T(8,128)(2,1)S(1)} %get-tuple-element.55), channel_id=1, source_target_pairs={{0,4},{4,8},{8,12},{12,16},{16,20},{20,24},{24,28},{1,5},{5,9},{9,... | collective-permute-start | bytes 73736 | tf_op jit(solution)/shard_map/ppermute | solution.py:24
  84.7 8.5 %collective-permute-start.7 = (bf16[6,1,16,128]{3,2,1,0:T(8,128)(2,1)S(1)}, bf16[6,1,16,128]{3,2,1,0:T(8,128)(2,1)S(1)}, u32[]{:S(2)}, u32[]{:S(2)}) collective-permute-start(bf16[6,1,16,128]{3,2,1,0:T(8,128)(2,1)S(1)} %get-tuple-element.56), channel_id=1, source_target_pairs={{4,0},{8,4},{12,8},{16,12},{20,16},{24,20},{28,24},{5,1},{9,5},{13... | collective-permute-start | bytes 73736 | tf_op jit(solution)/shard_map/ppermute | solution.py:27

commit v2 on v1

--- a/solution.py
+++ b/solution.py
@@ -136,6 +136,87 @@
     )(shaped)
 
 
+DIRECTIONS = [(dx, dy) for dx in (-1, 0, 1) for dy in (-1, 0, 1) if (dx, dy) != (0, 0)]
+
+
+def halo_span(step, size):
+    if step < 0:
+        return (0, 1), (size + 1, size + 2)
+    if step > 0:
+        return (size - 1, size), (0, 1)
+    return (0, size), (1, size + 1)
+
+
+def halo_kernel(field_ref, out_ref, held, send_sem, recv_sem):
+    nx, ny = field_ref.shape[0], field_ref.shape[1]
+    count_x, count_y = lax.axis_size("inl"), lax.axis_size("xln")
+    me_x, me_y = lax.axis_index("inl"), lax.axis_index("xln")
+    barrier = pltpu.get_barrier_semaphore()
+    for dx, dy in DIRECTIONS:
+        pl.semaphore_signal(
+            barrier,
+            inc=1,
+            device_id={"inl": lax.rem(me_x + dx + count_x, count_x), "xln": lax.rem(me_y + dy + count_y, count_y)},
+            device_id_type=MESH,
+        )
+    pl.semaphore_wait(barrier, len(DIRECTIONS))
+    copies = []
+    for index, (dx, dy) in enumerate(DIRECTIONS):
+        (sx0, sx1), (tx0, tx1) = halo_span(dx, nx)
+        (sy0, sy1), (ty0, ty1) = halo_span(dy, ny)
+        to_x, to_y = me_x + dx, me_y + dy
+        copy = pltpu.make_async_remote_copy(
+            src_ref=field_ref.at[sx0:sx1, sy0:sy1],
+            dst_ref=held.at[tx0:tx1, ty0:ty1],
+            send_sem=send_sem.at[index],
+            recv_sem=recv_sem.at[index],
+            device_id={"inl": to_x, "xln": to_y},
+            device_id_type=MESH,
+        )
+        sends = (to_x >= 0) & (to_x < count_x) & (to_y >= 0) & (to_y < count_y)
+        from_x, from_y = me_x - dx, me_y - dy
+        gets = (from_x >= 0) & (from_x < count_x) & (from_y >= 0) & (from_y < count_y)
+
+        @pl.when(sends)
+        def _():
+            copy.start()
+
+        @pl.when(jnp.logical_not(gets))
+        def _():
+            held[tx0:tx1, ty0:ty1] = jnp.zeros((tx1 - tx0, ty1 - ty0) + held.shape[2:], held.dtype)
+
+        copies.append((copy, sends, gets))
+    held[1 : nx + 1, 1 : ny + 1] = field_ref[...]
+    for copy, sends, gets in copies:
+
+        @pl.when(gets)
+        def _():
+            copy.wait_recv()
+
+        @pl.when(sends)
+        def _():
+            copy.wait_send()
+
+    out_ref[...] = held[...]
+
+
+def exchange_halo(field, collective):
+    nx, ny = field.shape[0], field.shape[1]
+    shape = (nx + 2, ny + 2) + field.shape[2:]
+    return pl.pallas_call(
+        halo_kernel,
+        out_shape=jax.ShapeDtypeStruct(shape, field.dtype),
+        in_specs=[pl.BlockSpec(memory_space=pltpu.VMEM)],
+        out_specs=pl.BlockSpec(memory_space=pltpu.VMEM),
+        scratch_shapes=[
+            pltpu.VMEM(shape, field.dtype),
+            pltpu.SemaphoreType.DMA((len(DIRECTIONS),)),
+            pltpu.SemaphoreType.DMA((len(DIRECTIONS),)),
+        ],
+        compiler_params=pltpu.CompilerParams(collective_id=collective, has_side_effects=True),
+    )(field)
+
+
 def local(skips, deconv_weight, norm_gain, conv_in, conv_out):
     inl_size = lax.axis_size("inl")
     tokens_here = skips[0]
@@ -163,10 +244,10 @@
         .transpose(1, 3, 0, 4, 2, 5, 6)
         .reshape(cell_x, cell_y, cell_z, channels)
     )
-    edged = with_halo(field, (("inl", 0), ("xln", 1)), 1)
+    edged = exchange_halo(field, 1)
     inner = conv_taps(edged, conv_in[0], cell_x, cell_y)
     merged = finish(inner, field, gains)
-    padded = with_halo(merged, (("inl", 0), ("xln", 1)), 1)
+    padded = exchange_halo(merged, 2)
     kernel_out = conv_out[0]
     return reduce_scatter(conv_rows(padded, kernel_out, cell_x, cell_y))
 

time: 110 us -> 91.5 us (0.83)
  the two profiles are of different devices: /device:TPU:1 before, /device:TPU:3 now
where the time goes in v2:
time: 91.5 us; the launch traced here: 90.2 us
  Pallas kernels  33.6 us (37%)
  blocking collectives  15.4 us (17%)
  local copies, waits for them, and re-layouts  12.6 us (14%)
  matrix products  12.2 us (13%)
  starting transfers between devices  8.92 us (10%)
  waiting for transfers between devices  5.75 us (6%)
  other arithmetic  1.3 us (1%)
    pallas_call x2, Pallas kernels, exchange_halo(): pl.pallas_call(halo_kernel, out_shape=jax.ShapeDtypeStruct(shape, field.d...  25.8 us
    all_to_all x1, blocking collectives, local(): lax.all_to_all(ready, 'inl', split_axis=3, concat_axis=0, tiled=True)  15.4 us
    all_to_all x1, starting transfers between devices, local(): lax.all_to_all(lax.all_to_all(ready, 'inl', split_axis=3, concat_axis=0,...  8.92 us
    pallas_call x1, Pallas kernels, reduce_scatter(): pl.pallas_call(functools.partial(reduce_scatter_kernel, count), out_shape...  7.82 us
    dot_general x27, matrix products, conv_taps(): jnp.dot(window.reshape(-1, channels), kernel[(offset_x * 3 + offset_y) *...  5.84 us
    all_to_all x1, waiting for transfers between devices, local(): lax.all_to_all(lax.all_to_all(ready, 'inl', split_axis=3, concat_axis=0,...  5.75 us
    dot_general x27, matrix products, conv_rows(): lax.dot_general(kernel_rows[(offset_x * 3 + offset_y) * 3 + offset_z], wi...  5.43 us
    slice x2, local copies, waits for them, and re-layouts, conv_taps(): deeper[offset_x:offset_x + out_x, offset_y:offset_y + out_y, offset_z:off...  3.28 us
  transfers between devices with their start and end apart: 1, of which 1 were waited for; matrix products, arithmetic and copies ran while one was open for 3% of the time, Pallas kernels for 0%

profile of v2, /device:TPU:3, one launch (start us, length us, event | category | flops | bytes accessed | tf_op | source)
XLA Modules:
  0.0 90.2 jit_solution(16508014770005586314)
XLA Ops:
  0.0 15.4 %all_to_all.21 = bf16[1,1,1,8,16,1024]{5,4,2,1,0,3:T(8,128)(2,1)} all-to-all(bf16[1,1,1,8,16,1024]{5,4,2,1,0,3:T(8,128)(2,1)} %bitcast.397), channel_id=1, replica_groups=mesh['inl'=8,'xln'=8,'section'=4] {'inl'}, dimensions={3} | all-to-all | bytes 524288 | tf_op jit(solution)/shard_map/all_to_all | solution.py:232
  15.4 8.9 %all-to-all-start.1 = ((bf16[8,1,1,1,16,1024]{5,4,3,2,1,0:T(8,128)(2,1)}), bf16[8,1,1,1,16,1024]{5,4,3,2,1,0:T(8,128)(2,1)S(1)}, u32[]{:S(2)}, u32[]{:S(2)}) async-start(bf16[8,1,1,1,16,1024]{5,4,3,2,1,0:T(8,128)(2,1)} %bitcast.2), calls=%async_computation.1 | async-start | bytes 524288 | tf_op jit(solution)/shard_map/all_to_all | solution.py:231
  24.3 2.9 %copy.11 = bf16[1024,1024]{1,0:T(8,128)(2,1)S(1)} copy(bf16[1024,1024]{0,1:T(8,128)(2,1)} %bitcast.339) | data formatting | bytes 4194304 | tf_op jit(solution)/shard_map/dot_general | solution.py:238
  27.2 5.8 %all-to-all-done.1 = bf16[8,1,1,1,16,1024]{5,4,3,2,1,0:T(8,128)(2,1)S(1)} async-done(((bf16[8,1,1,1,16,1024]{5,4,3,2,1,0:T(8,128)(2,1)}), bf16[8,1,1,1,16,1024]{5,4,3,2,1,0:T(8,128)(2,1)S(1)}, u32[]{:S(2)}, u32[]{:S(2)}) %all-to-all-start.1) | async-done | bytes 262176 | tf_op jit(solution)/shard_map/all_to_all | solution.py:231
  33.0 0.9 %multiply_reduce_fusion.1 = (f32[128,8]{0,1:T(8,128)S(1)}, f32[128,8,128]{2,0,1:T(8,128)S(1)}) fusion(bf16[128,1024,1]{1,0,2:T(8,128)(2,1)S(1)} %bitcast.396, bf16[8,128,1024]{2,1,0:T(8,128)(2,1)S(1)} %bitcast.336), kind=kOutput, calls=%fused_computation.118 | convolution fusion | flops 268696576 | bytes 2887680 | tf_op jit(solution)/shard_map/dot_general | solution.py:238
  33.9 0.3 fusion.18
  34.2 1.0 %copy.10 = bf16[8,2,8,2,2,2,128]{6,5,2,4,0,3,1:T(2,128)(2,1)} copy(bf16[8,2,8,2,2,2,128]{6,2,1,0,5,4,3:T(8,128)(2,1)S(1)} %bitcast.395) | data formatting | bytes 524288 | tf_op jit(solution)/shard_map/reshape;reshape | solution.py:243
  35.2 13.8 %shard_map.55 = bf16[6,18,16,128]{3,2,1,0:T(8,128)(2,1)} custom-call(bf16[4,16,16,128]{3,2,1,0:T(8,128)(2,1)} %bitcast.337), custom_call_target="tpu_custom_call" | custom-call | tf_op jit(solution)/shard_map/pallas_call | solution.py:206
  49.0 2.3 %fusion.138 = (bf16[4,16,16,128]{3,2,1,0:T(8,128)(2,1)S(1)}, bf16[4,16,16,128]{3,2,1,0:T(8,128)(2,1)S(1)}, bf16[4,16,16,128]{3,2,1,0:T(8,128)(2,1)S(1)}, bf16[4,...) fusion(bf16[6,18,16,128]{3,2,1,0:T(8,128)(2,1)} %shard_map.55), kind=kLoop, calls=%fused_computation.234 | loop fusion | bytes 4374528 | tf_op jit(solution)/shard_map/slice | solution.py:58
  51.3 1.0 %pad_slice_fusion.18 = (bf16[4,16,16,128]{3,2,1,0:T(8,128)(2,1)S(1)}, bf16[4,16,16,128]{3,2,1,0:T(8,128)(2,1)S(1)}, bf16[4,16,16,128]{3,2,1,0:T(8,128)(2,1)S(1)}...) fusion(bf16[6,18,16,128]{3,2,1,0:T(8,128)(2,1)S(1)} %copy-done.1), kind=kLoop, calls=%fused_computation.44 | loop fusion | bytes 5947392 | tf_op jit(solution)/shard_map/slice | solution.py:58
  52.7 0.2 convolution_add_fusion.25
  52.9 0.2 convolution_add_fusion.24
  53.1 0.2 convolution_add_fusion.23
  53.3 0.2 convolution_add_fusion.22
  53.6 0.2 convolution_add_fusion.21
  53.8 0.2 convolution_add_fusion.20
  54.0 0.2 convolution_add_fusion.19
  54.4 0.2 convolution_add_fusion.17
  54.6 0.2 convolution_add_fusion.16
  54.9 0.2 convolution_add_fusion.15
  55.1 0.2 convolution_add_fusion.14
  55.3 0.2 convolution_add_fusion.13
  55.5 0.2 convolution_add_fusion.12
  58.1 0.4 multiply_reduce_fusion
  58.7 1.0 %fusion.26.field_ref = bf16[4,16,16,128]{3,2,1,0:T(8,128)(2,1)} fusion(bf16[4,16,16,128]{3,2,1,0:T(8,128)(2,1)S(1)} %bitcast.338, f32[4,16,16,128]{3,2,1,0:T(8,128)S(1)} %bitcast.340, f32[128]{0:T(128)S(1)} %get-tuple-element.59, f32[4,16,16]{2,1,0:T(8,128)S(1)} %rsqrt.21), kind=kLoop, calls=%fused_computation.116 | loop fusion | flops 1703936 | bytes 1053184 | tf_op jit(solution)/shard_map/convert_element_type | solution.py:47
  59.7 11.9 %shard_map.56 = bf16[6,18,16,128]{3,2,1,0:T(8,128)(2,1)} custom-call(bf16[4,16,16,128]{3,2,1,0:T(8,128)(2,1)} %fusion.26.field_ref), custom_call_target="tpu_custom_call" | custom-call | tf_op jit(solution)/shard_map/pallas_call | solution.py:206
  71.6 2.3 %fusion.137 = (bf16[4,16,16,128]{3,2,1,0:T(8,128)(2,1)S(1)}, bf16[4,16,16,128]{3,2,1,0:T(8,128)(2,1)S(1)}, bf16[4,16,16,128]{3,2,1,0:T(8,128)(2,1)S(1)}, bf16[4,...) fusion(bf16[6,18,16,128]{3,2,1,0:T(8,128)(2,1)} %shard_map.56), kind=kLoop, calls=%fused_computation.233 | loop fusion | bytes 4374528 | tf_op jit(solution)/shard_map/slice | solution.py:79
  73.9 0.9 %pad_slice_fusion.6 = (bf16[4,16,16,128]{3,2,1,0:T(8,128)(2,1)S(1)}, bf16[4,16,16,128]{3,2,1,0:T(8,128)(2,1)S(1)}, bf16[4,16,16,128]{3,2,1,0:T(8,128)(2,1)S(1)},...) fusion(bf16[6,18,16,128]{3,2,1,0:T(8,128)(2,1)S(1)} %copy-done), kind=kLoop, calls=%fused_computation.32 | loop fusion | bytes 5947392 | tf_op jit(solution)/shard_map/slice | solution.py:79
  80.0 0.2 fusion.9
  80.3 0.7 reshape_reshape.7.parts_ref
  81.0 7.8 %shard_map.57 = bf16[8,4,256]{2,1,0:T(4,128)(2,1)} custom-call(f32[4,8,4,256]{3,2,1,0:T(4,128)} %reshape_reshape.7.parts_ref), custom_call_target="tpu_custom_call" | custom-call | tf_op jit(solution)/shard_map/pallas_call | solution.py:125
  88.8 1.3 %copy.13 = bf16[8,4,256]{2,1,0:T(4,128)(2,1)} copy(bf16[8,4,256]{2,1,0:T(4,128)(2,1)} %shard_map.57) | data formatting | bytes 32768
  (55 shorter events, 8.2 us)
Async XLA Ops:
  15.4 17.6 %all-to-all-start.1 = ((bf16[8,1,1,1,16,1024]{5,4,3,2,1,0:T(8,128)(2,1)}), bf16[8,1,1,1,16,1024]{5,4,3,2,1,0:T(8,128)(2,1)S(1)}, u32[]{:S(2)}, u32[]{:S(2)}) async-start(bf16[8,1,1,1,16,1024]{5,4,3,2,1,0:T(8,128)(2,1)} %bitcast.2), calls=%async_computation.1 | async-start | bytes 524288 | tf_op jit(solution)/shard_map/all_to_all | solution.py:231
  24.3 2.9 %copy-start.5 = (f32[1,2,128]{2,1,0:T(2,128)S(1)}, f32[1,2,128]{2,1,0:T(2,128)}, u32[]{:S(2)}) copy-start(f32[1,2,128]{2,1,0:T(2,128)} %param.7) | copy-start | bytes 3076
  49.0 2.3 %copy-start.1 = (bf16[6,18,16,128]{3,2,1,0:T(8,128)(2,1)S(1)}, bf16[6,18,16,128]{3,2,1,0:T(8,128)(2,1)}, u32[]{:S(2)}) copy-start(bf16[6,18,16,128]{3,2,1,0:T(8,128)(2,1)} %shard_map.55) | copy-start | bytes 1327108
  51.3 1.2 %copy-start.3 = (bf16[1,27,128,128]{3,2,1,0:T(8,128)(2,1)S(1)}, bf16[1,27,128,128]{3,2,1,0:T(8,128)(2,1)}, u32[]{:S(2)}) copy-start(bf16[1,27,128,128]{3,2,1,0:T(8,128)(2,1)} %param.8) | copy-start | bytes 2654212
  57.7 1.0 %copy-start.2 = (bf16[8,2,8,2,2,2,128]{6,5,2,4,0,3,1:T(2,128)(2,1)S(1)}, bf16[8,2,8,2,2,2,128]{6,5,2,4,0,3,1:T(2,128)(2,1)}, u32[]{:S(2)}) copy-start(bf16[8,2,8,2,2,2,128]{6,5,2,4,0,3,1:T(2,128)(2,1)} %copy.10) | copy-start | bytes 786436
  71.6 2.3 %copy-start = (bf16[6,18,16,128]{3,2,1,0:T(8,128)(2,1)S(1)}, bf16[6,18,16,128]{3,2,1,0:T(8,128)(2,1)}, u32[]{:S(2)}) copy-start(bf16[6,18,16,128]{3,2,1,0:T(8,128)(2,1)} %shard_map.56) | copy-start | bytes 1327108
  73.9 1.0 %copy-start.4 = (bf16[1,27,32,128]{3,2,1,0:T(8,128)(2,1)S(1)}, bf16[1,27,32,128]{3,2,1,0:T(8,128)(2,1)}, u32[]{:S(2)}) copy-start(bf16[1,27,32,128]{3,2,1,0:T(8,128)(2,1)} %param.9) | copy-start | bytes 663556

commit v3 on v2

--- a/solution.py
+++ b/solution.py
@@ -217,6 +217,85 @@
     )(field)
 
 
+def gather_kernel(tokens_ref, out_ref, held, send_sem, recv_sem):
+    count = lax.axis_size("inl")
+    me_x, me_y = lax.axis_index("inl"), lax.axis_index("xln")
+    rows = tokens_ref.shape[0] // count
+    diagonal = me_x == me_y
+    barrier = pltpu.get_barrier_semaphore()
+    for other in range(count):
+        for target in ({"inl": other, "xln": me_x}, {"inl": me_y, "xln": other}):
+
+            @pl.when((target["inl"] != me_x) | (target["xln"] != me_y))
+            def _():
+                pl.semaphore_signal(barrier, inc=1, device_id=target, device_id_type=MESH)
+
+    pl.semaphore_wait(barrier, 2 * count - 2 * diagonal.astype(jnp.int32))
+    copies = []
+    for other in range(count):
+        copy = pltpu.make_async_remote_copy(
+            src_ref=tokens_ref.at[pl.ds(other * rows, rows)],
+            dst_ref=held.at[me_y],
+            send_sem=send_sem.at[other],
+            recv_sem=recv_sem.at[me_y],
+            device_id={"inl": other, "xln": me_x},
+            device_id_type=MESH,
+        )
+        to_self = (other == me_x) & diagonal
+
+        @pl.when(jnp.logical_not(to_self))
+        def _():
+            copy.start()
+
+        copies.append((copy, to_self))
+    for source in range(count):
+        incoming = pltpu.make_async_remote_copy(
+            src_ref=tokens_ref.at[pl.ds(0, rows)],
+            dst_ref=held.at[source],
+            send_sem=send_sem.at[source],
+            recv_sem=recv_sem.at[source],
+            device_id={"inl": me_y, "xln": source},
+            device_id_type=MESH,
+        )
+        from_self = (source == me_y) & diagonal
+
+        @pl.when(jnp.logical_not(from_self))
+        def _():
+            incoming.wait_recv()
+
+        @pl.when(from_self)
+        def _():
+            out_ref[source] = tokens_ref[pl.ds(pl.multiple_of(me_x * rows, rows), rows)]
+
+        @pl.when(jnp.logical_not(from_self))
+        def _():
+            out_ref[source] = held[source]
+
+    for copy, to_self in copies:
+
+        @pl.when(jnp.logical_not(to_self))
+        def _():
+            copy.wait_send()
+
+
+def gather_bricks(tokens):
+    count = lax.axis_size("inl")
+    rows = tokens.shape[0] // count
+    shape = (lax.axis_size("xln"), rows, tokens.shape[1])
+    return pl.pallas_call(
+        gather_kernel,
+        out_shape=jax.ShapeDtypeStruct(shape, tokens.dtype),
+        in_specs=[pl.BlockSpec(memory_space=pltpu.VMEM)],
+        out_specs=pl.BlockSpec(memory_space=pltpu.VMEM),
+        scratch_shapes=[
+            pltpu.VMEM(shape, tokens.dtype),
+            pltpu.SemaphoreType.DMA((count,)),
+            pltpu.SemaphoreType.DMA((count,)),
+        ],
+        compiler_params=pltpu.CompilerParams(collective_id=3, has_side_effects=True),
+    )(tokens)
+
+
 def local(skips, deconv_weight, norm_gain, conv_in, conv_out):
     inl_size = lax.axis_size("inl")
     tokens_here = skips[0]
@@ -227,14 +306,7 @@
     cell_x = 2 * PXD
     cell_y = 2 * inl_size * lines
     cell_z = 2 * GZ
-    ready = tokens_here.reshape(1, 1, lines, inl_size, PXD * GZ, tokens_here.shape[1])
-    moved = lax.all_to_all(
-        lax.all_to_all(ready, "inl", split_axis=3, concat_axis=0, tiled=True),
-        "xln",
-        split_axis=0,
-        concat_axis=1,
-        tiled=True,
-    )
+    moved = gather_bricks(tokens_here)
     upsampled = jnp.dot(
         moved.reshape(-1, tokens_here.shape[1]), weight, preferred_element_type=jnp.float32
     )

time: 91.5 us -> 78.6 us (0.86)
  the two profiles are of different devices: /device:TPU:3 before, /device:TPU:34 now
where the time goes in v3:
time: 78.6 us; the launch traced here: 78.1 us
  Pallas kernels  50 us (64%)
  local copies, waits for them, and re-layouts  14.2 us (18%)
  matrix products  12.3 us (16%)
  other arithmetic  1.3 us (2%)
    pallas_call x2, Pallas kernels, exchange_halo(): pl.pallas_call(halo_kernel, out_shape=jax.ShapeDtypeStruct(shape, field.d...  26 us
    pallas_call x1, Pallas kernels, gather_bricks(): pl.pallas_call(gather_kernel, out_shape=jax.ShapeDtypeStruct(shape, token...  15.7 us
    pallas_call x1, Pallas kernels, reduce_scatter(): pl.pallas_call(functools.partial(reduce_scatter_kernel, count), out_shape...  8.31 us
    dot_general x27, matrix products, conv_taps(): jnp.dot(window.reshape(-1, channels), kernel[(offset_x * 3 + offset_y) *...  5.9 us
    dot_general x27, matrix products, conv_rows(): lax.dot_general(kernel_rows[(offset_x * 3 + offset_y) * 3 + offset_z], wi...  5.41 us
    slice x2, local copies, waits for them, and re-layouts, conv_taps(): deeper[offset_x:offset_x + out_x, offset_y:offset_y + out_y, offset_z:off...  3.43 us
    slice x2, local copies, waits for them, and re-layouts, conv_rows(): deeper[offset_x:offset_x + out_x, offset_y:offset_y + out_y, offset_z:off...  3.35 us
    dot_general x1, local copies, waits for them, and re-layouts, local(): jnp.dot(moved.reshape(-1, tokens_here.shape[1]), weight, preferred_elemen...  2.9 us

profile of v3, /device:TPU:34, one launch (start us, length us, event | category | flops | bytes accessed | tf_op | source)
XLA Modules:
  0.0 78.1 jit_solution(5200922868504388339)
XLA Ops:
  0.0 0.8 slice_bitcast_fusion
  0.8 15.7 %shard_map.55 = bf16[8,16,1024]{2,1,0:T(8,128)(2,1)} custom-call(bf16[128,1024]{1,0:T(8,128)(2,1)} %bitcast.394), custom_call_target="tpu_custom_call" | custom-call | tf_op jit(solution)/shard_map/pallas_call | solution.py:285
  16.5 2.9 %copy.8 = bf16[1024,1024]{1,0:T(8,128)(2,1)S(1)} copy(bf16[1024,1024]{0,1:T(8,128)(2,1)} %bitcast.336) | data formatting | bytes 4194304 | tf_op jit(solution)/shard_map/dot_general | solution.py:310
  19.4 0.9 %multiply_reduce_fusion.1 = (f32[128,8]{0,1:T(8,128)S(1)}, f32[128,8,128]{2,0,1:T(8,128)S(1)}) fusion(bf16[128,1024,1]{1,0,2:T(8,128)(2,1)S(1)} %bitcast.393, bf16[8,128,1024]{2,1,0:T(8,128)(2,1)S(1)} %bitcast.333), kind=kOutput, calls=%fused_computation.118 | convolution fusion | flops 268696576 | bytes 2887680 | tf_op jit(solution)/shard_map/dot_general | solution.py:310
  20.4 0.3 fusion.18
  20.7 1.0 %copy.7 = bf16[8,2,8,2,2,2,128]{6,5,2,4,0,3,1:T(2,128)(2,1)} copy(bf16[8,2,8,2,2,2,128]{6,2,1,0,5,4,3:T(8,128)(2,1)S(1)} %bitcast.392) | data formatting | bytes 524288 | tf_op jit(solution)/shard_map/reshape;reshape | solution.py:315
  21.7 13.7 %shard_map.56 = bf16[6,18,16,128]{3,2,1,0:T(8,128)(2,1)} custom-call(bf16[4,16,16,128]{3,2,1,0:T(8,128)(2,1)} %bitcast.334), custom_call_target="tpu_custom_call" | custom-call | tf_op jit(solution)/shard_map/pallas_call | solution.py:206
  35.4 2.4 %fusion.138 = (bf16[4,16,16,128]{3,2,1,0:T(8,128)(2,1)S(1)}, bf16[4,16,16,128]{3,2,1,0:T(8,128)(2,1)S(1)}, bf16[4,16,16,128]{3,2,1,0:T(8,128)(2,1)S(1)}, bf16[4,...) fusion(bf16[6,18,16,128]{3,2,1,0:T(8,128)(2,1)} %shard_map.56), kind=kLoop, calls=%fused_computation.234 | loop fusion | bytes 4374528 | tf_op jit(solution)/shard_map/slice | solution.py:58
  38.2 0.6 copy-done.1
  38.7 1.1 %pad_slice_fusion.18 = (bf16[4,16,16,128]{3,2,1,0:T(8,128)(2,1)S(1)}, bf16[4,16,16,128]{3,2,1,0:T(8,128)(2,1)S(1)}, bf16[4,16,16,128]{3,2,1,0:T(8,128)(2,1)S(1)}...) fusion(bf16[6,18,16,128]{3,2,1,0:T(8,128)(2,1)S(1)} %copy-done.1), kind=kLoop, calls=%fused_computation.44 | loop fusion | bytes 5947392 | tf_op jit(solution)/shard_map/slice | solution.py:58
  39.8 0.2 convolution_add_fusion.24
  40.0 0.2 convolution_add_fusion.23
  40.3 0.2 convolution_add_fusion.22
  40.5 0.2 convolution_add_fusion.21
  40.7 0.2 convolution_add_fusion.20
  41.1 0.2 convolution_add_fusion.18
  41.4 0.2 convolution_add_fusion.17
  41.6 0.2 convolution_add_fusion.16
  41.8 0.2 convolution_add_fusion.15
  42.0 0.2 convolution_add_fusion.14
  42.2 0.2 convolution_add_fusion.13
  44.7 0.2 convolution_add_fusion.2
  44.9 0.2 convolution_add_fusion.1
  45.1 0.4 multiply_reduce_fusion
  45.6 1.0 %fusion.26.field_ref = bf16[4,16,16,128]{3,2,1,0:T(8,128)(2,1)} fusion(bf16[4,16,16,128]{3,2,1,0:T(8,128)(2,1)S(1)} %bitcast.335, f32[4,16,16,128]{3,2,1,0:T(8,128)S(1)} %bitcast.337, f32[128]{0:T(128)S(1)} %get-tuple-element.59, f32[4,16,16]{2,1,0:T(8,128)S(1)} %rsqrt.21), kind=kLoop, calls=%fused_computation.116 | loop fusion | flops 1703936 | bytes 1053184 | tf_op jit(solution)/shard_map/convert_element_type | solution.py:47
  46.6 12.3 %shard_map.57 = bf16[6,18,16,128]{3,2,1,0:T(8,128)(2,1)} custom-call(bf16[4,16,16,128]{3,2,1,0:T(8,128)(2,1)} %fusion.26.field_ref), custom_call_target="tpu_custom_call" | custom-call | tf_op jit(solution)/shard_map/pallas_call | solution.py:206
  58.9 2.4 %fusion.137 = (bf16[4,16,16,128]{3,2,1,0:T(8,128)(2,1)S(1)}, bf16[4,16,16,128]{3,2,1,0:T(8,128)(2,1)S(1)}, bf16[4,16,16,128]{3,2,1,0:T(8,128)(2,1)S(1)}, bf16[4,...) fusion(bf16[6,18,16,128]{3,2,1,0:T(8,128)(2,1)} %shard_map.57), kind=kLoop, calls=%fused_computation.233 | loop fusion | bytes 4374528 | tf_op jit(solution)/shard_map/slice | solution.py:79
  61.9 1.0 %pad_slice_fusion.6 = (bf16[4,16,16,128]{3,2,1,0:T(8,128)(2,1)S(1)}, bf16[4,16,16,128]{3,2,1,0:T(8,128)(2,1)S(1)}, bf16[4,16,16,128]{3,2,1,0:T(8,128)(2,1)S(1)},...) fusion(bf16[6,18,16,128]{3,2,1,0:T(8,128)(2,1)S(1)} %copy-done), kind=kLoop, calls=%fused_computation.32 | loop fusion | bytes 5947392 | tf_op jit(solution)/shard_map/slice | solution.py:79
  67.5 0.2 fusion.9
  67.7 0.7 reshape_reshape.7.parts_ref
  68.4 8.3 %shard_map.58 = bf16[8,4,256]{2,1,0:T(4,128)(2,1)} custom-call(f32[4,8,4,256]{3,2,1,0:T(4,128)} %reshape_reshape.7.parts_ref), custom_call_target="tpu_custom_call" | custom-call | tf_op jit(solution)/shard_map/pallas_call | solution.py:125
  76.8 1.3 %copy.10 = bf16[8,4,256]{2,1,0:T(4,128)(2,1)} copy(bf16[8,4,256]{2,1,0:T(4,128)(2,1)} %shard_map.58) | data formatting | bytes 32768
  (53 shorter events, 8.1 us)
Async XLA Ops:
  16.5 2.9 %copy-start.3 = (bf16[8,16,1024]{2,1,0:T(8,128)(2,1)S(1)}, bf16[8,16,1024]{2,1,0:T(8,128)(2,1)}, u32[]{:S(2)}) copy-start(bf16[8,16,1024]{2,1,0:T(8,128)(2,1)} %shard_map.55) | copy-start | bytes 786436
  35.3 2.4 %copy-start.4 = (bf16[1,27,128,128]{3,2,1,0:T(8,128)(2,1)S(1)}, bf16[1,27,128,128]{3,2,1,0:T(8,128)(2,1)}, u32[]{:S(2)}) copy-start(bf16[1,27,128,128]{3,2,1,0:T(8,128)(2,1)} %param.8) | copy-start | bytes 2654212
  37.7 1.0 %copy-start.1 = (bf16[6,18,16,128]{3,2,1,0:T(8,128)(2,1)S(1)}, bf16[6,18,16,128]{3,2,1,0:T(8,128)(2,1)}, u32[]{:S(2)}) copy-start(bf16[6,18,16,128]{3,2,1,0:T(8,128)(2,1)} %shard_map.56) | copy-start | bytes 1327108
  44.6 1.0 %copy-start.2 = (bf16[8,2,8,2,2,2,128]{6,5,2,4,0,3,1:T(2,128)(2,1)S(1)}, bf16[8,2,8,2,2,2,128]{6,5,2,4,0,3,1:T(2,128)(2,1)}, u32[]{:S(2)}) copy-start(bf16[8,2,8,2,2,2,128]{6,5,2,4,0,3,1:T(2,128)(2,1)} %copy.7) | copy-start | bytes 786436
  58.9 2.4 %copy-start.5 = (bf16[1,27,32,128]{3,2,1,0:T(8,128)(2,1)S(1)}, bf16[1,27,32,128]{3,2,1,0:T(8,128)(2,1)}, u32[]{:S(2)}) copy-start(bf16[1,27,32,128]{3,2,1,0:T(8,128)(2,1)} %param.9) | copy-start | bytes 663556
  58.9 3.0 %copy-start = (bf16[6,18,16,128]{3,2,1,0:T(8,128)(2,1)S(1)}, bf16[6,18,16,128]{3,2,1,0:T(8,128)(2,1)}, u32[]{:S(2)}) copy-start(bf16[6,18,16,128]{3,2,1,0:T(8,128)(2,1)} %shard_map.57) | copy-start | bytes 1327108

commit v4 on v3

--- a/solution.py
+++ b/solution.py
@@ -197,7 +197,69 @@
         def _():
             copy.wait_send()
 
-    out_ref[...] = held[...]
+    if out_ref is not None:
+        out_ref[...] = held[...]
+
+
+def gelu_tanh(values):
+    return 0.5 * values * (1.0 + jnp.tanh(0.7978845608028654 * (values + 0.044715 * (values * values * values))))
+
+
+def conv_kernel(
+    residual, field_ref, kernel_ref, gains_ref, out_ref, held, shifted, send_sem, recv_sem
+):
+    halo_kernel(field_ref, None, held, send_sem, recv_sem)
+    nx, ny, nz, channels = field_ref.shape
+    cells = nx * ny * nz
+    width = shifted.shape[2]
+    parts = []
+    for offset_z in range(3):
+        part = jnp.zeros((cells, width), jnp.float32)
+        for offset_x in range(3):
+            for offset_y in range(3):
+                window = held[offset_x : offset_x + nx, offset_y : offset_y + ny].reshape(cells, channels)
+                tap = kernel_ref[(offset_x * 3 + offset_y) * 3 + offset_z]
+                if residual:
+                    part = part + jnp.dot(window, tap, preferred_element_type=jnp.float32)
+                else:
+                    part = part + lax.dot_general(
+                        window, tap, (((1,), (1,)), ((), ())), preferred_element_type=jnp.float32
+                    )
+        parts.append(part.reshape(nx * ny, nz, width))
+    edge = jnp.zeros((nx * ny, 1, width), jnp.float32)
+    shifted[:, 0:1] = edge
+    shifted[:, nz + 1 : nz + 2] = edge
+    shifted[:, 1 : nz + 1] = parts[0]
+    total = parts[1] + shifted[:, 0:nz]
+    shifted[:, 1 : nz + 1] = parts[2]
+    total = total + shifted[:, 2 : nz + 2]
+    if residual:
+        mean_square = jnp.mean(total * total, axis=-1, keepdims=True)
+        normed = total * lax.rsqrt(mean_square + epsilon) * gains_ref[1:2, :]
+        base = field_ref[...].reshape(nx * ny, nz, channels).astype(jnp.float32)
+        out_ref[...] = gelu_tanh(normed + base).astype(out_ref.dtype).reshape(out_ref.shape)
+    else:
+        out_ref[...] = total.reshape(out_ref.shape)
+
+
+def conv_stage(field, kernel, gains, residual, collective):
+    nx, ny, nz, channels = field.shape
+    width = kernel.shape[2] if residual else kernel.shape[1]
+    padded = (nx + 2, ny + 2, nz, channels)
+    dtype = jnp.bfloat16 if residual else jnp.float32
+    return pl.pallas_call(
+        functools.partial(conv_kernel, residual),
+        out_shape=jax.ShapeDtypeStruct((nx, ny, nz, width), dtype),
+        in_specs=[pl.BlockSpec(memory_space=pltpu.VMEM)] * 3,
+        out_specs=pl.BlockSpec(memory_space=pltpu.VMEM),
+        scratch_shapes=[
+            pltpu.VMEM(padded, field.dtype),
+            pltpu.VMEM((nx * ny, nz + 2, width), jnp.float32),
+            pltpu.SemaphoreType.DMA((len(DIRECTIONS),)),
+            pltpu.SemaphoreType.DMA((len(DIRECTIONS),)),
+        ],
+        compiler_params=pltpu.CompilerParams(collective_id=collective, has_side_effects=True),
+    )(field, kernel, gains)
 
 
 def exchange_halo(field, collective):
@@ -316,12 +378,11 @@
         .transpose(1, 3, 0, 4, 2, 5, 6)
         .reshape(cell_x, cell_y, cell_z, channels)
     )
-    edged = exchange_halo(field, 1)
-    inner = conv_taps(edged, conv_in[0], cell_x, cell_y)
-    merged = finish(inner, field, gains)
-    padded = exchange_halo(merged, 2)
-    kernel_out = conv_out[0]
-    return reduce_scatter(conv_rows(padded, kernel_out, cell_x, cell_y))
+    merged = conv_stage(field, conv_in[0], gains, True, 1)
+    partial = conv_stage(merged, conv_out[0], gains, False, 2)
+    outch = partial.shape[-1]
+    rows = partial.reshape(-1, outch).T.reshape(outch, cell_x, cell_y * cell_z)
+    return reduce_scatter(rows)
 
 
 def solution(mesh):

time: 78.6 us -> 64.5 us (0.82)
  matrix products: 12.3 us -> 1.89 us
  local copies, waits for them, and re-layouts: 14.2 us -> 7.07 us
  Pallas kernels: 50 us -> 54.8 us
  other arithmetic: 1.3 us -> 0.29 us
    dot_general x54 -> x0, matrix products: 11.3 us -> none  [the longest x27 5.9 us: conv_taps(): jnp.dot(window.reshape(-1, channels), kernel[(offset_x * 3 + offset_y) *...]
    slice x4 -> x0, local copies, waits for them, and re-layouts: 6.78 us -> none  [the longest x2 3.43 us: conv_taps(): deeper[offset_x:offset_x + out_x, offset_y:offset_y + out_y, offset_z:off...]
    pallas_call x2, Pallas kernels: 26 us -> 30.7 us  [conv_stage(): pl.pallas_call(functools.partial(conv_kernel, residual), out_shape=jax.Sh...]
    reshape x0 -> x1, local copies, waits for them, and re-layouts: none -> 1.21 us  [local(): rows = partial.reshape(-1, outch).T.reshape(outch, cell_x, cell_y * cell_z)]
    convert_element_type x1 -> x0, other arithmetic: 1.01 us -> none  [finish(): return jax.nn.gelu(normalize(inner, gains[1]) + residual_part.astype(jnp....]
    dot_general x1, matrix products: 0.94 us -> 1.89 us  [local(): jnp.dot(moved.reshape(-1, tokens_here.shape[1]), weight, preferred_elemen...]
    unnamed x13 -> x3, local copies, waits for them, and re-layouts: 1.98 us -> 1.34 us
where the time goes in v4:
time: 64.5 us; the launch traced here: 64.2 us
  Pallas kernels  54.8 us (85%)
  local copies, waits for them, and re-layouts  7.07 us (11%)
  matrix products  1.89 us (3%)
    pallas_call x2, Pallas kernels, conv_stage(): pl.pallas_call(functools.partial(conv_kernel, residual), out_shape=jax.Sh...  30.7 us
    pallas_call x1, Pallas kernels, gather_bricks(): pl.pallas_call(gather_kernel, out_shape=jax.ShapeDtypeStruct(shape, token...  15.9 us
    pallas_call x1, Pallas kernels, reduce_scatter(): pl.pallas_call(functools.partial(reduce_scatter_kernel, count), out_shape...  8.3 us
    dot_general x1, local copies, waits for them, and re-layouts, local(): jnp.dot(moved.reshape(-1, tokens_here.shape[1]), weight, preferred_elemen...  2.85 us
    dot_general x1, matrix products, local(): jnp.dot(moved.reshape(-1, tokens_here.shape[1]), weight, preferred_elemen...  1.89 us
    unnamed x3, local copies, waits for them, and re-layouts  1.34 us

profile of v4, /device:TPU:34, one launch (start us, length us, event | category | flops | bytes accessed | tf_op | source)
XLA Modules:
  0.0 64.2 jit_solution(15412648469172827035)
XLA Ops:
  0.0 2.9 %copy.9 = bf16[1024,1024]{1,0:T(8,128)(2,1)S(1)} copy(bf16[1024,1024]{0,1:T(8,128)(2,1)} %bitcast.23) | data formatting | bytes 4194304 | tf_op jit(solution)/shard_map/dot_general | solution.py:372
  2.9 0.0 copy-start
  2.9 15.9 %shard_map.55 = bf16[8,16,1024]{2,1,0:T(8,128)(2,1)} custom-call(bf16[128,1024]{1,0:T(8,128)(2,1)} %bitcast.29), custom_call_target="tpu_custom_call" | custom-call | tf_op jit(solution)/shard_map/pallas_call | solution.py:347
  18.8 1.9 %multiply_reduce_fusion = (f32[128,8]{0,1:T(8,128)S(1)}, f32[128,8,128]{2,0,1:T(8,128)S(1)}) fusion(bf16[128,1024,1]{1,0,2:T(8,128)(2,1)} %bitcast.26, bf16[8,128,1024]{2,1,0:T(8,128)(2,1)S(1)} %bitcast.21), kind=kOutput, calls=%fused_computation.9 | convolution fusion | flops 268696576 | bytes 2887680 | tf_op jit(solution)/shard_map/dot_general | solution.py:372
  20.7 0.0 copy-done
  20.7 0.3 fusion.7
  21.0 1.0 %copy.7 = bf16[8,2,8,2,2,2,128]{6,5,2,4,0,3,1:T(2,128)(2,1)} copy(bf16[8,2,8,2,2,2,128]{6,2,1,0,5,4,3:T(8,128)(2,1)S(1)} %bitcast.25) | data formatting | bytes 524288 | tf_op jit(solution)/shard_map/reshape;reshape | solution.py:377
  21.9 16.1 %shard_map.56.field_ref = bf16[4,16,16,128]{3,2,1,0:T(8,128)(2,1)} custom-call(bf16[4,16,16,128]{3,2,1,0:T(8,128)(2,1)} %bitcast.24, bf16[27,128,128]{2,1,0:T(8,128)(2,1)} %bitcast.27, f32[2,128]{1,0:T(2,128)} %bitcast.31), custom_call_target="tpu_custom_call" | custom-call | tf_op jit(solution)/shard_map/pallas_call | solution.py:250
  38.1 14.5 %shard_map.57 = f32[4,16,16,32]{3,2,1,0:T(8,128)} custom-call(bf16[4,16,16,128]{3,2,1,0:T(8,128)(2,1)} %shard_map.56.field_ref, bf16[27,32,128]{2,1,0:T(8,128)(2,1)} %bitcast.30, f32[2,128]{1,0:T(2,128)} %bitcast.32), custom_call_target="tpu_custom_call" | custom-call | tf_op jit(solution)/shard_map/pallas_call | solution.py:250
  52.6 1.2 %copy.8 = f32[1024,32]{0,1:T(8,128)S(1)} copy(f32[1024,32]{1,0:T(8,128)} %bitcast.22) | data formatting | bytes 262144 | tf_op jit(solution)/shard_map/reshape | solution.py:384
  53.8 0.7 %reshape_reshape.7.parts_ref = f32[4,8,4,256]{3,2,1,0:T(4,128)} reshape(f32[32,1024]{1,0:T(8,128)S(1)} %bitcast.28) | data formatting | bytes 262144 | tf_op jit(solution)/shard_map/reshape;reshape | solution.py:124
  54.5 8.3 %shard_map.58 = bf16[8,4,256]{2,1,0:T(4,128)(2,1)} custom-call(f32[4,8,4,256]{3,2,1,0:T(4,128)} %reshape_reshape.7.parts_ref), custom_call_target="tpu_custom_call" | custom-call | tf_op jit(solution)/shard_map/pallas_call | solution.py:125
  62.8 1.3 %copy.11 = bf16[8,4,256]{2,1,0:T(4,128)(2,1)} copy(bf16[8,4,256]{2,1,0:T(4,128)(2,1)} %shard_map.58) | data formatting | bytes 32768
  (2 shorter events, 0.0 us)
Async XLA Ops:
  2.9 17.8 %copy-start = (f32[1,2,128]{2,1,0:T(2,128)S(1)}, f32[1,2,128]{2,1,0:T(2,128)}, u32[]{:S(2)}) copy-start(f32[1,2,128]{2,1,0:T(2,128)} %param.7) | copy-start | bytes 3076

commit v5 on v1

v5 whole, which is shorter than its diff:
```python
import functools

import jax
import jax.numpy as jnp
from jax import lax
from jax.experimental import pallas as pl
from jax.experimental.pallas import tpu as pltpu
from jax.sharding import PartitionSpec as P

MESH = pl.DeviceIdType.MESH
PXD = 2
GZ = 8


epsilon = 1e-05


def normalize(values, scale):
    mean_square = jnp.mean(values * values, axis=-1, keepdims=True)
    return values * lax.rsqrt(mean_square + epsilon) * scale


def activate(upsampled, gains):
    width = gains.shape[1]
    shaped = upsampled.reshape(upsampled.shape[:-1] + (upsampled.shape[-1] // width, width))
    result = jax.nn.gelu(normalize(shaped, gains[0]), approximate=True).astype(jnp.bfloat16)
    return result.reshape(upsampled.shape)


def gelu_tanh(values):
    return 0.5 * values * (1.0 + jnp.tanh(0.7978845608028654 * (values + 0.044715 * (values * values * values))))


def reduce_scatter_kernel(count, parts_ref, out_ref, held, send_sem, recv_sem):
    me = lax.axis_index("section")
    barrier = pltpu.get_barrier_semaphore()
    for step in range(1, count):
        peer = lax.rem(me + step, count)
        pl.semaphore_signal(barrier, inc=1, device_id={"section": peer}, device_id_type=MESH)
    pl.semaphore_wait(barrier, count - 1)
    sends = []
    for step in range(1, count):
        peer = lax.rem(me + step, count)
        copy = pltpu.make_async_remote_copy(
            src_ref=parts_ref.at[peer],
            dst_ref=held.at[step],
            send_sem=send_sem.at[step],
            recv_sem=recv_sem.at[step],
            device_id={"section": peer},
            device_id_type=MESH,
        )
        copy.start()
        sends.append(copy)
    total = parts_ref[me]
    for step in range(1, count):
        sends[step - 1].wait_recv()
        total = total + held[step]
    for copy in sends:
        copy.wait_send()
    out_ref[...] = total.astype(out_ref.dtype)


def reduce_scatter(parts):
    count = lax.axis_size("section")
    shaped = parts.reshape((count, parts.shape[0] // count) + parts.shape[1:])
    return pl.pallas_call(
        functools.partial(reduce_scatter_kernel, count),
        out_shape=jax.ShapeDtypeStruct(shaped.shape[1:], jnp.bfloat16),
        in_specs=[pl.BlockSpec(memory_space=pltpu.VMEM)],
        out_specs=pl.BlockSpec(memory_space=pltpu.VMEM),
        scratch_shapes=[
            pltpu.VMEM(shaped.shape, jnp.float32),
            pltpu.SemaphoreType.DMA((count,)),
            pltpu.SemaphoreType.DMA((count,)),
        ],
        compiler_params=pltpu.CompilerParams(collective_id=0, has_side_effects=True),
    )(shaped)


def send_groups(me_x, me_y, count):
    return [
        (me_x, me_y + 1, None),
        (me_x + 1, 0, (me_y == count - 1) & (me_x + 1 < count)),
        (me_x - 1, count + 1, (me_y == 0) & (me_x > 0)),
    ]


def gather_kernel(tokens_ref, out_ref, held, send_sem, recv_sem):
    count = lax.axis_size("inl")
    me_x, me_y = lax.axis_index("inl"), lax.axis_index("xln")
    rows = tokens_ref.shape[0] // count
    slots = out_ref.shape[0]
    one = jnp.int32(1)
    groups = send_groups(me_x, me_y, count)
    sources = [(me_y - 1, count - 1, me_y >= 1)]
    sources += [(me_y, other, None) for other in range(count)]
    sources += [(me_y + 1, 0, me_y + 1 < count)]

    def is_me(x, y):
        return (x == me_x) & (y == me_y)

    barrier = pltpu.get_barrier_semaphore()
    expected = jnp.int32(0)
    for column, _, exists in groups:
        live = True if exists is None else exists
        expected = expected + jnp.where(live, count, 0)
        for other in range(count):

            @pl.when(jnp.logical_and(live, jnp.logical_not(is_me(other, column))))
            def _():
                pl.semaphore_signal(barrier, inc=1, device_id={"inl": other, "xln": column}, device_id_type=MESH)

            expected = expected - jnp.where(jnp.logical_and(live, is_me(other, column)), one, 0)
    for source_x, source_y, exists in sources:
        live = True if exists is None else exists
        mine = jnp.logical_and(live, is_me(source_x, source_y))
        expected = expected + jnp.where(jnp.logical_and(live, jnp.logical_not(mine)), one, 0)

        @pl.when(jnp.logical_and(live, jnp.logical_not(mine)))
        def _():
            pl.semaphore_signal(barrier, inc=1, device_id={"inl": source_x, "xln": source_y}, device_id_type=MESH)

    pl.semaphore_wait(barrier, expected)
    copies = []
    for index, (column, slot, exists) in enumerate(groups):
        live = True if exists is None else exists
        for other in range(count):
            copy = pltpu.make_async_remote_copy(
                src_ref=tokens_ref.at[pl.ds(other * rows, rows)],
                dst_ref=held.at[slot],
                send_sem=send_sem.at[index * count + other],
                recv_sem=recv_sem.at[slot],
                device_id={"inl": other, "xln": column},
                device_id_type=MESH,
            )
            remote = jnp.logical_and(live, jnp.logical_not(is_me(other, column)))

            @pl.when(remote)
            def _():
                copy.start()

            copies.append((copy, remote))
    for slot, (source_x, source_y, exists) in enumerate(sources):
        live = True if exists is None else exists
        mine = jnp.logical_and(live, is_me(source_x, source_y))
        remote = jnp.logical_and(live, jnp.logical_not(mine))
        incoming = pltpu.make_async_remote_copy(
            src_ref=tokens_ref.at[pl.ds(0, rows)],
            dst_ref=held.at[slot],
            send_sem=send_sem.at[0],
            recv_sem=recv_sem.at[slot],
            device_id={"inl": source_x, "xln": source_y},
            device_id_type=MESH,
        )

        @pl.when(remote)
        def _():
            incoming.wait_recv()
            out_ref[slot] = held[slot]

        @pl.when(mine)
        def _():
            out_ref[slot] = tokens_ref[pl.ds(pl.multiple_of(me_x * rows, rows), rows)]

        @pl.when(jnp.logical_not(live))
        def _():
            out_ref[slot] = jnp.zeros(out_ref.shape[1:], out_ref.dtype)

    for copy, remote in copies:

        @pl.when(remote)
        def _():
            copy.wait_send()


def gather_bricks(tokens):
    count = lax.axis_size("inl")
    rows = tokens.shape[0] // count
    shape = (lax.axis_size("xln") + 2, rows, tokens.shape[1])
    return pl.pallas_call(
        gather_kernel,
        out_shape=jax.ShapeDtypeStruct(shape, tokens.dtype),
        in_specs=[pl.BlockSpec(memory_space=pltpu.VMEM)],
        out_specs=pl.BlockSpec(memory_space=pltpu.VMEM),
        scratch_shapes=[
            pltpu.VMEM(shape, tokens.dtype),
            pltpu.SemaphoreType.DMA((3 * count,)),
            pltpu.SemaphoreType.DMA((shape[0],)),
        ],
        compiler_params=pltpu.CompilerParams(collective_id=3, has_side_effects=True),
    )(tokens)


def halo_x(field_ref, held, send_sem, recv_sem):
    nx = field_ref.shape[0]
    count = lax.axis_size("inl")
    me = lax.axis_index("inl")
    barrier = pltpu.get_barrier_semaphore()
    for step in (-1, 1):
        pl.semaphore_signal(
            barrier, inc=1, device_id={"inl": lax.rem(me + step + count, count)}, device_id_type=MESH
        )
    pl.semaphore_wait(barrier, 2)
    copies = []
    for index, step in enumerate((-1, 1)):
        source, target = (0, nx + 1) if step < 0 else (nx - 1, 0)
        copy = pltpu.make_async_remote_copy(
            src_ref=field_ref.at[source : source + 1],
            dst_ref=held.at[target : target + 1],
            send_sem=send_sem.at[index],
            recv_sem=recv_sem.at[index],
            device_id={"inl": me + step},
            device_id_type=MESH,
        )
        sends = (me + step >= 0) & (me + step < count)
        gets = (me - step >= 0) & (me - step < count)

        @pl.when(sends)
        def _():
            copy.start()

        @pl.when(jnp.logical_not(gets))
        def _():
            held[target : target + 1] = jnp.zeros((1,) + held.shape[1:], held.dtype)

        copies.append((copy, sends, gets))
    held[1 : nx + 1] = field_ref[...]
    for copy, sends, gets in copies:

        @pl.when(gets)
        def _():
            copy.wait_recv()

        @pl.when(sends)
        def _():
            copy.wait_send()


def conv_kernel(
    residual, field_ref, kernel_ref, gains_ref, out_ref, held, shifted, send_sem, recv_sem
):
    halo_x(field_ref, held, send_sem, recv_sem)
    nx, ny_in, nz, channels = field_ref.shape
    ny = ny_in - 2
    cells = nx * ny * nz
    width = shifted.shape[2]
    parts = []
    for offset_z in range(3):
        part = jnp.zeros((cells, width), jnp.float32)
        for offset_x in range(3):
            for offset_y in range(3):
                window = held[offset_x : offset_x + nx, offset_y : offset_y + ny].reshape(cells, channels)
                tap = kernel_ref[(offset_x * 3 + offset_y) * 3 + offset_z]
                if residual:
                    part = part + jnp.dot(window, tap, preferred_element_type=jnp.float32)
                else:
                    part = part + lax.dot_general(
                        window, tap, (((1,), (1,)), ((), ())), preferred_element_type=jnp.float32
                    )
        parts.append(part.reshape(nx * ny, nz, width))
    edge = jnp.zeros((nx * ny, 1, width), jnp.float32)
    shifted[:, 0:1] = edge
    shifted[:, nz + 1 : nz + 2] = edge
    shifted[:, 1 : nz + 1] = parts[0]
    total = parts[1] + shifted[:, 0:nz]
    shifted[:, 1 : nz + 1] = parts[2]
    total = total + shifted[:, 2 : nz + 2]
    if residual:
        mean_square = jnp.mean(total * total, axis=-1, keepdims=True)
        normed = total * lax.rsqrt(mean_square + epsilon) * gains_ref[1:2, :]
        base = field_ref[:, 1 : ny + 1].reshape(nx * ny, nz, channels).astype(jnp.float32)
        mixed = gelu_tanh(normed + base).reshape(nx, ny, nz, channels)
        me_y, count_y = lax.axis_index("xln"), lax.axis_size("xln")
        row = lax.broadcasted_iota(jnp.int32, mixed.shape, 1)
        outside = ((row == 0) & (me_y == 0)) | ((row == ny - 1) & (me_y == count_y - 1))
        out_ref[...] = jnp.where(outside, 0.0, mixed).astype(out_ref.dtype)
    else:
        out_ref[...] = total.reshape(out_ref.shape)


def conv_stage(field, kernel, gains, residual, collective):
    nx, ny_in, nz, channels = field.shape
    width = kernel.shape[2] if residual else kernel.shape[1]
    padded = (nx + 2, ny_in, nz, channels)
    ny = ny_in - 2
    dtype = jnp.bfloat16 if residual else jnp.float32
    return pl.pallas_call(
        functools.partial(conv_kernel, residual),
        out_shape=jax.ShapeDtypeStruct((nx, ny, nz, width), dtype),
        in_specs=[pl.BlockSpec(memory_space=pltpu.VMEM)] * 3,
        out_specs=pl.BlockSpec(memory_space=pltpu.VMEM),
        scratch_shapes=[
            pltpu.VMEM(padded, field.dtype),
            pltpu.VMEM((nx * ny, nz + 2, width), jnp.float32),
            pltpu.SemaphoreType.DMA((2,)),
            pltpu.SemaphoreType.DMA((2,)),
        ],
        compiler_params=pltpu.CompilerParams(collective_id=collective, has_side_effects=True),
    )(field, kernel, gains)


def local(skips, deconv_weight, norm_gain, conv_in, conv_out):
    inl_size = lax.axis_size("inl")
    tokens_here = skips[0]
    weight = deconv_weight[0]
    gains = norm_gain[0]
    channels = gains.shape[1]
    cell_x = 2 * PXD
    cell_y = 2 * lax.axis_size("xln")
    cell_z = 2 * GZ
    assert tokens_here.shape[0] == inl_size * PXD * GZ
    moved = gather_bricks(tokens_here)
    lines = moved.shape[0]
    upsampled = jnp.dot(
        moved.reshape(-1, tokens_here.shape[1]), weight, preferred_element_type=jnp.float32
    )
    brick = activate(upsampled, gains)
    field = (
        brick.reshape(lines, PXD, GZ, 2, 2, 2, channels)
        .transpose(1, 3, 0, 4, 2, 5, 6)
        .reshape(cell_x, 2 * lines, cell_z, channels)
    )
    merged = conv_stage(field, conv_in[0], gains, True, 1)
    partial = conv_stage(merged, conv_out[0], gains, False, 2)
    outch = partial.shape[-1]
    rows = partial.reshape(-1, outch).T.reshape(outch, cell_x, cell_y * cell_z)
    return reduce_scatter(rows)


def solution(mesh):
    return jax.shard_map(
        local,
        mesh=mesh,
        in_specs=(
            P("section", ("inl", "xln"), None),
            P("section", None, None),
            P("section", None, None),
            P("section", None, None, None),
            P("section", None, None, None),
        ),
        out_specs=P("section", "inl", "xln"),
        check_vma=False,
    )
```

time: 110 us -> 57.3 us (0.52)
  the two profiles are of different devices: /device:TPU:1 before, /device:TPU:3 now
where the time goes in v5:
time: 57.3 us; the launch traced here: 57 us
  Pallas kernels  47.5 us (83%)
  local copies, waits for them, and re-layouts  7.09 us (12%)
  matrix products  2 us (3%)
    pallas_call x1, Pallas kernels, gather_bricks(): pl.pallas_call(gather_kernel, out_shape=jax.ShapeDtypeStruct(shape, token...  24.1 us
    pallas_call x2, Pallas kernels, conv_stage(): pl.pallas_call(functools.partial(conv_kernel, residual), out_shape=jax.Sh...  16.2 us
    pallas_call x1, Pallas kernels, reduce_scatter(): pl.pallas_call(functools.partial(reduce_scatter_kernel, count), out_shape...  7.15 us
    dot_general x1, local copies, waits for them, and re-layouts, local(): jnp.dot(moved.reshape(-1, tokens_here.shape[1]), weight, preferred_elemen...  2.85 us
    dot_general x1, matrix products, local(): jnp.dot(moved.reshape(-1, tokens_here.shape[1]), weight, preferred_elemen...  2 us
    unnamed x3, local copies, waits for them, and re-layouts  1.34 us
    reshape x1, local copies, waits for them, and re-layouts, local(): rows = partial.reshape(-1, outch).T.reshape(outch, cell_x, cell_y * cell_z)  1.21 us

profile of v5, /device:TPU:3, one launch (start us, length us, event | category | flops | bytes accessed | tf_op | source)
XLA Modules:
  0.0 57.0 jit_solution(4117972190318474205)
XLA Ops:
  0.0 2.9 %copy.9 = bf16[1024,1024]{1,0:T(8,128)(2,1)S(1)} copy(bf16[1024,1024]{0,1:T(8,128)(2,1)} %bitcast.23) | data formatting | bytes 4194304 | tf_op jit(solution)/shard_map/dot_general | solution.py:314
  2.9 0.0 copy-start
  2.9 24.1 %shard_map.55 = bf16[10,16,1024]{2,1,0:T(8,128)(2,1)} custom-call(bf16[128,1024]{1,0:T(8,128)(2,1)} %bitcast.29), custom_call_target="tpu_custom_call" | custom-call | tf_op jit(solution)/shard_map/pallas_call | solution.py:180
  27.0 2.0 %multiply_reduce_fusion = (f32[160,8]{0,1:T(8,128)S(1)}, f32[160,8,128]{2,0,1:T(8,128)S(1)}) fusion(bf16[160,1024,1]{1,0,2:T(8,128)(2,1)} %bitcast.24, bf16[8,128,1024]{2,1,0:T(8,128)(2,1)S(1)} %bitcast.21), kind=kOutput, calls=%fused_computation.9 | convolution fusion | flops 335870720 | bytes 3085312 | tf_op jit(solution)/shard_map/dot_general | solution.py:314
  29.0 0.0 copy-done
  29.0 0.3 fusion.7
  29.4 1.0 %copy.7 = bf16[10,2,8,2,2,2,128]{6,5,2,4,0,3,1:T(2,128)(2,1)} copy(bf16[10,2,8,2,2,2,128]{6,2,1,0,5,4,3:T(8,128)(2,1)S(1)} %bitcast.25) | data formatting | bytes 655360 | tf_op jit(solution)/shard_map/reshape;reshape | solution.py:319
  30.4 8.4 %shard_map.56.field_ref = bf16[4,18,16,128]{3,2,1,0:T(8,128)(2,1)} custom-call(bf16[4,20,16,128]{3,2,1,0:T(8,128)(2,1)} %bitcast.26, bf16[27,128,128]{2,1,0:T(8,128)(2,1)} %bitcast.27, f32[2,128]{1,0:T(2,128)} %bitcast.31), custom_call_target="tpu_custom_call" | custom-call | tf_op jit(solution)/shard_map/pallas_call | solution.py:287
  38.7 7.8 %shard_map.57 = f32[4,16,16,32]{3,2,1,0:T(8,128)} custom-call(bf16[4,18,16,128]{3,2,1,0:T(8,128)(2,1)} %shard_map.56.field_ref, bf16[27,32,128]{2,1,0:T(8,128)(2,1)} %bitcast.30, f32[2,128]{1,0:T(2,128)} %bitcast.32), custom_call_target="tpu_custom_call" | custom-call | tf_op jit(solution)/shard_map/pallas_call | solution.py:287
  46.6 1.2 %copy.8 = f32[1024,32]{0,1:T(8,128)S(1)} copy(f32[1024,32]{1,0:T(8,128)} %bitcast.22) | data formatting | bytes 262144 | tf_op jit(solution)/shard_map/reshape | solution.py:326
  47.8 0.7 %reshape_reshape.7.parts_ref = f32[4,8,4,256]{3,2,1,0:T(4,128)} reshape(f32[32,1024]{1,0:T(8,128)S(1)} %bitcast.28) | data formatting | bytes 262144 | tf_op jit(solution)/shard_map/reshape;reshape | solution.py:65
  48.5 7.2 %shard_map.58 = bf16[8,4,256]{2,1,0:T(4,128)(2,1)} custom-call(f32[4,8,4,256]{3,2,1,0:T(4,128)} %reshape_reshape.7.parts_ref), custom_call_target="tpu_custom_call" | custom-call | tf_op jit(solution)/shard_map/pallas_call | solution.py:66
  55.7 1.3 %copy.11 = bf16[8,4,256]{2,1,0:T(4,128)(2,1)} copy(bf16[8,4,256]{2,1,0:T(4,128)(2,1)} %shard_map.58) | data formatting | bytes 32768
  (2 shorter events, 0.0 us)
Async XLA Ops:
  2.9 26.1 %copy-start = (f32[1,2,128]{2,1,0:T(2,128)S(1)}, f32[1,2,128]{2,1,0:T(2,128)}, u32[]{:S(2)}) copy-start(f32[1,2,128]{2,1,0:T(2,128)} %param.7) | copy-start | bytes 3076

commit v6 on v5

--- a/solution.py
+++ b/solution.py
@@ -85,12 +85,14 @@
     ]
 
 
-def gather_kernel(tokens_ref, out_ref, held, send_sem, recv_sem):
+def gather_kernel(tokens_ref, weight_hbm, gains_ref, out_ref, weight, field, held, send_sem, recv_sem, weight_sem):
     count = lax.axis_size("inl")
     me_x, me_y = lax.axis_index("inl"), lax.axis_index("xln")
     rows = tokens_ref.shape[0] // count
-    slots = out_ref.shape[0]
+    width = gains_ref.shape[1]
     one = jnp.int32(1)
+    loading = pltpu.make_async_copy(weight_hbm, weight, weight_sem)
+    loading.start()
     groups = send_groups(me_x, me_y, count)
     sources = [(me_y - 1, count - 1, me_y >= 1)]
     sources += [(me_y, other, None) for other in range(count)]
@@ -120,13 +122,20 @@
         def _():
             pl.semaphore_signal(barrier, inc=1, device_id={"inl": source_x, "xln": source_y}, device_id_type=MESH)
 
+    loading.wait()
+    upsampled = jnp.dot(tokens_ref[...], weight[...], preferred_element_type=jnp.float32)
+    for group in range(upsampled.shape[1] // width):
+        part = upsampled[:, group * width : (group + 1) * width]
+        mean_square = jnp.mean(part * part, axis=-1, keepdims=True)
+        normed = part * lax.rsqrt(mean_square + epsilon) * gains_ref[0:1, :]
+        field[:, group * width : (group + 1) * width] = gelu_tanh(normed).astype(field.dtype)
     pl.semaphore_wait(barrier, expected)
     copies = []
     for index, (column, slot, exists) in enumerate(groups):
         live = True if exists is None else exists
         for other in range(count):
             copy = pltpu.make_async_remote_copy(
-                src_ref=tokens_ref.at[pl.ds(other * rows, rows)],
+                src_ref=field.at[pl.ds(other * rows, rows)],
                 dst_ref=held.at[slot],
                 send_sem=send_sem.at[index * count + other],
                 recv_sem=recv_sem.at[slot],
@@ -145,7 +154,7 @@
         mine = jnp.logical_and(live, is_me(source_x, source_y))
         remote = jnp.logical_and(live, jnp.logical_not(mine))
         incoming = pltpu.make_async_remote_copy(
-            src_ref=tokens_ref.at[pl.ds(0, rows)],
+            src_ref=field.at[pl.ds(0, rows)],
             dst_ref=held.at[slot],
             send_sem=send_sem.at[0],
             recv_sem=recv_sem.at[slot],
@@ -160,7 +169,7 @@
 
         @pl.when(mine)
         def _():
-            out_ref[slot] = tokens_ref[pl.ds(pl.multiple_of(me_x * rows, rows), rows)]
+            out_ref[slot] = field[pl.ds(pl.multiple_of(me_x * rows, rows), rows)]
 
         @pl.when(jnp.logical_not(live))
         def _():
@@ -173,22 +182,29 @@
             copy.wait_send()
 
 
-def gather_bricks(tokens):
+def gather_bricks(tokens, weight, gains):
     count = lax.axis_size("inl")
     rows = tokens.shape[0] // count
-    shape = (lax.axis_size("xln") + 2, rows, tokens.shape[1])
+    shape = (lax.axis_size("xln") + 2, rows, weight.shape[1])
     return pl.pallas_call(
         gather_kernel,
-        out_shape=jax.ShapeDtypeStruct(shape, tokens.dtype),
-        in_specs=[pl.BlockSpec(memory_space=pltpu.VMEM)],
+        out_shape=jax.ShapeDtypeStruct(shape, jnp.bfloat16),
+        in_specs=[
+            pl.BlockSpec(memory_space=pltpu.VMEM),
+            pl.BlockSpec(memory_space=pl.ANY),
+            pl.BlockSpec(memory_space=pltpu.VMEM),
+        ],
         out_specs=pl.BlockSpec(memory_space=pltpu.VMEM),
         scratch_shapes=[
-            pltpu.VMEM(shape, tokens.dtype),
+            pltpu.VMEM(weight.shape, weight.dtype),
+            pltpu.VMEM((tokens.shape[0], weight.shape[1]), jnp.bfloat16),
+            pltpu.VMEM(shape, jnp.bfloat16),
             pltpu.SemaphoreType.DMA((3 * count,)),
             pltpu.SemaphoreType.DMA((shape[0],)),
+            pltpu.SemaphoreType.DMA(()),
         ],
         compiler_params=pltpu.CompilerParams(collective_id=3, has_side_effects=True),
-    )(tokens)
+    )(tokens, weight, gains)
 
 
 def halo_x(field_ref, held, send_sem, recv_sem):
@@ -309,12 +325,8 @@
     cell_y = 2 * lax.axis_size("xln")
     cell_z = 2 * GZ
     assert tokens_here.shape[0] == inl_size * PXD * GZ
-    moved = gather_bricks(tokens_here)
-    lines = moved.shape[0]
-    upsampled = jnp.dot(
-        moved.reshape(-1, tokens_here.shape[1]), weight, preferred_element_type=jnp.float32
-    )
-    brick = activate(upsampled, gains)
+    brick = gather_bricks(tokens_here, weight, gains)
+    lines = brick.shape[0]
     field = (
         brick.reshape(lines, PXD, GZ, 2, 2, 2, channels)
         .transpose(1, 3, 0, 4, 2, 5, 6)

time: 57.3 us -> 52.9 us (0.923)
  matrix products: 2 us -> 0 us
  local copies, waits for them, and re-layouts: 7.09 us -> 5.2 us
    dot_general x1 -> x0, local copies, waits for them, and re-layouts: 2.85 us -> none  [local(): jnp.dot(moved.reshape(-1, tokens_here.shape[1]), weight, preferred_elemen...]
    dot_general x1 -> x0, matrix products: 2 us -> none  [local(): jnp.dot(moved.reshape(-1, tokens_here.shape[1]), weight, preferred_elemen...]
    reshape x0 -> x1, local copies, waits for them, and re-layouts: none -> 1.95 us  [local(): brick.reshape(lines, PXD, GZ, 2, 2, 2, channels)]
    another operation x1 -> x0, local copies, waits for them, and re-layouts: 0.98 us -> none  [local(): brick.reshape(lines, PXD, GZ, 2, 2, 2, channels)]
    unnamed x3 -> x1, local copies, waits for them, and re-layouts: 1.34 us -> 1.33 us
where the time goes in v6:
time: 52.9 us; the launch traced here: 52.6 us
  Pallas kernels  47.4 us (90%)
  local copies, waits for them, and re-layouts  5.2 us (10%)
    pallas_call x1, Pallas kernels, gather_bricks(): pl.pallas_call(gather_kernel, out_shape=jax.ShapeDtypeStruct(shape, jnp.b...  24 us
    pallas_call x2, Pallas kernels, conv_stage(): pl.pallas_call(functools.partial(conv_kernel, residual), out_shape=jax.Sh...  16.2 us
    pallas_call x1, Pallas kernels, reduce_scatter(): pl.pallas_call(functools.partial(reduce_scatter_kernel, count), out_shape...  7.16 us
    reshape x1, local copies, waits for them, and re-layouts, local(): brick.reshape(lines, PXD, GZ, 2, 2, 2, channels)  1.95 us
    unnamed x1, local copies, waits for them, and re-layouts  1.33 us
    reshape x1, local copies, waits for them, and re-layouts, local(): rows = partial.reshape(-1, outch).T.reshape(outch, cell_x, cell_y * cell_z)  1.21 us

profile of v6, /device:TPU:3, one launch (start us, length us, event | category | flops | bytes accessed | tf_op | source)
XLA Modules:
  0.0 52.6 jit_solution(6524688635809130052)
XLA Ops:
  0.0 24.0 %shard_map.55 = bf16[10,16,1024]{2,1,0:T(8,128)(2,1)} custom-call(bf16[128,1024]{1,0:T(8,128)(2,1)} %bitcast.17, bf16[1024,1024]{1,0:T(8,128)(2,1)} %bitcast.12, f32[2,128]{1,0:T(2,128)} %bitcast.19), custom_call_target="tpu_custom_call" | custom-call | tf_op jit(solution)/shard_map/pallas_call | solution.py:189
  24.0 1.9 %copy.6 = bf16[10,2,8,2,2,2,128]{6,5,2,4,0,3,1:T(2,128)(2,1)} copy(bf16[10,2,8,2,2,2,128]{6,2,5,4,3,1,0:T(8,128)(2,1)} %bitcast.14) | data formatting | bytes 655360 | tf_op jit(solution)/shard_map/reshape | solution.py:331
  26.0 8.4 %shard_map.56.field_ref = bf16[4,18,16,128]{3,2,1,0:T(8,128)(2,1)} custom-call(bf16[4,20,16,128]{3,2,1,0:T(8,128)(2,1)} %bitcast.13, bf16[27,128,128]{2,1,0:T(8,128)(2,1)} %bitcast.15, f32[2,128]{1,0:T(2,128)} %bitcast.20), custom_call_target="tpu_custom_call" | custom-call | tf_op jit(solution)/shard_map/pallas_call | solution.py:303
  34.3 7.8 %shard_map.57 = f32[4,16,16,32]{3,2,1,0:T(8,128)} custom-call(bf16[4,18,16,128]{3,2,1,0:T(8,128)(2,1)} %shard_map.56.field_ref, bf16[27,32,128]{2,1,0:T(8,128)(2,1)} %bitcast.18, f32[2,128]{1,0:T(2,128)} %bitcast.21), custom_call_target="tpu_custom_call" | custom-call | tf_op jit(solution)/shard_map/pallas_call | solution.py:303
  42.2 1.2 %copy.7 = f32[1024,32]{0,1:T(8,128)S(1)} copy(f32[1024,32]{1,0:T(8,128)} %bitcast.11) | data formatting | bytes 262144 | tf_op jit(solution)/shard_map/reshape | solution.py:338
  43.4 0.7 %reshape_reshape.3.parts_ref = f32[4,8,4,256]{3,2,1,0:T(4,128)} reshape(f32[32,1024]{1,0:T(8,128)S(1)} %bitcast.16) | data formatting | bytes 262144 | tf_op jit(solution)/shard_map/reshape;reshape | solution.py:65
  44.1 7.2 %shard_map.58 = bf16[8,4,256]{2,1,0:T(4,128)(2,1)} custom-call(f32[4,8,4,256]{3,2,1,0:T(4,128)} %reshape_reshape.3.parts_ref), custom_call_target="tpu_custom_call" | custom-call | tf_op jit(solution)/shard_map/pallas_call | solution.py:66
  51.3 1.3 %copy.9 = bf16[8,4,256]{2,1,0:T(4,128)(2,1)} copy(bf16[8,4,256]{2,1,0:T(4,128)(2,1)} %shard_map.58) | data formatting | bytes 32768

commit v7 on v6

--- a/solution.py
+++ b/solution.py
@@ -207,7 +207,7 @@
     )(tokens, weight, gains)
 
 
-def halo_x(field_ref, held, send_sem, recv_sem):
+def halo_x(field_ref, held, send_sem, recv_sem, others=0):
     nx = field_ref.shape[0]
     count = lax.axis_size("inl")
     me = lax.axis_index("inl")
@@ -216,7 +216,7 @@
         pl.semaphore_signal(
             barrier, inc=1, device_id={"inl": lax.rem(me + step + count, count)}, device_id_type=MESH
         )
-    pl.semaphore_wait(barrier, 2)
+    pl.semaphore_wait(barrier, 2 + others)
     copies = []
     for index, step in enumerate((-1, 1)):
         source, target = (0, nx + 1) if step < 0 else (nx - 1, 0)
@@ -315,6 +315,92 @@
     )(field, kernel, gains)
 
 
+def final_kernel(field_ref, kernel_ref, out_ref, held, spread, shifted, parts, inbox, send_sem, recv_sem, sum_send, sum_recv):
+    count = lax.axis_size("section")
+    me = lax.axis_index("section")
+    for step in range(1, count):
+        pl.semaphore_signal(
+            pltpu.get_barrier_semaphore(),
+            inc=1,
+            device_id={"section": lax.rem(me + step, count)},
+            device_id_type=MESH,
+        )
+    halo_x(field_ref, held, send_sem, recv_sem, count - 1)
+    nx, ny_in, nz, channels = field_ref.shape
+    ny = ny_in - 2
+    cells = nx * ny * nz
+    outch = kernel_ref.shape[1]
+    planes = (nx + 2) * ny_in
+    edge = jnp.zeros((planes, 1, channels), jnp.float32)
+    shifted[:, 0:1] = edge
+    shifted[:, nz + 1 : nz + 2] = edge
+    shifted[:, 1 : nz + 1] = held[...].reshape(planes, nz, channels).astype(jnp.float32)
+    spread[0] = shifted[:, 0:nz].astype(spread.dtype).reshape(held.shape)
+    spread[1] = held[...]
+    spread[2] = shifted[:, 2 : nz + 2].astype(spread.dtype).reshape(held.shape)
+    total = jnp.zeros((outch, cells), jnp.float32)
+    for offset_x in range(3):
+        for offset_y in range(3):
+            for offset_z in range(3):
+                window = spread[offset_z, offset_x : offset_x + nx, offset_y : offset_y + ny].reshape(cells, channels)
+                total = total + lax.dot_general(
+                    kernel_ref[(offset_x * 3 + offset_y) * 3 + offset_z],
+                    window,
+                    (((1,), (1,)), ((), ())),
+                    preferred_element_type=jnp.float32,
+                )
+    block = outch // count
+    for peer in range(count):
+        parts[peer] = total[peer * block : (peer + 1) * block]
+    sends = []
+    for step in range(1, count):
+        peer = lax.rem(me + step, count)
+        copy = pltpu.make_async_remote_copy(
+            src_ref=parts.at[peer],
+            dst_ref=inbox.at[step],
+            send_sem=sum_send.at[step],
+            recv_sem=sum_recv.at[step],
+            device_id={"section": peer},
+            device_id_type=MESH,
+        )
+        copy.start()
+        sends.append(copy)
+    result = parts[me]
+    for step in range(1, count):
+        sends[step - 1].wait_recv()
+        result = result + inbox[step]
+    for copy in sends:
+        copy.wait_send()
+    out_ref[...] = result.reshape(out_ref.shape).astype(out_ref.dtype)
+
+
+def final_stage(field, kernel, collective):
+    nx, ny_in, nz, channels = field.shape
+    ny = ny_in - 2
+    count = lax.axis_size("section")
+    outch = kernel.shape[1]
+    padded = (nx + 2, ny_in, nz, channels)
+    block = outch // count
+    return pl.pallas_call(
+        final_kernel,
+        out_shape=jax.ShapeDtypeStruct((block, nx, ny * nz), jnp.bfloat16),
+        in_specs=[pl.BlockSpec(memory_space=pltpu.VMEM)] * 2,
+        out_specs=pl.BlockSpec(memory_space=pltpu.VMEM),
+        scratch_shapes=[
+            pltpu.VMEM(padded, field.dtype),
+            pltpu.VMEM((3,) + padded, field.dtype),
+            pltpu.VMEM(((nx + 2) * ny_in, nz + 2, channels), jnp.float32),
+            pltpu.VMEM((count, block, nx * ny * nz), jnp.float32),
+            pltpu.VMEM((count, block, nx * ny * nz), jnp.float32),
+            pltpu.SemaphoreType.DMA((2,)),
+            pltpu.SemaphoreType.DMA((2,)),
+            pltpu.SemaphoreType.DMA((count,)),
+            pltpu.SemaphoreType.DMA((count,)),
+        ],
+        compiler_params=pltpu.CompilerParams(collective_id=collective, has_side_effects=True),
+    )(field, kernel)
+
+
 def local(skips, deconv_weight, norm_gain, conv_in, conv_out):
     inl_size = lax.axis_size("inl")
     tokens_here = skips[0]
@@ -333,10 +419,7 @@
         .reshape(cell_x, 2 * lines, cell_z, channels)
     )
     merged = conv_stage(field, conv_in[0], gains, True, 1)
-    partial = conv_stage(merged, conv_out[0], gains, False, 2)
-    outch = partial.shape[-1]
-    rows = partial.reshape(-1, outch).T.reshape(outch, cell_x, cell_y * cell_z)
-    return reduce_scatter(rows)
+    return final_stage(merged, conv_out[0], 2)
 
 
 def solution(mesh):

time: 52.9 us -> 49.3 us (0.932); the launches traced: 52.6 us -> 48.4 us
  Pallas kernels: 47.4 us -> 45.1 us
  local copies, waits for them, and re-layouts: 5.2 us -> 3.28 us
    pallas_call x2 -> x1, Pallas kernels: 16.2 us -> 8.37 us  [conv_stage(): pl.pallas_call(functools.partial(conv_kernel, residual), out_shape=jax.Sh...]
    pallas_call x1, Pallas kernels: 7.16 us -> 12.8 us  [final_stage(): pl.pallas_call(final_kernel, out_shape=jax.ShapeDtypeStruct((block, nx, n...]
    reshape x1 -> x0, local copies, waits for them, and re-layouts: 1.21 us -> none  [local(): rows = partial.reshape(-1, outch).T.reshape(outch, cell_x, cell_y * cell_z)]
    another operation x1 -> x0, local copies, waits for them, and re-layouts: 0.71 us -> none  [reduce_scatter(): shaped = parts.reshape((count, parts.shape[0] // count) + parts.shape[1:])]
where the time goes in v7:
time: 49.3 us; the launch traced here: 48.4 us
  Pallas kernels  45.1 us (91%)
  local copies, waits for them, and re-layouts  3.28 us (7%)
    pallas_call x1, Pallas kernels, gather_bricks(): pl.pallas_call(gather_kernel, out_shape=jax.ShapeDtypeStruct(shape, jnp.b...  24 us
    pallas_call x1, Pallas kernels, final_stage(): pl.pallas_call(final_kernel, out_shape=jax.ShapeDtypeStruct((block, nx, n...  12.8 us
    pallas_call x1, Pallas kernels, conv_stage(): pl.pallas_call(functools.partial(conv_kernel, residual), out_shape=jax.Sh...  8.37 us
    reshape x1, local copies, waits for them, and re-layouts, local(): brick.reshape(lines, PXD, GZ, 2, 2, 2, channels)  1.95 us
    unnamed x1, local copies, waits for them, and re-layouts  1.33 us

profile of v7, /device:TPU:3, one launch (start us, length us, event | category | flops | bytes accessed | tf_op | source)
XLA Modules:
  0.0 48.4 jit_solution(9399213969669305709)
XLA Ops:
  0.0 24.0 %shard_map.55 = bf16[10,16,1024]{2,1,0:T(8,128)(2,1)} custom-call(bf16[128,1024]{1,0:T(8,128)(2,1)} %bitcast.13, bf16[1024,1024]{1,0:T(8,128)(2,1)} %bitcast.9, f32[2,128]{1,0:T(2,128)} %bitcast.15), custom_call_target="tpu_custom_call" | custom-call | tf_op jit(solution)/shard_map/pallas_call | solution.py:189
  24.0 1.9 %copy.6 = bf16[10,2,8,2,2,2,128]{6,5,2,4,0,3,1:T(2,128)(2,1)} copy(bf16[10,2,8,2,2,2,128]{6,2,5,4,3,1,0:T(8,128)(2,1)} %bitcast.11) | data formatting | bytes 655360 | tf_op jit(solution)/shard_map/reshape | solution.py:417
  26.0 8.4 %shard_map.56.field_ref = bf16[4,18,16,128]{3,2,1,0:T(8,128)(2,1)} custom-call(bf16[4,20,16,128]{3,2,1,0:T(8,128)(2,1)} %bitcast.10, bf16[27,128,128]{2,1,0:T(8,128)(2,1)} %bitcast.12, f32[2,128]{1,0:T(2,128)} %bitcast.16), custom_call_target="tpu_custom_call" | custom-call | tf_op jit(solution)/shard_map/pallas_call | solution.py:303
  34.3 12.8 %shard_map.57 = bf16[8,4,256]{2,1,0:T(4,128)(2,1)} custom-call(bf16[4,18,16,128]{3,2,1,0:T(8,128)(2,1)} %shard_map.56.field_ref, bf16[27,32,128]{2,1,0:T(8,128)(2,1)} %bitcast.14), custom_call_target="tpu_custom_call" | custom-call | tf_op jit(solution)/shard_map/pallas_call | solution.py:384
  47.1 1.3 %copy.8 = bf16[8,4,256]{2,1,0:T(4,128)(2,1)} copy(bf16[8,4,256]{2,1,0:T(4,128)(2,1)} %shard_map.57) | data formatting | bytes 32768

commit v8 on v7

--- a/solution.py
+++ b/solution.py
@@ -211,12 +211,13 @@
     nx = field_ref.shape[0]
     count = lax.axis_size("inl")
     me = lax.axis_index("inl")
-    barrier = pltpu.get_barrier_semaphore()
-    for step in (-1, 1):
-        pl.semaphore_signal(
-            barrier, inc=1, device_id={"inl": lax.rem(me + step + count, count)}, device_id_type=MESH
-        )
-    pl.semaphore_wait(barrier, 2 + others)
+    if others is not None:
+        barrier = pltpu.get_barrier_semaphore()
+        for step in (-1, 1):
+            pl.semaphore_signal(
+                barrier, inc=1, device_id={"inl": lax.rem(me + step + count, count)}, device_id_type=MESH
+            )
+        pl.semaphore_wait(barrier, 2 + others)
     copies = []
     for index, step in enumerate((-1, 1)):
         source, target = (0, nx + 1) if step < 0 else (nx - 1, 0)
@@ -401,6 +402,132 @@
     )(field, kernel)
 
 
+def block_kernel(
+    field_ref, kernel_in_ref, gains_ref, kernel_out_ref, out_ref,
+    held, shifted, mixed, held_out, spread, shifted_out, parts, inbox,
+    send_sem, recv_sem, send_out, recv_out, sum_send, sum_recv,
+):
+    count = lax.axis_size("section")
+    me = lax.axis_index("section")
+    for step in range(1, count):
+        pl.semaphore_signal(
+            pltpu.get_barrier_semaphore(),
+            inc=1,
+            device_id={"section": lax.rem(me + step, count)},
+            device_id_type=MESH,
+        )
+    halo_x(field_ref, held, send_sem, recv_sem, count - 1)
+    nx, ny_in, nz, channels = field_ref.shape
+    ny = ny_in - 2
+    cells = nx * ny * nz
+    width = channels
+    parts_in = []
+    for offset_z in range(3):
+        part = jnp.zeros((cells, width), jnp.float32)
+        for offset_x in range(3):
+            for offset_y in range(3):
+                window = held[offset_x : offset_x + nx, offset_y : offset_y + ny].reshape(cells, channels)
+                tap = kernel_in_ref[(offset_x * 3 + offset_y) * 3 + offset_z]
+                part = part + jnp.dot(window, tap, preferred_element_type=jnp.float32)
+        parts_in.append(part.reshape(nx * ny, nz, width))
+    edge = jnp.zeros((nx * ny, 1, width), jnp.float32)
+    shifted[:, 0:1] = edge
+    shifted[:, nz + 1 : nz + 2] = edge
+    shifted[:, 1 : nz + 1] = parts_in[0]
+    total = parts_in[1] + shifted[:, 0:nz]
+    shifted[:, 1 : nz + 1] = parts_in[2]
+    total = total + shifted[:, 2 : nz + 2]
+    mean_square = jnp.mean(total * total, axis=-1, keepdims=True)
+    normed = total * lax.rsqrt(mean_square + epsilon) * gains_ref[1:2, :]
+    base = field_ref[:, 1 : ny + 1].reshape(nx * ny, nz, channels).astype(jnp.float32)
+    activated = gelu_tanh(normed + base).reshape(nx, ny, nz, channels)
+    me_y, count_y = lax.axis_index("xln"), lax.axis_size("xln")
+    row = lax.broadcasted_iota(jnp.int32, activated.shape, 1)
+    outside = ((row == 0) & (me_y == 0)) | ((row == ny - 1) & (me_y == count_y - 1))
+    mixed[...] = jnp.where(outside, 0.0, activated).astype(mixed.dtype)
+
+    halo_x(mixed, held_out, send_out, recv_out, None)
+    ny_out = ny - 2
+    cells_out = nx * ny_out * nz
+    outch = kernel_out_ref.shape[1]
+    planes = (nx + 2) * ny
+    edge = jnp.zeros((planes, 1, channels), jnp.float32)
+    shifted_out[:, 0:1] = edge
+    shifted_out[:, nz + 1 : nz + 2] = edge
+    shifted_out[:, 1 : nz + 1] = held_out[...].reshape(planes, nz, channels).astype(jnp.float32)
+    spread[0] = shifted_out[:, 0:nz].astype(spread.dtype).reshape(held_out.shape)
+    spread[1] = held_out[...]
+    spread[2] = shifted_out[:, 2 : nz + 2].astype(spread.dtype).reshape(held_out.shape)
+    result_t = jnp.zeros((outch, cells_out), jnp.float32)
+    for offset_x in range(3):
+        for offset_y in range(3):
+            for offset_z in range(3):
+                window = spread[offset_z, offset_x : offset_x + nx, offset_y : offset_y + ny_out].reshape(
+                    cells_out, channels
+                )
+                result_t = result_t + lax.dot_general(
+                    kernel_out_ref[(offset_x * 3 + offset_y) * 3 + offset_z],
+                    window,
+                    (((1,), (1,)), ((), ())),
+                    preferred_element_type=jnp.float32,
+                )
+    block = outch // count
+    for peer in range(count):
+        parts[peer] = result_t[peer * block : (peer + 1) * block]
+    sends = []
+    for step in range(1, count):
+        peer = lax.rem(me + step, count)
+        copy = pltpu.make_async_remote_copy(
+            src_ref=parts.at[peer],
+            dst_ref=inbox.at[step],
+            send_sem=sum_send.at[step],
+            recv_sem=sum_recv.at[step],
+            device_id={"section": peer},
+            device_id_type=MESH,
+        )
+        copy.start()
+        sends.append(copy)
+    result = parts[me]
+    for step in range(1, count):
+        sends[step - 1].wait_recv()
+        result = result + inbox[step]
+    for copy in sends:
+        copy.wait_send()
+    out_ref[...] = result.reshape(out_ref.shape).astype(out_ref.dtype)
+
+
+def decoder_block(field, kernel_in, gains, kernel_out, collective):
+    nx, ny_in, nz, channels = field.shape
+    ny = ny_in - 2
+    ny_out = ny - 2
+    count = lax.axis_size("section")
+    outch = kernel_out.shape[1]
+    block = outch // count
+    return pl.pallas_call(
+        block_kernel,
+        out_shape=jax.ShapeDtypeStruct((block, nx, ny_out * nz), jnp.bfloat16),
+        in_specs=[pl.BlockSpec(memory_space=pltpu.VMEM)] * 4,
+        out_specs=pl.BlockSpec(memory_space=pltpu.VMEM),
+        scratch_shapes=[
+            pltpu.VMEM((nx + 2, ny_in, nz, channels), field.dtype),
+            pltpu.VMEM((nx * ny, nz + 2, channels), jnp.float32),
+            pltpu.VMEM((nx, ny, nz, channels), field.dtype),
+            pltpu.VMEM((nx + 2, ny, nz, channels), field.dtype),
+            pltpu.VMEM((3, nx + 2, ny, nz, channels), field.dtype),
+            pltpu.VMEM(((nx + 2) * ny, nz + 2, channels), jnp.float32),
+            pltpu.VMEM((count, block, nx * ny_out * nz), jnp.float32),
+            pltpu.VMEM((count, block, nx * ny_out * nz), jnp.float32),
+            pltpu.SemaphoreType.DMA((2,)),
+            pltpu.SemaphoreType.DMA((2,)),
+            pltpu.SemaphoreType.DMA((2,)),
+            pltpu.SemaphoreType.DMA((2,)),
+            pltpu.SemaphoreType.DMA((count,)),
+            pltpu.SemaphoreType.DMA((count,)),
+        ],
+        compiler_params=pltpu.CompilerParams(collective_id=collective, has_side_effects=True),
+    )(field, kernel_in, gains, kernel_out)
+
+
 def local(skips, deconv_weight, norm_gain, conv_in, conv_out):
     inl_size = lax.axis_size("inl")
     tokens_here = skips[0]
@@ -418,8 +545,7 @@
         .transpose(1, 3, 0, 4, 2, 5, 6)
         .reshape(cell_x, 2 * lines, cell_z, channels)
     )
-    merged = conv_stage(field, conv_in[0], gains, True, 1)
-    return final_stage(merged, conv_out[0], 2)
+    return decoder_block(field, conv_in[0], gains, conv_out[0], 1)
 
 
 def solution(mesh):

time: 49.3 us -> 49.4 us (level); the launches traced: 48.4 us -> 49.1 us
  Pallas kernels: 45.1 us -> 45.8 us
    pallas_call x2 -> x1, Pallas kernels: 21.1 us -> 21.8 us  [decoder_block(): pl.pallas_call(block_kernel, out_shape=jax.ShapeDtypeStruct((block, nx, n...]
where the time goes in v8:
time: 49.4 us; the launch traced here: 49.1 us
  Pallas kernels  45.8 us (93%)
  local copies, waits for them, and re-layouts  3.28 us (7%)
    pallas_call x1, Pallas kernels, gather_bricks(): pl.pallas_call(gather_kernel, out_shape=jax.ShapeDtypeStruct(shape, jnp.b...  24 us
    pallas_call x1, Pallas kernels, decoder_block(): pl.pallas_call(block_kernel, out_shape=jax.ShapeDtypeStruct((block, nx, n...  21.8 us
    reshape x1, local copies, waits for them, and re-layouts, local(): brick.reshape(lines, PXD, GZ, 2, 2, 2, channels)  1.95 us
    unnamed x1, local copies, waits for them, and re-layouts  1.33 us

profile of v8, /device:TPU:3, one launch (start us, length us, event | category | flops | bytes accessed | tf_op | source)
XLA Modules:
  0.0 49.1 jit_solution(10543310408782424069)
XLA Ops:
  0.0 24.0 %shard_map.55 = bf16[10,16,1024]{2,1,0:T(8,128)(2,1)} custom-call(bf16[128,1024]{1,0:T(8,128)(2,1)} %bitcast.13, bf16[1024,1024]{1,0:T(8,128)(2,1)} %bitcast.9, f32[2,128]{1,0:T(2,128)} %bitcast.15), custom_call_target="tpu_custom_call" | custom-call | tf_op jit(solution)/shard_map/pallas_call | solution.py:189
  24.0 1.9 %copy.6 = bf16[10,2,8,2,2,2,128]{6,5,2,4,0,3,1:T(2,128)(2,1)} copy(bf16[10,2,8,2,2,2,128]{6,2,5,4,3,1,0:T(8,128)(2,1)} %bitcast.10) | data formatting | bytes 655360 | tf_op jit(solution)/shard_map/reshape | solution.py:544
  26.0 21.8 %shard_map.56 = bf16[8,4,256]{2,1,0:T(4,128)(2,1)} custom-call(bf16[4,20,16,128]{3,2,1,0:T(8,128)(2,1)} %bitcast.11, bf16[27,128,128]{2,1,0:T(8,128)(2,1)} %bitcast.12, f32[2,128]{1,0:T(2,128)} %bitcast.16, bf16[27,32,128]{2,1,0:T(8,128)(2,1)} %bitcast.14), custom_call_target="tpu_custom_call" | custom-call | tf_op jit(solution)/shard_map/pallas_call | solution.py:506
  47.7 1.3 %copy.8 = bf16[8,4,256]{2,1,0:T(4,128)(2,1)} copy(bf16[8,4,256]{2,1,0:T(4,128)(2,1)} %shard_map.56) | data formatting | bytes 32768

commit v9 on v8

--- a/solution.py
+++ b/solution.py
@@ -133,11 +133,12 @@
     copies = []
     for index, (column, slot, exists) in enumerate(groups):
         live = True if exists is None else exists
-        for other in range(count):
+        for turn in range(count):
+            other = lax.rem(me_y + turn, count)
             copy = pltpu.make_async_remote_copy(
-                src_ref=field.at[pl.ds(other * rows, rows)],
+                src_ref=field.at[pl.ds(pl.multiple_of(other * rows, rows), rows)],
                 dst_ref=held.at[slot],
-                send_sem=send_sem.at[index * count + other],
+                send_sem=send_sem.at[index * count + turn],
                 recv_sem=recv_sem.at[slot],
                 device_id={"inl": other, "xln": column},
                 device_id_type=MESH,

time: 49.4 us -> 49.4 us (level)
  no operation moved by 1% of the time
where the time goes in v9:
time: 49.4 us; the launch traced here: 49.1 us
  Pallas kernels  45.8 us (93%)
  local copies, waits for them, and re-layouts  3.28 us (7%)
    pallas_call x1, Pallas kernels, gather_bricks(): pl.pallas_call(gather_kernel, out_shape=jax.ShapeDtypeStruct(shape, jnp.b...  24 us
    pallas_call x1, Pallas kernels, decoder_block(): pl.pallas_call(block_kernel, out_shape=jax.ShapeDtypeStruct((block, nx, n...  21.8 us
    reshape x1, local copies, waits for them, and re-layouts, local(): brick.reshape(lines, PXD, GZ, 2, 2, 2, channels)  1.95 us
    unnamed x1, local copies, waits for them, and re-layouts  1.33 us

profile of v9, /device:TPU:3, one launch (start us, length us, event | category | flops | bytes accessed | tf_op | source)
XLA Modules:
  0.0 49.1 jit_solution(9525175544288941656)
XLA Ops:
  0.0 24.0 %shard_map.55 = bf16[10,16,1024]{2,1,0:T(8,128)(2,1)} custom-call(bf16[128,1024]{1,0:T(8,128)(2,1)} %bitcast.13, bf16[1024,1024]{1,0:T(8,128)(2,1)} %bitcast.9, f32[2,128]{1,0:T(2,128)} %bitcast.15), custom_call_target="tpu_custom_call" | custom-call | tf_op jit(solution)/shard_map/pallas_call | solution.py:190
  24.0 1.9 %copy.6 = bf16[10,2,8,2,2,2,128]{6,5,2,4,0,3,1:T(2,128)(2,1)} copy(bf16[10,2,8,2,2,2,128]{6,2,5,4,3,1,0:T(8,128)(2,1)} %bitcast.10) | data formatting | bytes 655360 | tf_op jit(solution)/shard_map/reshape | solution.py:545
  25.9 21.8 %shard_map.56 = bf16[8,4,256]{2,1,0:T(4,128)(2,1)} custom-call(bf16[4,20,16,128]{3,2,1,0:T(8,128)(2,1)} %bitcast.11, bf16[27,128,128]{2,1,0:T(8,128)(2,1)} %bitcast.12, f32[2,128]{1,0:T(2,128)} %bitcast.16, bf16[27,32,128]{2,1,0:T(8,128)(2,1)} %bitcast.14), custom_call_target="tpu_custom_call" | custom-call | tf_op jit(solution)/shard_map/pallas_call | solution.py:507
  47.7 1.3 %copy.8 = bf16[8,4,256]{2,1,0:T(4,128)(2,1)} copy(bf16[8,4,256]{2,1,0:T(4,128)(2,1)} %shard_map.56) | data formatting | bytes 32768

commit v10 on v9

--- a/solution.py
+++ b/solution.py
@@ -215,10 +215,13 @@
     if others is not None:
         barrier = pltpu.get_barrier_semaphore()
         for step in (-1, 1):
-            pl.semaphore_signal(
-                barrier, inc=1, device_id={"inl": lax.rem(me + step + count, count)}, device_id_type=MESH
-            )
-        pl.semaphore_wait(barrier, 2 + others)
+
+            @pl.when((me + step >= 0) & (me + step < count))
+            def _():
+                pl.semaphore_signal(barrier, inc=1, device_id={"inl": me + step}, device_id_type=MESH)
+
+        present = (me > 0).astype(jnp.int32) + (me < count - 1).astype(jnp.int32)
+        pl.semaphore_wait(barrier, present + others)
     copies = []
     for index, step in enumerate((-1, 1)):
         source, target = (0, nx + 1) if step < 0 else (nx - 1, 0)

time: 49.4 us -> 49.4 us (level)
  no operation moved by 1% of the time
where the time goes in v10:
time: 49.4 us; the launch traced here: 49.1 us
  Pallas kernels  45.8 us (93%)
  local copies, waits for them, and re-layouts  3.28 us (7%)
    pallas_call x1, Pallas kernels, gather_bricks(): pl.pallas_call(gather_kernel, out_shape=jax.ShapeDtypeStruct(shape, jnp.b...  24 us
    pallas_call x1, Pallas kernels, decoder_block(): pl.pallas_call(block_kernel, out_shape=jax.ShapeDtypeStruct((block, nx, n...  21.8 us
    reshape x1, local copies, waits for them, and re-layouts, local(): brick.reshape(lines, PXD, GZ, 2, 2, 2, channels)  1.95 us
    unnamed x1, local copies, waits for them, and re-layouts  1.33 us

profile of v10, /device:TPU:3, one launch (start us, length us, event | category | flops | bytes accessed | tf_op | source)
XLA Modules:
  0.0 49.1 jit_solution(6341225623937098995)
XLA Ops:
  0.0 24.0 %shard_map.55 = bf16[10,16,1024]{2,1,0:T(8,128)(2,1)} custom-call(bf16[128,1024]{1,0:T(8,128)(2,1)} %bitcast.13, bf16[1024,1024]{1,0:T(8,128)(2,1)} %bitcast.9, f32[2,128]{1,0:T(2,128)} %bitcast.15), custom_call_target="tpu_custom_call" | custom-call | tf_op jit(solution)/shard_map/pallas_call | solution.py:190
  24.0 1.9 %copy.6 = bf16[10,2,8,2,2,2,128]{6,5,2,4,0,3,1:T(2,128)(2,1)} copy(bf16[10,2,8,2,2,2,128]{6,2,5,4,3,1,0:T(8,128)(2,1)} %bitcast.10) | data formatting | bytes 655360 | tf_op jit(solution)/shard_map/reshape | solution.py:548
  25.9 21.8 %shard_map.56 = bf16[8,4,256]{2,1,0:T(4,128)(2,1)} custom-call(bf16[4,20,16,128]{3,2,1,0:T(8,128)(2,1)} %bitcast.11, bf16[27,128,128]{2,1,0:T(8,128)(2,1)} %bitcast.12, f32[2,128]{1,0:T(2,128)} %bitcast.16, bf16[27,32,128]{2,1,0:T(8,128)(2,1)} %bitcast.14), custom_call_target="tpu_custom_call" | custom-call | tf_op jit(solution)/shard_map/pallas_call | solution.py:510
  47.7 1.3 %copy.8 = bf16[8,4,256]{2,1,0:T(4,128)(2,1)} copy(bf16[8,4,256]{2,1,0:T(4,128)(2,1)} %shard_map.56) | data formatting | bytes 32768

commit v11 on v6

--- a/solution.py
+++ b/solution.py
@@ -15,66 +15,8 @@
 epsilon = 1e-05
 
 
-def normalize(values, scale):
-    mean_square = jnp.mean(values * values, axis=-1, keepdims=True)
-    return values * lax.rsqrt(mean_square + epsilon) * scale
-
-
-def activate(upsampled, gains):
-    width = gains.shape[1]
-    shaped = upsampled.reshape(upsampled.shape[:-1] + (upsampled.shape[-1] // width, width))
-    result = jax.nn.gelu(normalize(shaped, gains[0]), approximate=True).astype(jnp.bfloat16)
-    return result.reshape(upsampled.shape)
-
-
 def gelu_tanh(values):
     return 0.5 * values * (1.0 + jnp.tanh(0.7978845608028654 * (values + 0.044715 * (values * values * values))))
-
-
-def reduce_scatter_kernel(count, parts_ref, out_ref, held, send_sem, recv_sem):
-    me = lax.axis_index("section")
-    barrier = pltpu.get_barrier_semaphore()
-    for step in range(1, count):
-        peer = lax.rem(me + step, count)
-        pl.semaphore_signal(barrier, inc=1, device_id={"section": peer}, device_id_type=MESH)
-    pl.semaphore_wait(barrier, count - 1)
-    sends = []
-    for step in range(1, count):
-        peer = lax.rem(me + step, count)
-        copy = pltpu.make_async_remote_copy(
-            src_ref=parts_ref.at[peer],
-            dst_ref=held.at[step],
-            send_sem=send_sem.at[step],
-            recv_sem=recv_sem.at[step],
-            device_id={"section": peer},
-            device_id_type=MESH,
-        )
-        copy.start()
-        sends.append(copy)
-    total = parts_ref[me]
-    for step in range(1, count):
-        sends[step - 1].wait_recv()
-        total = total + held[step]
-    for copy in sends:
-        copy.wait_send()
-    out_ref[...] = total.astype(out_ref.dtype)
-
-
-def reduce_scatter(parts):
-    count = lax.axis_size("section")
-    shaped = parts.reshape((count, parts.shape[0] // count) + parts.shape[1:])
-    return pl.pallas_call(
-        functools.partial(reduce_scatter_kernel, count),
-        out_shape=jax.ShapeDtypeStruct(shaped.shape[1:], jnp.bfloat16),
-        in_specs=[pl.BlockSpec(memory_space=pltpu.VMEM)],
-        out_specs=pl.BlockSpec(memory_space=pltpu.VMEM),
-        scratch_shapes=[
-            pltpu.VMEM(shaped.shape, jnp.float32),
-            pltpu.SemaphoreType.DMA((count,)),
-            pltpu.SemaphoreType.DMA((count,)),
-        ],
-        compiler_params=pltpu.CompilerParams(collective_id=0, has_side_effects=True),
-    )(shaped)
 
 
 def send_groups(me_x, me_y, count):
@@ -133,11 +75,12 @@
     copies = []
     for index, (column, slot, exists) in enumerate(groups):
         live = True if exists is None else exists
-        for other in range(count):
+        for turn in range(count):
+            other = lax.rem(me_y + turn, count)
             copy = pltpu.make_async_remote_copy(
-                src_ref=field.at[pl.ds(other * rows, rows)],
+                src_ref=field.at[pl.ds(pl.multiple_of(other * rows, rows), rows)],
                 dst_ref=held.at[slot],
-                send_sem=send_sem.at[index * count + other],
+                send_sem=send_sem.at[index * count + turn],
                 recv_sem=recv_sem.at[slot],
                 device_id={"inl": other, "xln": column},
                 device_id_type=MESH,
@@ -207,16 +150,20 @@
     )(tokens, weight, gains)
 
 
-def halo_x(field_ref, held, send_sem, recv_sem):
+def halo_x(field_ref, held, send_sem, recv_sem, others=0):
     nx = field_ref.shape[0]
     count = lax.axis_size("inl")
     me = lax.axis_index("inl")
-    barrier = pltpu.get_barrier_semaphore()
-    for step in (-1, 1):
-        pl.semaphore_signal(
-            barrier, inc=1, device_id={"inl": lax.rem(me + step + count, count)}, device_id_type=MESH
-        )
-    pl.semaphore_wait(barrier, 2)
+    if others is not None:
+        barrier = pltpu.get_barrier_semaphore()
+        for step in (-1, 1):
+
+            @pl.when((me + step >= 0) & (me + step < count))
+            def _():
+                pl.semaphore_signal(barrier, inc=1, device_id={"inl": me + step}, device_id_type=MESH)
+
+        present = (me > 0).astype(jnp.int32) + (me < count - 1).astype(jnp.int32)
+        pl.semaphore_wait(barrier, present + others)
     copies = []
     for index, step in enumerate((-1, 1)):
         source, target = (0, nx + 1) if step < 0 else (nx - 1, 0)
@@ -252,67 +199,126 @@
             copy.wait_send()
 
 
-def conv_kernel(
-    residual, field_ref, kernel_ref, gains_ref, out_ref, held, shifted, send_sem, recv_sem
+def block_kernel(
+    field_ref, kernel_in_ref, gains_ref, kernel_out_ref, out_ref,
+    held, shifted, mixed, held_out, shifted_out, parts, inbox,
+    send_sem, recv_sem, send_out, recv_out, sum_send, sum_recv,
 ):
-    halo_x(field_ref, held, send_sem, recv_sem)
+    count = lax.axis_size("section")
+    me = lax.axis_index("section")
+    for step in range(1, count):
+        pl.semaphore_signal(
+            pltpu.get_barrier_semaphore(),
+            inc=1,
+            device_id={"section": lax.rem(me + step, count)},
+            device_id_type=MESH,
+        )
+    halo_x(field_ref, held, send_sem, recv_sem, count - 1)
     nx, ny_in, nz, channels = field_ref.shape
     ny = ny_in - 2
     cells = nx * ny * nz
-    width = shifted.shape[2]
-    parts = []
+    width = channels
+    parts_in = []
     for offset_z in range(3):
         part = jnp.zeros((cells, width), jnp.float32)
         for offset_x in range(3):
             for offset_y in range(3):
                 window = held[offset_x : offset_x + nx, offset_y : offset_y + ny].reshape(cells, channels)
-                tap = kernel_ref[(offset_x * 3 + offset_y) * 3 + offset_z]
-                if residual:
-                    part = part + jnp.dot(window, tap, preferred_element_type=jnp.float32)
-                else:
-                    part = part + lax.dot_general(
-                        window, tap, (((1,), (1,)), ((), ())), preferred_element_type=jnp.float32
-                    )
-        parts.append(part.reshape(nx * ny, nz, width))
+                tap = kernel_in_ref[(offset_x * 3 + offset_y) * 3 + offset_z]
+                part = part + jnp.dot(window, tap, preferred_element_type=jnp.float32)
+        parts_in.append(part.reshape(nx * ny, nz, width))
     edge = jnp.zeros((nx * ny, 1, width), jnp.float32)
     shifted[:, 0:1] = edge
     shifted[:, nz + 1 : nz + 2] = edge
-    shifted[:, 1 : nz + 1] = parts[0]
-    total = parts[1] + shifted[:, 0:nz]
-    shifted[:, 1 : nz + 1] = parts[2]
+    shifted[:, 1 : nz + 1] = parts_in[0]
+    total = parts_in[1] + shifted[:, 0:nz]
+    shifted[:, 1 : nz + 1] = parts_in[2]
     total = total + shifted[:, 2 : nz + 2]
-    if residual:
-        mean_square = jnp.mean(total * total, axis=-1, keepdims=True)
-        normed = total * lax.rsqrt(mean_square + epsilon) * gains_ref[1:2, :]
-        base = field_ref[:, 1 : ny + 1].reshape(nx * ny, nz, channels).astype(jnp.float32)
-        mixed = gelu_tanh(normed + base).reshape(nx, ny, nz, channels)
-        me_y, count_y = lax.axis_index("xln"), lax.axis_size("xln")
-        row = lax.broadcasted_iota(jnp.int32, mixed.shape, 1)
-        outside = ((row == 0) & (me_y == 0)) | ((row == ny - 1) & (me_y == count_y - 1))
-        out_ref[...] = jnp.where(outside, 0.0, mixed).astype(out_ref.dtype)
-    else:
-        out_ref[...] = total.reshape(out_ref.shape)
-
-
-def conv_stage(field, kernel, gains, residual, collective):
+    mean_square = jnp.mean(total * total, axis=-1, keepdims=True)
+    normed = total * lax.rsqrt(mean_square + epsilon) * gains_ref[1:2, :]
+    base = field_ref[:, 1 : ny + 1].reshape(nx * ny, nz, channels).astype(jnp.float32)
+    activated = gelu_tanh(normed + base).reshape(nx, ny, nz, channels)
+    me_y, count_y = lax.axis_index("xln"), lax.axis_size("xln")
+    row = lax.broadcasted_iota(jnp.int32, activated.shape, 1)
+    outside = ((row == 0) & (me_y == 0)) | ((row == ny - 1) & (me_y == count_y - 1))
+    mixed[...] = jnp.where(outside, 0.0, activated).astype(mixed.dtype)
+
+    halo_x(mixed, held_out, send_out, recv_out, None)
+    ny_out = ny - 2
+    cells_out = nx * ny_out * nz
+    outch = kernel_out_ref.shape[1] // 3
+    columns = jnp.concatenate(
+        [
+            held_out[offset_x : offset_x + nx, offset_y : offset_y + ny_out].reshape(cells_out, channels)
+            for offset_x in range(3)
+            for offset_y in range(3)
+        ],
+        axis=1,
+    )
+    by_depth = jnp.dot(columns, kernel_out_ref[...], preferred_element_type=jnp.float32)
+    planes = nx * ny_out
+    edge = jnp.zeros((planes, 1, outch), jnp.float32)
+    shifted_out[:, 0:1] = edge
+    shifted_out[:, nz + 1 : nz + 2] = edge
+    shifted_out[:, 1 : nz + 1] = by_depth[:, 0:outch].reshape(planes, nz, outch)
+    summed = by_depth[:, outch : 2 * outch].reshape(planes, nz, outch) + shifted_out[:, 0:nz]
+    shifted_out[:, 1 : nz + 1] = by_depth[:, 2 * outch : 3 * outch].reshape(planes, nz, outch)
+    summed = summed + shifted_out[:, 2 : nz + 2]
+    result_t = summed.reshape(cells_out, outch).T
+    block = outch // count
+    for peer in range(count):
+        parts[peer] = result_t[peer * block : (peer + 1) * block]
+    sends = []
+    for step in range(1, count):
+        peer = lax.rem(me + step, count)
+        copy = pltpu.make_async_remote_copy(
+            src_ref=parts.at[peer],
+            dst_ref=inbox.at[step],
+            send_sem=sum_send.at[step],
+            recv_sem=sum_recv.at[step],
+            device_id={"section": peer},
+            device_id_type=MESH,
+        )
+        copy.start()
+        sends.append(copy)
+    result = parts[me]
+    for step in range(1, count):
+        sends[step - 1].wait_recv()
+        result = result + inbox[step]
+    for copy in sends:
+        copy.wait_send()
+    out_ref[...] = result.reshape(out_ref.shape).astype(out_ref.dtype)
+
+
+def decoder_block(field, kernel_in, gains, kernel_out, collective):
     nx, ny_in, nz, channels = field.shape
-    width = kernel.shape[2] if residual else kernel.shape[1]
-    padded = (nx + 2, ny_in, nz, channels)
     ny = ny_in - 2
-    dtype = jnp.bfloat16 if residual else jnp.float32
+    ny_out = ny - 2
+    count = lax.axis_size("section")
+    outch = kernel_out.shape[1] // 3
+    block = outch // count
     return pl.pallas_call(
-        functools.partial(conv_kernel, residual),
-        out_shape=jax.ShapeDtypeStruct((nx, ny, nz, width), dtype),
-        in_specs=[pl.BlockSpec(memory_space=pltpu.VMEM)] * 3,
+        block_kernel,
+        out_shape=jax.ShapeDtypeStruct((block, nx, ny_out * nz), jnp.bfloat16),
+        in_specs=[pl.BlockSpec(memory_space=pltpu.VMEM)] * 4,
         out_specs=pl.BlockSpec(memory_space=pltpu.VMEM),
         scratch_shapes=[
-            pltpu.VMEM(padded, field.dtype),
-            pltpu.VMEM((nx * ny, nz + 2, width), jnp.float32),
+            pltpu.VMEM((nx + 2, ny_in, nz, channels), field.dtype),
+            pltpu.VMEM((nx * ny, nz + 2, channels), jnp.float32),
+            pltpu.VMEM((nx, ny, nz, channels), field.dtype),
+            pltpu.VMEM((nx + 2, ny, nz, channels), field.dtype),
+            pltpu.VMEM((nx * ny_out, nz + 2, outch), jnp.float32),
+            pltpu.VMEM((count, block, nx * ny_out * nz), jnp.float32),
+            pltpu.VMEM((count, block, nx * ny_out * nz), jnp.float32),
             pltpu.SemaphoreType.DMA((2,)),
             pltpu.SemaphoreType.DMA((2,)),
+            pltpu.SemaphoreType.DMA((2,)),
+            pltpu.SemaphoreType.DMA((2,)),
+            pltpu.SemaphoreType.DMA((count,)),
+            pltpu.SemaphoreType.DMA((count,)),
         ],
         compiler_params=pltpu.CompilerParams(collective_id=collective, has_side_effects=True),
-    )(field, kernel, gains)
+    )(field, kernel_in, gains, kernel_out)
 
 
 def local(skips, deconv_weight, norm_gain, conv_in, conv_out):
@@ -332,11 +338,11 @@
         .transpose(1, 3, 0, 4, 2, 5, 6)
         .reshape(cell_x, 2 * lines, cell_z, channels)
     )
-    merged = conv_stage(field, conv_in[0], gains, True, 1)
-    partial = conv_stage(merged, conv_out[0], gains, False, 2)
-    outch = partial.shape[-1]
-    rows = partial.reshape(-1, outch).T.reshape(outch, cell_x, cell_y * cell_z)
-    return reduce_scatter(rows)
+    taps, outch, channels_in = conv_out.shape[1:]
+    out_weight = (
+        conv_out[0].reshape(taps // 3, 3, outch, channels_in).transpose(0, 3, 1, 2).reshape(-1, 3 * outch)
+    )
+    return decoder_block(field, conv_in[0], gains, out_weight, 1)
 
 
 def solution(mesh):

time: 52.9 us -> 47.5 us (0.90)
  Pallas kernels: 47.4 us -> 42.8 us
  local copies, waits for them, and re-layouts: 5.2 us -> 4.36 us
    pallas_call x3 -> x1, Pallas kernels: 23.4 us -> 18.7 us  [decoder_block(): pl.pallas_call(block_kernel, out_shape=jax.ShapeDtypeStruct((block, nx, n...]
    another operation x1, local copies, waits for them, and re-layouts: 0.71 us -> 0.11 us  [local(): conv_out[0].reshape(taps // 3, 3, outch, channels_in).transpose(0, 3, 1, 2)]
    unnamed x1 -> x4, local copies, waits for them, and re-layouts: 1.33 us -> 1.4 us
where the time goes in v11:
time: 47.5 us; the launch traced here: 47.1 us
  Pallas kernels  42.8 us (90%)
  local copies, waits for them, and re-layouts  4.36 us (9%)
    pallas_call x1, Pallas kernels, gather_bricks(): pl.pallas_call(gather_kernel, out_shape=jax.ShapeDtypeStruct(shape, jnp.b...  24 us
    pallas_call x1, Pallas kernels, decoder_block(): pl.pallas_call(block_kernel, out_shape=jax.ShapeDtypeStruct((block, nx, n...  18.7 us
    reshape x1, local copies, waits for them, and re-layouts, local(): brick.reshape(lines, PXD, GZ, 2, 2, 2, channels)  1.95 us
    unnamed x4, local copies, waits for them, and re-layouts  1.4 us

profile of v11, /device:TPU:3, one launch (start us, length us, event | category | flops | bytes accessed | tf_op | source)
XLA Modules:
  0.0 47.1 jit_solution(8218987105504525929)
XLA Ops:
  0.0 0.0 copy-start
  0.0 24.0 %shard_map.55 = bf16[10,16,1024]{2,1,0:T(8,128)(2,1)} custom-call(bf16[128,1024]{1,0:T(8,128)(2,1)} %bitcast.23, bf16[1024,1024]{1,0:T(8,128)(2,1)} %bitcast.17, f32[2,128]{1,0:T(2,128)} %bitcast.25), custom_call_target="tpu_custom_call" | custom-call | tf_op jit(solution)/shard_map/pallas_call | solution.py:132
  24.0 2.0 %copy.8 = bf16[10,2,8,2,2,2,128]{6,5,2,4,0,3,1:T(2,128)(2,1)} copy(bf16[10,2,8,2,2,2,128]{6,2,5,4,3,1,0:T(8,128)(2,1)} %bitcast.19) | data formatting | bytes 655360 | tf_op jit(solution)/shard_map/reshape | solution.py:337
  26.0 0.0 copy-done
  26.0 0.1 copy.9
  26.1 0.1 copy.13
  26.2 0.9 %copy.10.kernel_out_ref = bf16[1152,96]{1,0:T(8,128)(2,1)} copy(bf16[1152,96]{0,1:T(8,128)(2,1)S(1)} %bitcast.21) | data formatting | bytes 442368 | tf_op jit(solution)/shard_map/reshape | solution.py:343
  27.1 18.7 %shard_map.56 = bf16[8,4,256]{2,1,0:T(4,128)(2,1)} custom-call(bf16[4,20,16,128]{3,2,1,0:T(8,128)(2,1)} %bitcast.20, bf16[27,128,128]{2,1,0:T(8,128)(2,1)} %bitcast.22, f32[2,128]{1,0:T(2,128)} %bitcast.26, bf16[1152,96]{1,0:T(8,128)(2,1)} %copy.10.kernel_out_ref), custom_call_target="tpu_custom_call" | custom-call | tf_op jit(solution)/shard_map/pallas_call | solution.py:300
  45.8 1.3 %copy.15 = bf16[8,4,256]{2,1,0:T(4,128)(2,1)} copy(bf16[8,4,256]{2,1,0:T(4,128)(2,1)} %shard_map.56) | data formatting | bytes 32768
Async XLA Ops:
  0.0 26.0 %copy-start = (bf16[1,27,32,128]{3,2,1,0:T(8,128)(2,1)S(1)}, bf16[1,27,32,128]{3,2,1,0:T(8,128)(2,1)}, u32[]{:S(2)}) copy-start(bf16[1,27,32,128]{3,2,1,0:T(8,128)(2,1)} %param.9) | copy-start | bytes 663556

commit v12 on v11

--- a/solution.py
+++ b/solution.py
@@ -247,15 +247,16 @@
     ny_out = ny - 2
     cells_out = nx * ny_out * nz
     outch = kernel_out_ref.shape[1] // 3
-    columns = jnp.concatenate(
-        [
-            held_out[offset_x : offset_x + nx, offset_y : offset_y + ny_out].reshape(cells_out, channels)
-            for offset_x in range(3)
-            for offset_y in range(3)
-        ],
-        axis=1,
-    )
-    by_depth = jnp.dot(columns, kernel_out_ref[...], preferred_element_type=jnp.float32)
+    by_depth = jnp.zeros((cells_out, 3 * outch), jnp.float32)
+    for offset_x in range(3):
+        for offset_y in range(3):
+            window = held_out[offset_x : offset_x + nx, offset_y : offset_y + ny_out].reshape(cells_out, channels)
+            by_depth = by_depth + lax.dot_general(
+                window,
+                kernel_out_ref[offset_x * 3 + offset_y],
+                (((1,), (1,)), ((), ())),
+                preferred_element_type=jnp.float32,
+            )
     planes = nx * ny_out
     edge = jnp.zeros((planes, 1, outch), jnp.float32)
     shifted_out[:, 0:1] = edge
@@ -339,9 +340,7 @@
         .reshape(cell_x, 2 * lines, cell_z, channels)
     )
     taps, outch, channels_in = conv_out.shape[1:]
-    out_weight = (
-        conv_out[0].reshape(taps // 3, 3, outch, channels_in).transpose(0, 3, 1, 2).reshape(-1, 3 * outch)
-    )
+    out_weight = conv_out[0].reshape(taps // 3, 3 * outch, channels_in)
     return decoder_block(field, conv_in[0], gains, out_weight, 1)
 
 

time: 47.5 us -> 46.3 us (0.975)
  local copies, waits for them, and re-layouts: 4.36 us -> 3.28 us
    reshape x1 -> x0, local copies, waits for them, and re-layouts: 0.89 us -> none  [local(): conv_out[0].reshape(taps // 3, 3, outch, channels_in).transpose(0, 3, 1, 2)]
    unnamed x4 -> x1, local copies, waits for them, and re-layouts: 1.4 us -> 1.33 us
where the time goes in v12:
time: 46.3 us; the launch traced here: 46 us
  Pallas kernels  42.7 us (92%)
  local copies, waits for them, and re-layouts  3.28 us (7%)
    pallas_call x1, Pallas kernels, gather_bricks(): pl.pallas_call(gather_kernel, out_shape=jax.ShapeDtypeStruct(shape, jnp.b...  24 us
    pallas_call x1, Pallas kernels, decoder_block(): pl.pallas_call(block_kernel, out_shape=jax.ShapeDtypeStruct((block, nx, n...  18.7 us
    reshape x1, local copies, waits for them, and re-layouts, local(): brick.reshape(lines, PXD, GZ, 2, 2, 2, channels)  1.95 us
    unnamed x1, local copies, waits for them, and re-layouts  1.33 us

profile of v12, /device:TPU:3, one launch (start us, length us, event | category | flops | bytes accessed | tf_op | source)
XLA Modules:
  0.0 46.0 jit_solution(10487429632422954005)
XLA Ops:
  0.0 24.0 %shard_map.55 = bf16[10,16,1024]{2,1,0:T(8,128)(2,1)} custom-call(bf16[128,1024]{1,0:T(8,128)(2,1)} %bitcast.13, bf16[1024,1024]{1,0:T(8,128)(2,1)} %bitcast.9, f32[2,128]{1,0:T(2,128)} %bitcast.15), custom_call_target="tpu_custom_call" | custom-call | tf_op jit(solution)/shard_map/pallas_call | solution.py:132
  24.0 1.9 %copy.6 = bf16[10,2,8,2,2,2,128]{6,5,2,4,0,3,1:T(2,128)(2,1)} copy(bf16[10,2,8,2,2,2,128]{6,2,5,4,3,1,0:T(8,128)(2,1)} %bitcast.10) | data formatting | bytes 655360 | tf_op jit(solution)/shard_map/reshape | solution.py:338
  25.9 18.7 %shard_map.56 = bf16[8,4,256]{2,1,0:T(4,128)(2,1)} custom-call(bf16[4,20,16,128]{3,2,1,0:T(8,128)(2,1)} %bitcast.11, bf16[27,128,128]{2,1,0:T(8,128)(2,1)} %bitcast.12, f32[2,128]{1,0:T(2,128)} %bitcast.16, bf16[9,96,128]{2,1,0:T(8,128)(2,1)} %bitcast.14), custom_call_target="tpu_custom_call" | custom-call | tf_op jit(solution)/shard_map/pallas_call | solution.py:301
  44.6 1.3 %copy.8 = bf16[8,4,256]{2,1,0:T(4,128)(2,1)} copy(bf16[8,4,256]{2,1,0:T(4,128)(2,1)} %shard_map.56) | data formatting | bytes 32768

commit v13 on v12

--- a/solution.py
+++ b/solution.py
@@ -150,20 +150,24 @@
     )(tokens, weight, gains)
 
 
-def halo_x(field_ref, held, send_sem, recv_sem, others=0):
+def halo_signal():
+    count = lax.axis_size("inl")
+    me = lax.axis_index("inl")
+    for step in (-1, 1):
+
+        @pl.when((me + step >= 0) & (me + step < count))
+        def _():
+            pl.semaphore_signal(
+                pltpu.get_barrier_semaphore(), inc=1, device_id={"inl": me + step}, device_id_type=MESH
+            )
+
+    return (me > 0).astype(jnp.int32) + (me < count - 1).astype(jnp.int32)
+
+
+def halo_start(field_ref, held, send_sem, recv_sem):
     nx = field_ref.shape[0]
     count = lax.axis_size("inl")
     me = lax.axis_index("inl")
-    if others is not None:
-        barrier = pltpu.get_barrier_semaphore()
-        for step in (-1, 1):
-
-            @pl.when((me + step >= 0) & (me + step < count))
-            def _():
-                pl.semaphore_signal(barrier, inc=1, device_id={"inl": me + step}, device_id_type=MESH)
-
-        present = (me > 0).astype(jnp.int32) + (me < count - 1).astype(jnp.int32)
-        pl.semaphore_wait(barrier, present + others)
     copies = []
     for index, step in enumerate((-1, 1)):
         source, target = (0, nx + 1) if step < 0 else (nx - 1, 0)
@@ -187,7 +191,10 @@
             held[target : target + 1] = jnp.zeros((1,) + held.shape[1:], held.dtype)
 
         copies.append((copy, sends, gets))
-    held[1 : nx + 1] = field_ref[...]
+    return copies
+
+
+def halo_finish(copies):
     for copy, sends, gets in copies:
 
         @pl.when(gets)
@@ -206,57 +213,75 @@
 ):
     count = lax.axis_size("section")
     me = lax.axis_index("section")
+    barrier = pltpu.get_barrier_semaphore()
     for step in range(1, count):
         pl.semaphore_signal(
-            pltpu.get_barrier_semaphore(),
-            inc=1,
-            device_id={"section": lax.rem(me + step, count)},
-            device_id_type=MESH,
+            barrier, inc=1, device_id={"section": lax.rem(me + step, count)}, device_id_type=MESH
         )
-    halo_x(field_ref, held, send_sem, recv_sem, count - 1)
+    present = halo_signal()
     nx, ny_in, nz, channels = field_ref.shape
     ny = ny_in - 2
-    cells = nx * ny * nz
-    width = channels
-    parts_in = []
-    for offset_z in range(3):
-        part = jnp.zeros((cells, width), jnp.float32)
+    ny_out = ny - 2
+    outch = kernel_out_ref.shape[1] // 3
+    me_y, count_y = lax.axis_index("xln"), lax.axis_size("xln")
+    edge = jnp.zeros((nx * ny, 1, channels), jnp.float32)
+    shifted[:, 0:1] = edge
+    shifted[:, nz + 1 : nz + 2] = edge
+    held[1 : nx + 1] = field_ref[...]
+
+    def inner_rows(first, last):
+        rows = last - first
+        cells = rows * ny * nz
+        planes = rows * ny
+        parts_in = []
+        for offset_z in range(3):
+            part = jnp.zeros((cells, channels), jnp.float32)
+            for offset_x in range(3):
+                for offset_y in range(3):
+                    window = held[first + offset_x : last + offset_x, offset_y : offset_y + ny].reshape(cells, channels)
+                    tap = kernel_in_ref[(offset_x * 3 + offset_y) * 3 + offset_z]
+                    part = part + jnp.dot(window, tap, preferred_element_type=jnp.float32)
+            parts_in.append(part.reshape(planes, nz, channels))
+        shifted[0:planes, 1 : nz + 1] = parts_in[0]
+        total = parts_in[1] + shifted[0:planes, 0:nz]
+        shifted[0:planes, 1 : nz + 1] = parts_in[2]
+        total = total + shifted[0:planes, 2 : nz + 2]
+        mean_square = jnp.mean(total * total, axis=-1, keepdims=True)
+        normed = total * lax.rsqrt(mean_square + epsilon) * gains_ref[1:2, :]
+        base = field_ref[first:last, 1 : ny + 1].reshape(planes, nz, channels).astype(jnp.float32)
+        activated = gelu_tanh(normed + base).reshape(rows, ny, nz, channels)
+        row = lax.broadcasted_iota(jnp.int32, activated.shape, 1)
+        outside = ((row == 0) & (me_y == 0)) | ((row == ny - 1) & (me_y == count_y - 1))
+        mixed[first:last] = jnp.where(outside, 0.0, activated).astype(mixed.dtype)
+
+    def outer_rows(first, last):
+        cells = (last - first) * ny_out * nz
+        by_depth = jnp.zeros((cells, 3 * outch), jnp.float32)
         for offset_x in range(3):
             for offset_y in range(3):
-                window = held[offset_x : offset_x + nx, offset_y : offset_y + ny].reshape(cells, channels)
-                tap = kernel_in_ref[(offset_x * 3 + offset_y) * 3 + offset_z]
-                part = part + jnp.dot(window, tap, preferred_element_type=jnp.float32)
-        parts_in.append(part.reshape(nx * ny, nz, width))
-    edge = jnp.zeros((nx * ny, 1, width), jnp.float32)
-    shifted[:, 0:1] = edge
-    shifted[:, nz + 1 : nz + 2] = edge
-    shifted[:, 1 : nz + 1] = parts_in[0]
-    total = parts_in[1] + shifted[:, 0:nz]
-    shifted[:, 1 : nz + 1] = parts_in[2]
-    total = total + shifted[:, 2 : nz + 2]
-    mean_square = jnp.mean(total * total, axis=-1, keepdims=True)
-    normed = total * lax.rsqrt(mean_square + epsilon) * gains_ref[1:2, :]
-    base = field_ref[:, 1 : ny + 1].reshape(nx * ny, nz, channels).astype(jnp.float32)
-    activated = gelu_tanh(normed + base).reshape(nx, ny, nz, channels)
-    me_y, count_y = lax.axis_index("xln"), lax.axis_size("xln")
-    row = lax.broadcasted_iota(jnp.int32, activated.shape, 1)
-    outside = ((row == 0) & (me_y == 0)) | ((row == ny - 1) & (me_y == count_y - 1))
-    mixed[...] = jnp.where(outside, 0.0, activated).astype(mixed.dtype)
-
-    halo_x(mixed, held_out, send_out, recv_out, None)
-    ny_out = ny - 2
+                window = held_out[first + offset_x : last + offset_x, offset_y : offset_y + ny_out].reshape(
+                    cells, channels
+                )
+                by_depth = by_depth + lax.dot_general(
+                    window,
+                    kernel_out_ref[offset_x * 3 + offset_y],
+                    (((1,), (1,)), ((), ())),
+                    preferred_element_type=jnp.float32,
+                )
+        return by_depth
+
+    inner_rows(1, nx - 1)
+    pl.semaphore_wait(barrier, present + count - 1)
+    halo_finish(halo_start(field_ref, held, send_sem, recv_sem))
+    inner_rows(0, 1)
+    inner_rows(nx - 1, nx)
+
+    copies = halo_start(mixed, held_out, send_out, recv_out)
+    held_out[1 : nx + 1] = mixed[...]
+    middle = outer_rows(1, nx - 1)
+    halo_finish(copies)
+    by_depth = jnp.concatenate([outer_rows(0, 1), middle, outer_rows(nx - 1, nx)], axis=0)
     cells_out = nx * ny_out * nz
-    outch = kernel_out_ref.shape[1] // 3
-    by_depth = jnp.zeros((cells_out, 3 * outch), jnp.float32)
-    for offset_x in range(3):
-        for offset_y in range(3):
-            window = held_out[offset_x : offset_x + nx, offset_y : offset_y + ny_out].reshape(cells_out, channels)
-            by_depth = by_depth + lax.dot_general(
-                window,
-                kernel_out_ref[offset_x * 3 + offset_y],
-                (((1,), (1,)), ((), ())),
-                preferred_element_type=jnp.float32,
-            )
     planes = nx * ny_out
     edge = jnp.zeros((planes, 1, outch), jnp.float32)
     shifted_out[:, 0:1] = edge

time: 46.3 us -> 44.7 us (0.965)
  Pallas kernels: 42.7 us -> 41.2 us
    pallas_call x1, Pallas kernels: 18.7 us -> 17.2 us  [decoder_block(): pl.pallas_call(block_kernel, out_shape=jax.ShapeDtypeStruct((block, nx, n...]
where the time goes in v13:
time: 44.7 us; the launch traced here: 44.5 us
  Pallas kernels  41.2 us (92%)
  local copies, waits for them, and re-layouts  3.28 us (7%)
    pallas_call x1, Pallas kernels, gather_bricks(): pl.pallas_call(gather_kernel, out_shape=jax.ShapeDtypeStruct(shape, jnp.b...  24 us
    pallas_call x1, Pallas kernels, decoder_block(): pl.pallas_call(block_kernel, out_shape=jax.ShapeDtypeStruct((block, nx, n...  17.2 us
    reshape x1, local copies, waits for them, and re-layouts, local(): brick.reshape(lines, PXD, GZ, 2, 2, 2, channels)  1.95 us
    unnamed x1, local copies, waits for them, and re-layouts  1.33 us

profile of v13, /device:TPU:3, one launch (start us, length us, event | category | flops | bytes accessed | tf_op | source)
XLA Modules:
  0.0 44.5 jit_solution(1523686188662512177)
XLA Ops:
  0.0 24.0 %shard_map.55 = bf16[10,16,1024]{2,1,0:T(8,128)(2,1)} custom-call(bf16[128,1024]{1,0:T(8,128)(2,1)} %bitcast.13, bf16[1024,1024]{1,0:T(8,128)(2,1)} %bitcast.9, f32[2,128]{1,0:T(2,128)} %bitcast.15), custom_call_target="tpu_custom_call" | custom-call | tf_op jit(solution)/shard_map/pallas_call | solution.py:132
  24.0 1.9 %copy.6 = bf16[10,2,8,2,2,2,128]{6,5,2,4,0,3,1:T(2,128)(2,1)} copy(bf16[10,2,8,2,2,2,128]{6,2,5,4,3,1,0:T(8,128)(2,1)} %bitcast.10) | data formatting | bytes 655360 | tf_op jit(solution)/shard_map/reshape | solution.py:363
  25.9 17.2 %shard_map.56 = bf16[8,4,256]{2,1,0:T(4,128)(2,1)} custom-call(bf16[4,20,16,128]{3,2,1,0:T(8,128)(2,1)} %bitcast.11, bf16[27,128,128]{2,1,0:T(8,128)(2,1)} %bitcast.12, f32[2,128]{1,0:T(2,128)} %bitcast.16, bf16[9,96,128]{2,1,0:T(8,128)(2,1)} %bitcast.14), custom_call_target="tpu_custom_call" | custom-call | tf_op jit(solution)/shard_map/pallas_call | solution.py:326
  43.1 1.3 %copy.8 = bf16[8,4,256]{2,1,0:T(4,128)(2,1)} copy(bf16[8,4,256]{2,1,0:T(4,128)(2,1)} %shard_map.56) | data formatting | bytes 32768

commit v14 on v13

--- a/solution.py
+++ b/solution.py
@@ -276,43 +276,59 @@
     inner_rows(0, 1)
     inner_rows(nx - 1, nx)
 
+    edge = jnp.zeros((nx * ny_out, 1, outch), jnp.float32)
+    shifted_out[:, 0:1] = edge
+    shifted_out[:, nz + 1 : nz + 2] = edge
+
+    def by_channel(by_depth, rows):
+        planes = rows * ny_out
+        shifted_out[0:planes, 1 : nz + 1] = by_depth[:, 0:outch].reshape(planes, nz, outch)
+        summed = by_depth[:, outch : 2 * outch].reshape(planes, nz, outch) + shifted_out[0:planes, 0:nz]
+        shifted_out[0:planes, 1 : nz + 1] = by_depth[:, 2 * outch : 3 * outch].reshape(planes, nz, outch)
+        summed = summed + shifted_out[0:planes, 2 : nz + 2]
+        return summed.reshape(planes * nz, outch).T
+
+    block = outch // count
+
+    def share(phase, values):
+        for peer in range(count):
+            parts[phase, peer] = values[peer * block : (peer + 1) * block]
+        sends = []
+        for step in range(1, count):
+            peer = lax.rem(me + step, count)
+            copy = pltpu.make_async_remote_copy(
+                src_ref=parts.at[phase, peer],
+                dst_ref=inbox.at[phase, step],
+                send_sem=sum_send.at[phase, step],
+                recv_sem=sum_recv.at[phase, step],
+                device_id={"section": peer},
+                device_id_type=MESH,
+            )
+            copy.start()
+            sends.append(copy)
+        return sends
+
+    def gather(phase, sends):
+        result = parts[phase, me]
+        for step in range(1, count):
+            sends[step - 1].wait_recv()
+            result = result + inbox[phase, step]
+        for copy in sends:
+            copy.wait_send()
+        return result
+
     copies = halo_start(mixed, held_out, send_out, recv_out)
     held_out[1 : nx + 1] = mixed[...]
-    middle = outer_rows(1, nx - 1)
+    middle_sends = share(0, by_channel(outer_rows(1, nx - 1), nx - 2))
     halo_finish(copies)
-    by_depth = jnp.concatenate([outer_rows(0, 1), middle, outer_rows(nx - 1, nx)], axis=0)
-    cells_out = nx * ny_out * nz
-    planes = nx * ny_out
-    edge = jnp.zeros((planes, 1, outch), jnp.float32)
-    shifted_out[:, 0:1] = edge
-    shifted_out[:, nz + 1 : nz + 2] = edge
-    shifted_out[:, 1 : nz + 1] = by_depth[:, 0:outch].reshape(planes, nz, outch)
-    summed = by_depth[:, outch : 2 * outch].reshape(planes, nz, outch) + shifted_out[:, 0:nz]
-    shifted_out[:, 1 : nz + 1] = by_depth[:, 2 * outch : 3 * outch].reshape(planes, nz, outch)
-    summed = summed + shifted_out[:, 2 : nz + 2]
-    result_t = summed.reshape(cells_out, outch).T
-    block = outch // count
-    for peer in range(count):
-        parts[peer] = result_t[peer * block : (peer + 1) * block]
-    sends = []
-    for step in range(1, count):
-        peer = lax.rem(me + step, count)
-        copy = pltpu.make_async_remote_copy(
-            src_ref=parts.at[peer],
-            dst_ref=inbox.at[step],
-            send_sem=sum_send.at[step],
-            recv_sem=sum_recv.at[step],
-            device_id={"section": peer},
-            device_id_type=MESH,
-        )
-        copy.start()
-        sends.append(copy)
-    result = parts[me]
-    for step in range(1, count):
-        sends[step - 1].wait_recv()
-        result = result + inbox[step]
-    for copy in sends:
-        copy.wait_send()
+    row_cells = ny_out * nz
+    ends = jnp.concatenate(
+        [by_channel(outer_rows(0, 1), 1), by_channel(outer_rows(nx - 1, nx), 1)], axis=1
+    )
+    end_sends = share(1, ends)
+    middle = gather(0, middle_sends)
+    ends = gather(1, end_sends)
+    result = jnp.concatenate([ends[:, 0:row_cells], middle, ends[:, row_cells:]], axis=1)
     out_ref[...] = result.reshape(out_ref.shape).astype(out_ref.dtype)
 
 
@@ -334,14 +350,14 @@
             pltpu.VMEM((nx, ny, nz, channels), field.dtype),
             pltpu.VMEM((nx + 2, ny, nz, channels), field.dtype),
             pltpu.VMEM((nx * ny_out, nz + 2, outch), jnp.float32),
-            pltpu.VMEM((count, block, nx * ny_out * nz), jnp.float32),
-            pltpu.VMEM((count, block, nx * ny_out * nz), jnp.float32),
+            pltpu.VMEM((2, count, block, (nx - 2) * ny_out * nz), jnp.float32),
+            pltpu.VMEM((2, count, block, (nx - 2) * ny_out * nz), jnp.float32),
             pltpu.SemaphoreType.DMA((2,)),
             pltpu.SemaphoreType.DMA((2,)),
             pltpu.SemaphoreType.DMA((2,)),
             pltpu.SemaphoreType.DMA((2,)),
-            pltpu.SemaphoreType.DMA((count,)),
-            pltpu.SemaphoreType.DMA((count,)),
+            pltpu.SemaphoreType.DMA((2, count)),
+            pltpu.SemaphoreType.DMA((2, count)),
         ],
         compiler_params=pltpu.CompilerParams(collective_id=collective, has_side_effects=True),
     )(field, kernel_in, gains, kernel_out)

time: 44.7 us -> 44.6 us (level)
  no operation moved by 1% of the time
where the time goes in v14:
time: 44.6 us; the launch traced here: 44.3 us
  Pallas kernels  41 us (92%)
  local copies, waits for them, and re-layouts  3.28 us (7%)
    pallas_call x1, Pallas kernels, gather_bricks(): pl.pallas_call(gather_kernel, out_shape=jax.ShapeDtypeStruct(shape, jnp.b...  24 us
    pallas_call x1, Pallas kernels, decoder_block(): pl.pallas_call(block_kernel, out_shape=jax.ShapeDtypeStruct((block, nx, n...  17.1 us
    reshape x1, local copies, waits for them, and re-layouts, local(): brick.reshape(lines, PXD, GZ, 2, 2, 2, channels)  1.95 us
    unnamed x1, local copies, waits for them, and re-layouts  1.33 us

profile of v14, /device:TPU:3, one launch (start us, length us, event | category | flops | bytes accessed | tf_op | source)
XLA Modules:
  0.0 44.3 jit_solution(16616137011880736762)
XLA Ops:
  0.0 24.0 %shard_map.55 = bf16[10,16,1024]{2,1,0:T(8,128)(2,1)} custom-call(bf16[128,1024]{1,0:T(8,128)(2,1)} %bitcast.13, bf16[1024,1024]{1,0:T(8,128)(2,1)} %bitcast.9, f32[2,128]{1,0:T(2,128)} %bitcast.15), custom_call_target="tpu_custom_call" | custom-call | tf_op jit(solution)/shard_map/pallas_call | solution.py:132
  24.0 1.9 %copy.6 = bf16[10,2,8,2,2,2,128]{6,5,2,4,0,3,1:T(2,128)(2,1)} copy(bf16[10,2,8,2,2,2,128]{6,2,5,4,3,1,0:T(8,128)(2,1)} %bitcast.10) | data formatting | bytes 655360 | tf_op jit(solution)/shard_map/reshape | solution.py:379
  25.9 17.1 %shard_map.56 = bf16[8,4,256]{2,1,0:T(4,128)(2,1)} custom-call(bf16[4,20,16,128]{3,2,1,0:T(8,128)(2,1)} %bitcast.11, bf16[27,128,128]{2,1,0:T(8,128)(2,1)} %bitcast.12, f32[2,128]{1,0:T(2,128)} %bitcast.16, bf16[9,96,128]{2,1,0:T(8,128)(2,1)} %bitcast.14), custom_call_target="tpu_custom_call" | custom-call | tf_op jit(solution)/shard_map/pallas_call | solution.py:342
  43.0 1.3 %copy.8 = bf16[8,4,256]{2,1,0:T(4,128)(2,1)} copy(bf16[8,4,256]{2,1,0:T(4,128)(2,1)} %shard_map.56) | data formatting | bytes 32768

commit v15 on v14

--- a/solution.py
+++ b/solution.py
@@ -71,6 +71,26 @@
         mean_square = jnp.mean(part * part, axis=-1, keepdims=True)
         normed = part * lax.rsqrt(mean_square + epsilon) * gains_ref[0:1, :]
         field[:, group * width : (group + 1) * width] = gelu_tanh(normed).astype(field.dtype)
+    depth = 2 * (rows // 2)
+    target = lax.broadcasted_iota(jnp.int32, (2 * rows, 2 * rows), 0)
+    origin = lax.broadcasted_iota(jnp.int32, (2 * rows, 2 * rows), 1)
+    half = rows // 2
+    same = (
+        (target // depth == (origin % rows) // half)
+        & ((target % depth) // 2 == origin % half)
+        & (target % 2 == origin // rows)
+    )
+    interleave = jnp.where(same, 1.0, 0.0).astype(jnp.bfloat16)
+
+    def place(slot, block):
+        for u in range(2):
+            for v in range(2):
+                first = ((u * 2 + v) * 2) * width
+                pair = jnp.concatenate([block[:, first : first + width], block[:, first + width : first + 2 * width]], axis=0)
+                cells = jnp.dot(interleave, pair, preferred_element_type=jnp.float32).astype(out_ref.dtype)
+                for ix in range(2):
+                    out_ref[2 * ix + u, 2 * slot + v] = cells[ix * depth : (ix + 1) * depth]
+
     pl.semaphore_wait(barrier, expected)
     copies = []
     for index, (column, slot, exists) in enumerate(groups):
@@ -108,15 +128,17 @@
         @pl.when(remote)
         def _():
             incoming.wait_recv()
-            out_ref[slot] = held[slot]
+            place(slot, held[slot])
 
         @pl.when(mine)
         def _():
-            out_ref[slot] = field[pl.ds(pl.multiple_of(me_x * rows, rows), rows)]
+            place(slot, field[pl.ds(pl.multiple_of(me_x * rows, rows), rows)])
 
         @pl.when(jnp.logical_not(live))
         def _():
-            out_ref[slot] = jnp.zeros(out_ref.shape[1:], out_ref.dtype)
+            out_ref[:, 2 * slot : 2 * slot + 2] = jnp.zeros(
+                (out_ref.shape[0], 2) + out_ref.shape[2:], out_ref.dtype
+            )
 
     for copy, remote in copies:
 
@@ -129,9 +151,10 @@
     count = lax.axis_size("inl")
     rows = tokens.shape[0] // count
     shape = (lax.axis_size("xln") + 2, rows, weight.shape[1])
+    brick = (2 * PXD, 2 * shape[0], 2 * GZ, gains.shape[1])
     return pl.pallas_call(
         gather_kernel,
-        out_shape=jax.ShapeDtypeStruct(shape, jnp.bfloat16),
+        out_shape=jax.ShapeDtypeStruct(brick, jnp.bfloat16),
         in_specs=[
             pl.BlockSpec(memory_space=pltpu.VMEM),
             pl.BlockSpec(memory_space=pl.ANY),
@@ -373,13 +396,7 @@
     cell_y = 2 * lax.axis_size("xln")
     cell_z = 2 * GZ
     assert tokens_here.shape[0] == inl_size * PXD * GZ
-    brick = gather_bricks(tokens_here, weight, gains)
-    lines = brick.shape[0]
-    field = (
-        brick.reshape(lines, PXD, GZ, 2, 2, 2, channels)
-        .transpose(1, 3, 0, 4, 2, 5, 6)
-        .reshape(cell_x, 2 * lines, cell_z, channels)
-    )
+    field = gather_bricks(tokens_here, weight, gains)
     taps, outch, channels_in = conv_out.shape[1:]
     out_weight = conv_out[0].reshape(taps // 3, 3 * outch, channels_in)
     return decoder_block(field, conv_in[0], gains, out_weight, 1)

time: 44.6 us -> 42.8 us (0.960)
  local copies, waits for them, and re-layouts: 3.28 us -> 1.33 us
    reshape x1 -> x0, local copies, waits for them, and re-layouts: 1.95 us -> none  [local(): brick.reshape(lines, PXD, GZ, 2, 2, 2, channels)]
where the time goes in v15:
time: 42.8 us; the launch traced here: 42.6 us
  Pallas kernels  41.3 us (96%)
  local copies, waits for them, and re-layouts  1.33 us (3%)
    pallas_call x1, Pallas kernels, gather_bricks(): pl.pallas_call(gather_kernel, out_shape=jax.ShapeDtypeStruct(brick, jnp.b...  24.1 us
    pallas_call x1, Pallas kernels, decoder_block(): pl.pallas_call(block_kernel, out_shape=jax.ShapeDtypeStruct((block, nx, n...  17.2 us
    unnamed x1, local copies, waits for them, and re-layouts  1.33 us

profile of v15, /device:TPU:3, one launch (start us, length us, event | category | flops | bytes accessed | tf_op | source)
XLA Modules:
  0.0 42.6 jit_solution(11438204979406116940)
XLA Ops:
  0.0 24.1 %shard_map.55.field_ref = bf16[4,20,16,128]{3,2,1,0:T(8,128)(2,1)} custom-call(bf16[128,1024]{1,0:T(8,128)(2,1)} %bitcast.7, bf16[1024,1024]{1,0:T(8,128)(2,1)} %bitcast.5, f32[2,128]{1,0:T(2,128)} %bitcast.9), custom_call_target="tpu_custom_call" | custom-call | tf_op jit(solution)/shard_map/pallas_call | solution.py:155
  24.1 17.2 %shard_map.56 = bf16[8,4,256]{2,1,0:T(4,128)(2,1)} custom-call(bf16[4,20,16,128]{3,2,1,0:T(8,128)(2,1)} %shard_map.55.field_ref, bf16[27,128,128]{2,1,0:T(8,128)(2,1)} %bitcast.6, f32[2,128]{1,0:T(2,128)} %bitcast.10, bf16[9,96,128]{2,1,0:T(8,128)(2,1)} %bitcast.8), custom_call_target="tpu_custom_call" | custom-call | tf_op jit(solution)/shard_map/pallas_call | solution.py:365
  41.3 1.3 %copy.7 = bf16[8,4,256]{2,1,0:T(4,128)(2,1)} copy(bf16[8,4,256]{2,1,0:T(4,128)(2,1)} %shard_map.56) | data formatting | bytes 32768

commit v16 on v15

--- a/solution.py
+++ b/solution.py
@@ -252,19 +252,23 @@
     shifted[:, nz + 1 : nz + 2] = edge
     held[1 : nx + 1] = field_ref[...]
 
-    def inner_rows(first, last):
-        rows = last - first
-        cells = rows * ny * nz
-        planes = rows * ny
+    def inner_taps(first, last, offsets_x):
+        cells = (last - first) * ny * nz
         parts_in = []
         for offset_z in range(3):
             part = jnp.zeros((cells, channels), jnp.float32)
-            for offset_x in range(3):
+            for offset_x in offsets_x:
                 for offset_y in range(3):
                     window = held[first + offset_x : last + offset_x, offset_y : offset_y + ny].reshape(cells, channels)
                     tap = kernel_in_ref[(offset_x * 3 + offset_y) * 3 + offset_z]
                     part = part + jnp.dot(window, tap, preferred_element_type=jnp.float32)
-            parts_in.append(part.reshape(planes, nz, channels))
+            parts_in.append(part)
+        return parts_in
+
+    def inner_rows(first, last, parts_in):
+        rows = last - first
+        planes = rows * ny
+        parts_in = [part.reshape(planes, nz, channels) for part in parts_in]
         shifted[0:planes, 1 : nz + 1] = parts_in[0]
         total = parts_in[1] + shifted[0:planes, 0:nz]
         shifted[0:planes, 1 : nz + 1] = parts_in[2]
@@ -293,11 +297,13 @@
                 )
         return by_depth
 
-    inner_rows(1, nx - 1)
+    inner_rows(1, nx - 1, inner_taps(1, nx - 1, (0, 1, 2)))
+    low = inner_taps(0, 1, (1, 2))
+    high = inner_taps(nx - 1, nx, (0, 1))
     pl.semaphore_wait(barrier, present + count - 1)
     halo_finish(halo_start(field_ref, held, send_sem, recv_sem))
-    inner_rows(0, 1)
-    inner_rows(nx - 1, nx)
+    inner_rows(0, 1, [a + b for a, b in zip(low, inner_taps(0, 1, (0,)))])
+    inner_rows(nx - 1, nx, [a + b for a, b in zip(high, inner_taps(nx - 1, nx, (2,)))])
 
     edge = jnp.zeros((nx * ny_out, 1, outch), jnp.float32)
     shifted_out[:, 0:1] = edge

time: 42.8 us -> 42 us (0.981)
  Pallas kernels: 41.3 us -> 40.5 us
    pallas_call x1, Pallas kernels: 17.2 us -> 16.4 us  [decoder_block(): pl.pallas_call(block_kernel, out_shape=jax.ShapeDtypeStruct((block, nx, n...]
where the time goes in v16:
time: 42 us; the launch traced here: 41.8 us
  Pallas kernels  40.5 us (96%)
  local copies, waits for them, and re-layouts  1.33 us (3%)
    pallas_call x1, Pallas kernels, gather_bricks(): pl.pallas_call(gather_kernel, out_shape=jax.ShapeDtypeStruct(brick, jnp.b...  24.1 us
    pallas_call x1, Pallas kernels, decoder_block(): pl.pallas_call(block_kernel, out_shape=jax.ShapeDtypeStruct((block, nx, n...  16.4 us
    unnamed x1, local copies, waits for them, and re-layouts  1.33 us

profile of v16, /device:TPU:3, one launch (start us, length us, event | category | flops | bytes accessed | tf_op | source)
XLA Modules:
  0.0 41.8 jit_solution(12197973408490479910)
XLA Ops:
  0.0 24.1 %shard_map.55.field_ref = bf16[4,20,16,128]{3,2,1,0:T(8,128)(2,1)} custom-call(bf16[128,1024]{1,0:T(8,128)(2,1)} %bitcast.7, bf16[1024,1024]{1,0:T(8,128)(2,1)} %bitcast.5, f32[2,128]{1,0:T(2,128)} %bitcast.9), custom_call_target="tpu_custom_call" | custom-call | tf_op jit(solution)/shard_map/pallas_call | solution.py:155
  24.1 16.4 %shard_map.56 = bf16[8,4,256]{2,1,0:T(4,128)(2,1)} custom-call(bf16[4,20,16,128]{3,2,1,0:T(8,128)(2,1)} %shard_map.55.field_ref, bf16[27,128,128]{2,1,0:T(8,128)(2,1)} %bitcast.6, f32[2,128]{1,0:T(2,128)} %bitcast.10, bf16[9,96,128]{2,1,0:T(8,128)(2,1)} %bitcast.8), custom_call_target="tpu_custom_call" | custom-call | tf_op jit(solution)/shard_map/pallas_call | solution.py:371
  40.5 1.3 %copy.7 = bf16[8,4,256]{2,1,0:T(4,128)(2,1)} copy(bf16[8,4,256]{2,1,0:T(4,128)(2,1)} %shard_map.56) | data formatting | bytes 32768

commit v17 on v16

--- a/solution.py
+++ b/solution.py
@@ -27,7 +27,9 @@
     ]
 
 
-def gather_kernel(tokens_ref, weight_hbm, gains_ref, out_ref, weight, field, held, send_sem, recv_sem, weight_sem):
+def gather_kernel(
+    tokens_ref, weight_hbm, gains_ref, out_ref, weight, field, held, send_sem, recv_sem, weight_sem, extra=0
+):
     count = lax.axis_size("inl")
     me_x, me_y = lax.axis_index("inl"), lax.axis_index("xln")
     rows = tokens_ref.shape[0] // count
@@ -91,7 +93,7 @@
                 for ix in range(2):
                     out_ref[2 * ix + u, 2 * slot + v] = cells[ix * depth : (ix + 1) * depth]
 
-    pl.semaphore_wait(barrier, expected)
+    pl.semaphore_wait(barrier, expected + extra)
     copies = []
     for index, (column, slot, exists) in enumerate(groups):
         live = True if exists is None else exists
@@ -145,32 +147,6 @@
         @pl.when(remote)
         def _():
             copy.wait_send()
-
-
-def gather_bricks(tokens, weight, gains):
-    count = lax.axis_size("inl")
-    rows = tokens.shape[0] // count
-    shape = (lax.axis_size("xln") + 2, rows, weight.shape[1])
-    brick = (2 * PXD, 2 * shape[0], 2 * GZ, gains.shape[1])
-    return pl.pallas_call(
-        gather_kernel,
-        out_shape=jax.ShapeDtypeStruct(brick, jnp.bfloat16),
-        in_specs=[
-            pl.BlockSpec(memory_space=pltpu.VMEM),
-            pl.BlockSpec(memory_space=pl.ANY),
-            pl.BlockSpec(memory_space=pltpu.VMEM),
-        ],
-        out_specs=pl.BlockSpec(memory_space=pltpu.VMEM),
-        scratch_shapes=[
-            pltpu.VMEM(weight.shape, weight.dtype),
-            pltpu.VMEM((tokens.shape[0], weight.shape[1]), jnp.bfloat16),
-            pltpu.VMEM(shape, jnp.bfloat16),
-            pltpu.SemaphoreType.DMA((3 * count,)),
-            pltpu.SemaphoreType.DMA((shape[0],)),
-            pltpu.SemaphoreType.DMA(()),
-        ],
-        compiler_params=pltpu.CompilerParams(collective_id=3, has_side_effects=True),
-    )(tokens, weight, gains)
 
 
 def halo_signal():
@@ -229,19 +205,29 @@
             copy.wait_send()
 
 
+def entry_signals():
+    count = lax.axis_size("section")
+    me = lax.axis_index("section")
+    for step in range(1, count):
+        pl.semaphore_signal(
+            pltpu.get_barrier_semaphore(),
+            inc=1,
+            device_id={"section": lax.rem(me + step, count)},
+            device_id_type=MESH,
+        )
+    return halo_signal() + count - 1
+
+
 def block_kernel(
-    field_ref, kernel_in_ref, gains_ref, kernel_out_ref, out_ref,
+    merged, field_ref, kernel_in_ref, gains_ref, kernel_out_ref, out_ref,
     held, shifted, mixed, held_out, shifted_out, parts, inbox,
     send_sem, recv_sem, send_out, recv_out, sum_send, sum_recv,
 ):
     count = lax.axis_size("section")
     me = lax.axis_index("section")
     barrier = pltpu.get_barrier_semaphore()
-    for step in range(1, count):
-        pl.semaphore_signal(
-            barrier, inc=1, device_id={"section": lax.rem(me + step, count)}, device_id_type=MESH
-        )
-    present = halo_signal()
+    if not merged:
+        expected = entry_signals()
     nx, ny_in, nz, channels = field_ref.shape
     ny = ny_in - 2
     ny_out = ny - 2
@@ -300,7 +286,8 @@
     inner_rows(1, nx - 1, inner_taps(1, nx - 1, (0, 1, 2)))
     low = inner_taps(0, 1, (1, 2))
     high = inner_taps(nx - 1, nx, (0, 1))
-    pl.semaphore_wait(barrier, present + count - 1)
+    if not merged:
+        pl.semaphore_wait(barrier, expected)
     halo_finish(halo_start(field_ref, held, send_sem, recv_sem))
     inner_rows(0, 1, [a + b for a, b in zip(low, inner_taps(0, 1, (0,)))])
     inner_rows(nx - 1, nx, [a + b for a, b in zip(high, inner_taps(nx - 1, nx, (2,)))])
@@ -361,23 +348,60 @@
     out_ref[...] = result.reshape(out_ref.shape).astype(out_ref.dtype)
 
 
-def decoder_block(field, kernel_in, gains, kernel_out, collective):
-    nx, ny_in, nz, channels = field.shape
+def whole_kernel(tokens_ref, weight_hbm, gains_ref, kernel_in_hbm, kernel_out_hbm, out_ref, *scratch):
+    weight, field, rows_in, send_rows, recv_rows, weight_sem = scratch[:6]
+    brick, kernel_in, kernel_out, kernel_sem = scratch[6:10]
+    loads = [
+        pltpu.make_async_copy(kernel_in_hbm, kernel_in, kernel_sem.at[0]),
+        pltpu.make_async_copy(kernel_out_hbm, kernel_out, kernel_sem.at[1]),
+    ]
+    for load in loads:
+        load.start()
+    extra = entry_signals()
+    gather_kernel(
+        tokens_ref, weight_hbm, gains_ref, brick, weight, field, rows_in, send_rows, recv_rows, weight_sem, extra
+    )
+    for load in loads:
+        load.wait()
+    block_kernel(True, brick, kernel_in, gains_ref, kernel_out, out_ref, *scratch[10:])
+
+
+def decoder_block(tokens, weight, gains, kernel_in, kernel_out, collective):
+    count_x = lax.axis_size("inl")
+    rows = tokens.shape[0] // count_x
+    slots = lax.axis_size("xln") + 2
+    nx, ny_in, nz, channels = 2 * PXD, 2 * slots, 2 * GZ, gains.shape[1]
     ny = ny_in - 2
     ny_out = ny - 2
     count = lax.axis_size("section")
     outch = kernel_out.shape[1] // 3
     block = outch // count
     return pl.pallas_call(
-        block_kernel,
+        whole_kernel,
         out_shape=jax.ShapeDtypeStruct((block, nx, ny_out * nz), jnp.bfloat16),
-        in_specs=[pl.BlockSpec(memory_space=pltpu.VMEM)] * 4,
+        in_specs=[
+            pl.BlockSpec(memory_space=pltpu.VMEM),
+            pl.BlockSpec(memory_space=pl.ANY),
+            pl.BlockSpec(memory_space=pltpu.VMEM),
+            pl.BlockSpec(memory_space=pl.ANY),
+            pl.BlockSpec(memory_space=pl.ANY),
+        ],
         out_specs=pl.BlockSpec(memory_space=pltpu.VMEM),
         scratch_shapes=[
-            pltpu.VMEM((nx + 2, ny_in, nz, channels), field.dtype),
+            pltpu.VMEM(weight.shape, weight.dtype),
+            pltpu.VMEM((tokens.shape[0], weight.shape[1]), jnp.bfloat16),
+            pltpu.VMEM((slots, rows, weight.shape[1]), jnp.bfloat16),
+            pltpu.SemaphoreType.DMA((3 * count_x,)),
+            pltpu.SemaphoreType.DMA((slots,)),
+            pltpu.SemaphoreType.DMA(()),
+            pltpu.VMEM((nx, ny_in, nz, channels), jnp.bfloat16),
+            pltpu.VMEM(kernel_in.shape, kernel_in.dtype),
+            pltpu.VMEM(kernel_out.shape, kernel_out.dtype),
+            pltpu.SemaphoreType.DMA((2,)),
+            pltpu.VMEM((nx + 2, ny_in, nz, channels), jnp.bfloat16),
             pltpu.VMEM((nx * ny, nz + 2, channels), jnp.float32),
-            pltpu.VMEM((nx, ny, nz, channels), field.dtype),
-            pltpu.VMEM((nx + 2, ny, nz, channels), field.dtype),
+            pltpu.VMEM((nx, ny, nz, channels), jnp.bfloat16),
+            pltpu.VMEM((nx + 2, ny, nz, channels), jnp.bfloat16),
             pltpu.VMEM((nx * ny_out, nz + 2, outch), jnp.float32),
             pltpu.VMEM((2, count, block, (nx - 2) * ny_out * nz), jnp.float32),
             pltpu.VMEM((2, count, block, (nx - 2) * ny_out * nz), jnp.float32),
@@ -389,7 +413,7 @@
             pltpu.SemaphoreType.DMA((2, count)),
         ],
         compiler_params=pltpu.CompilerParams(collective_id=collective, has_side_effects=True),
-    )(field, kernel_in, gains, kernel_out)
+    )(tokens, weight, gains, kernel_in, kernel_out)
 
 
 def local(skips, deconv_weight, norm_gain, conv_in, conv_out):
@@ -402,10 +426,9 @@
     cell_y = 2 * lax.axis_size("xln")
     cell_z = 2 * GZ
     assert tokens_here.shape[0] == inl_size * PXD * GZ
-    field = gather_bricks(tokens_here, weight, gains)
     taps, outch, channels_in = conv_out.shape[1:]
     out_weight = conv_out[0].reshape(taps // 3, 3 * outch, channels_in)
-    return decoder_block(field, conv_in[0], gains, out_weight, 1)
+    return decoder_block(tokens_here, weight, gains, conv_in[0], out_weight, 3)
 
 
 def solution(mesh):

time: 42 us -> 39.8 us (0.948)
  Pallas kernels: 40.5 us -> 38.3 us
    pallas_call x2 -> x1, Pallas kernels: 40.5 us -> 38.3 us  [decoder_block(): pl.pallas_call(whole_kernel, out_shape=jax.ShapeDtypeStruct((block, nx, n...]
where the time goes in v17:
time: 39.8 us; the launch traced here: 39.6 us
  Pallas kernels  38.3 us (96%)
  local copies, waits for them, and re-layouts  1.33 us (3%)
    pallas_call x1, Pallas kernels, decoder_block(): pl.pallas_call(whole_kernel, out_shape=jax.ShapeDtypeStruct((block, nx, n...  38.3 us
    unnamed x1, local copies, waits for them, and re-layouts  1.33 us

profile of v17, /device:TPU:3, one launch (start us, length us, event | category | flops | bytes accessed | tf_op | source)
XLA Modules:
  0.0 39.6 jit_solution(1631679950970607619)
XLA Ops:
  0.0 38.3 %shard_map.55 = bf16[8,4,256]{2,1,0:T(4,128)(2,1)} custom-call(bf16[128,1024]{1,0:T(8,128)(2,1)} %bitcast.7, bf16[1024,1024]{1,0:T(8,128)(2,1)} %bitcast.5, f32[2,128]{1,0:T(2,128)} %bitcast.9, bf16[27,128,128]{2,1,0:T(8,128)(2,1)} %bitcast.6, bf16[9,96,128]{2,1,0:T(8,128)(2,1)} %bitcast.8), custom_call_target="tpu_custom_call" | custom-call | tf_op jit(solution)/shard_map/pallas_call | solution.py:379
  38.3 1.3 %copy.7 = bf16[8,4,256]{2,1,0:T(4,128)(2,1)} copy(bf16[8,4,256]{2,1,0:T(4,128)(2,1)} %shard_map.55) | data formatting | bytes 32768

commit v18 on v17

--- a/solution.py
+++ b/solution.py
@@ -28,7 +28,8 @@
 
 
 def gather_kernel(
-    tokens_ref, weight_hbm, gains_ref, out_ref, weight, field, held, send_sem, recv_sem, weight_sem, extra=0
+    tokens_ref, weight_hbm, gains_ref, out_ref, weight, field, held, send_sem, recv_sem, weight_sem, extra=0,
+    hooks=None,
 ):
     count = lax.axis_size("inl")
     me_x, me_y = lax.axis_index("inl"), lax.axis_index("xln")
@@ -142,6 +143,9 @@
                 (out_ref.shape[0], 2) + out_ref.shape[2:], out_ref.dtype
             )
 
+        if hooks and slot in hooks:
+            hooks[slot]()
+
     for copy, remote in copies:
 
         @pl.when(remote)
@@ -205,6 +209,45 @@
             copy.wait_send()
 
 
+def conv_in_rows(field_ref, kernel_in_ref, gains_ref, held, shifted, mixed):
+    nx, ny_in, nz, channels = field_ref.shape
+    ny = ny_in - 2
+    me_y, count_y = lax.axis_index("xln"), lax.axis_size("xln")
+
+    def inner_taps(first, last, offsets_x, low=0, high=ny):
+        cells = (last - first) * (high - low) * nz
+        parts_in = []
+        for offset_z in range(3):
+            part = jnp.zeros((cells, channels), jnp.float32)
+            for offset_x in offsets_x:
+                for offset_y in range(3):
+                    window = held[first + offset_x : last + offset_x, low + offset_y : high + offset_y].reshape(
+                        cells, channels
+                    )
+                    tap = kernel_in_ref[(offset_x * 3 + offset_y) * 3 + offset_z]
+                    part = part + jnp.dot(window, tap, preferred_element_type=jnp.float32)
+            parts_in.append(part)
+        return parts_in
+
+    def inner_rows(first, last, parts_in, low=0, high=ny):
+        rows = last - first
+        planes = rows * (high - low)
+        parts_in = [part.reshape(planes, nz, channels) for part in parts_in]
+        shifted[0:planes, 1 : nz + 1] = parts_in[0]
+        total = parts_in[1] + shifted[0:planes, 0:nz]
+        shifted[0:planes, 1 : nz + 1] = parts_in[2]
+        total = total + shifted[0:planes, 2 : nz + 2]
+        mean_square = jnp.mean(total * total, axis=-1, keepdims=True)
+        normed = total * lax.rsqrt(mean_square + epsilon) * gains_ref[1:2, :]
+        base = field_ref[first:last, 1 + low : 1 + high].reshape(planes, nz, channels).astype(jnp.float32)
+        activated = gelu_tanh(normed + base).reshape(rows, high - low, nz, channels)
+        row = low + lax.broadcasted_iota(jnp.int32, activated.shape, 1)
+        outside = ((row == 0) & (me_y == 0)) | ((row == ny - 1) & (me_y == count_y - 1))
+        mixed[first:last, low:high] = jnp.where(outside, 0.0, activated).astype(mixed.dtype)
+
+    return inner_taps, inner_rows
+
+
 def entry_signals():
     count = lax.axis_size("section")
     me = lax.axis_index("section")
@@ -219,7 +262,7 @@
 
 
 def block_kernel(
-    merged, field_ref, kernel_in_ref, gains_ref, kernel_out_ref, out_ref,
+    merged, done, field_ref, kernel_in_ref, gains_ref, kernel_out_ref, out_ref,
     held, shifted, mixed, held_out, shifted_out, parts, inbox,
     send_sem, recv_sem, send_out, recv_out, sum_send, sum_recv,
 ):
@@ -233,39 +276,15 @@
     ny_out = ny - 2
     outch = kernel_out_ref.shape[1] // 3
     me_y, count_y = lax.axis_index("xln"), lax.axis_size("xln")
-    edge = jnp.zeros((nx * ny, 1, channels), jnp.float32)
-    shifted[:, 0:1] = edge
-    shifted[:, nz + 1 : nz + 2] = edge
-    held[1 : nx + 1] = field_ref[...]
-
-    def inner_taps(first, last, offsets_x):
-        cells = (last - first) * ny * nz
-        parts_in = []
-        for offset_z in range(3):
-            part = jnp.zeros((cells, channels), jnp.float32)
-            for offset_x in offsets_x:
-                for offset_y in range(3):
-                    window = held[first + offset_x : last + offset_x, offset_y : offset_y + ny].reshape(cells, channels)
-                    tap = kernel_in_ref[(offset_x * 3 + offset_y) * 3 + offset_z]
-                    part = part + jnp.dot(window, tap, preferred_element_type=jnp.float32)
-            parts_in.append(part)
-        return parts_in
-
-    def inner_rows(first, last, parts_in):
-        rows = last - first
-        planes = rows * ny
-        parts_in = [part.reshape(planes, nz, channels) for part in parts_in]
-        shifted[0:planes, 1 : nz + 1] = parts_in[0]
-        total = parts_in[1] + shifted[0:planes, 0:nz]
-        shifted[0:planes, 1 : nz + 1] = parts_in[2]
-        total = total + shifted[0:planes, 2 : nz + 2]
-        mean_square = jnp.mean(total * total, axis=-1, keepdims=True)
-        normed = total * lax.rsqrt(mean_square + epsilon) * gains_ref[1:2, :]
-        base = field_ref[first:last, 1 : ny + 1].reshape(planes, nz, channels).astype(jnp.float32)
-        activated = gelu_tanh(normed + base).reshape(rows, ny, nz, channels)
-        row = lax.broadcasted_iota(jnp.int32, activated.shape, 1)
-        outside = ((row == 0) & (me_y == 0)) | ((row == ny - 1) & (me_y == count_y - 1))
-        mixed[first:last] = jnp.where(outside, 0.0, activated).astype(mixed.dtype)
+    if not done:
+        edge = jnp.zeros((nx * ny, 1, channels), jnp.float32)
+        shifted[:, 0:1] = edge
+        shifted[:, nz + 1 : nz + 2] = edge
+        held[1 : nx + 1] = field_ref[...]
+    else:
+        held[1 : nx + 1, done + 2 :] = field_ref[:, done + 2 :]
+
+    inner_taps, inner_rows = conv_in_rows(field_ref, kernel_in_ref, gains_ref, held, shifted, mixed)
 
     def outer_rows(first, last):
         cells = (last - first) * ny_out * nz
@@ -283,7 +302,7 @@
                 )
         return by_depth
 
-    inner_rows(1, nx - 1, inner_taps(1, nx - 1, (0, 1, 2)))
+    inner_rows(1, nx - 1, inner_taps(1, nx - 1, (0, 1, 2), done, ny), done, ny)
     low = inner_taps(0, 1, (1, 2))
     high = inner_taps(nx - 1, nx, (0, 1))
     if not merged:
@@ -358,12 +377,25 @@
     for load in loads:
         load.start()
     extra = entry_signals()
+    held, shifted, mixed = scratch[10:13]
+    nx, ny_in, nz, channels = brick.shape
+    done = ny_in // 2
+    inner_taps, inner_rows = conv_in_rows(brick, kernel_in, gains_ref, held, shifted, mixed)
+
+    def early():
+        loads[0].wait()
+        edge = jnp.zeros((shifted.shape[0], 1, channels), jnp.float32)
+        shifted[:, 0:1] = edge
+        shifted[:, nz + 1 : nz + 2] = edge
+        held[1 : nx + 1, 0 : done + 2] = brick[:, 0 : done + 2]
+        inner_rows(1, nx - 1, inner_taps(1, nx - 1, (0, 1, 2), 0, done), 0, done)
+
     gather_kernel(
-        tokens_ref, weight_hbm, gains_ref, brick, weight, field, rows_in, send_rows, recv_rows, weight_sem, extra
+        tokens_ref, weight_hbm, gains_ref, brick, weight, field, rows_in, send_rows, recv_rows, weight_sem, extra,
+        {done // 2: early},
     )
-    for load in loads:
-        load.wait()
-    block_kernel(True, brick, kernel_in, gains_ref, kernel_out, out_ref, *scratch[10:])
+    loads[1].wait()
+    block_kernel(True, done, brick, kernel_in, gains_ref, kernel_out, out_ref, *scratch[10:])
 
 
 def decoder_block(tokens, weight, gains, kernel_in, kernel_out, collective):

time: 39.8 us -> 39.4 us (0.990); the launches traced: 39.6 us -> 38.7 us
  Pallas kernels: 38.3 us -> 37.4 us
    pallas_call x1, Pallas kernels: 38.3 us -> 37.4 us  [decoder_block(): pl.pallas_call(whole_kernel, out_shape=jax.ShapeDtypeStruct((block, nx, n...]
where the time goes in v18:
time: 39.4 us; the launch traced here: 38.7 us
  Pallas kernels  37.4 us (95%)
  local copies, waits for them, and re-layouts  1.33 us (3%)
    pallas_call x1, Pallas kernels, decoder_block(): pl.pallas_call(whole_kernel, out_shape=jax.ShapeDtypeStruct((block, nx, n...  37.4 us
    unnamed x1, local copies, waits for them, and re-layouts  1.33 us

profile of v18, /device:TPU:3, one launch (start us, length us, event | category | flops | bytes accessed | tf_op | source)
XLA Modules:
  0.0 38.7 jit_solution(6413538908101029869)
XLA Ops:
  0.0 37.4 %shard_map.55 = bf16[8,4,256]{2,1,0:T(4,128)(2,1)} custom-call(bf16[128,1024]{1,0:T(8,128)(2,1)} %bitcast.7, bf16[1024,1024]{1,0:T(8,128)(2,1)} %bitcast.5, f32[2,128]{1,0:T(2,128)} %bitcast.9, bf16[27,128,128]{2,1,0:T(8,128)(2,1)} %bitcast.6, bf16[9,96,128]{2,1,0:T(8,128)(2,1)} %bitcast.8), custom_call_target="tpu_custom_call" | custom-call | tf_op jit(solution)/shard_map/pallas_call | solution.py:411
  37.4 1.3 %copy.7 = bf16[8,4,256]{2,1,0:T(4,128)(2,1)} copy(bf16[8,4,256]{2,1,0:T(4,128)(2,1)} %shard_map.55) | data formatting | bytes 32768

commit v19 on v18

--- a/solution.py
+++ b/solution.py
@@ -302,12 +302,15 @@
                 )
         return by_depth
 
+    if merged:
+        first_halo = halo_start(field_ref, held, send_sem, recv_sem)
     inner_rows(1, nx - 1, inner_taps(1, nx - 1, (0, 1, 2), done, ny), done, ny)
     low = inner_taps(0, 1, (1, 2))
     high = inner_taps(nx - 1, nx, (0, 1))
     if not merged:
         pl.semaphore_wait(barrier, expected)
-    halo_finish(halo_start(field_ref, held, send_sem, recv_sem))
+        first_halo = halo_start(field_ref, held, send_sem, recv_sem)
+    halo_finish(first_halo)
     inner_rows(0, 1, [a + b for a, b in zip(low, inner_taps(0, 1, (0,)))])
     inner_rows(nx - 1, nx, [a + b for a, b in zip(high, inner_taps(nx - 1, nx, (2,)))])
 

time: 39.4 us -> 38.1 us (0.967)
  Pallas kernels: 37.4 us -> 36.2 us
    pallas_call x1, Pallas kernels: 37.4 us -> 36.2 us  [decoder_block(): pl.pallas_call(whole_kernel, out_shape=jax.ShapeDtypeStruct((block, nx, n...]
where the time goes in v19:
time: 38.1 us; the launch traced here: 37.5 us
  Pallas kernels  36.2 us (95%)
  local copies, waits for them, and re-layouts  1.33 us (3%)
    pallas_call x1, Pallas kernels, decoder_block(): pl.pallas_call(whole_kernel, out_shape=jax.ShapeDtypeStruct((block, nx, n...  36.2 us
    unnamed x1, local copies, waits for them, and re-layouts  1.33 us

profile of v19, /device:TPU:3, one launch (start us, length us, event | category | flops | bytes accessed | tf_op | source)
XLA Modules:
  0.0 37.5 jit_solution(9121992898377805441)
XLA Ops:
  0.0 36.2 %shard_map.55 = bf16[8,4,256]{2,1,0:T(4,128)(2,1)} custom-call(bf16[128,1024]{1,0:T(8,128)(2,1)} %bitcast.7, bf16[1024,1024]{1,0:T(8,128)(2,1)} %bitcast.5, f32[2,128]{1,0:T(2,128)} %bitcast.9, bf16[27,128,128]{2,1,0:T(8,128)(2,1)} %bitcast.6, bf16[9,96,128]{2,1,0:T(8,128)(2,1)} %bitcast.8), custom_call_target="tpu_custom_call" | custom-call | tf_op jit(solution)/shard_map/pallas_call | solution.py:414
  36.2 1.3 %copy.7 = bf16[8,4,256]{2,1,0:T(4,128)(2,1)} copy(bf16[8,4,256]{2,1,0:T(4,128)(2,1)} %shard_map.55) | data formatting | bytes 32768

commit v20 on v19

--- a/solution.py
+++ b/solution.py
@@ -143,6 +143,8 @@
                 (out_ref.shape[0], 2) + out_ref.shape[2:], out_ref.dtype
             )
 
+        if hooks and "each" in hooks:
+            hooks["each"](slot)
         if hooks and slot in hooks:
             hooks[slot]()
 
@@ -167,7 +169,7 @@
     return (me > 0).astype(jnp.int32) + (me < count - 1).astype(jnp.int32)
 
 
-def halo_start(field_ref, held, send_sem, recv_sem):
+def halo_start(field_ref, held, send_sem, recv_sem, start=True):
     nx = field_ref.shape[0]
     count = lax.axis_size("inl")
     me = lax.axis_index("inl")
@@ -185,9 +187,11 @@
         sends = (me + step >= 0) & (me + step < count)
         gets = (me - step >= 0) & (me - step < count)
 
-        @pl.when(sends)
-        def _():
-            copy.start()
+        if start:
+
+            @pl.when(sends)
+            def _():
+                copy.start()
 
         @pl.when(jnp.logical_not(gets))
         def _():
@@ -303,7 +307,7 @@
         return by_depth
 
     if merged:
-        first_halo = halo_start(field_ref, held, send_sem, recv_sem)
+        first_halo = halo_start(field_ref, held, send_sem, recv_sem, start=False)
     inner_rows(1, nx - 1, inner_taps(1, nx - 1, (0, 1, 2), done, ny), done, ny)
     low = inner_taps(0, 1, (1, 2))
     high = inner_taps(nx - 1, nx, (0, 1))
@@ -393,9 +397,30 @@
         held[1 : nx + 1, 0 : done + 2] = brick[:, 0 : done + 2]
         inner_rows(1, nx - 1, inner_taps(1, nx - 1, (0, 1, 2), 0, done), 0, done)
 
+    send_halo, recv_halo = scratch[17], scratch[18]
+    count_x = lax.axis_size("inl")
+    me_x = lax.axis_index("inl")
+
+    def edge_rows(slot):
+        for index, step in enumerate((-1, 1)):
+            source, target = (0, nx + 1) if step < 0 else (nx - 1, 0)
+            rows = pl.ds(2 * slot, 2)
+            copy = pltpu.make_async_remote_copy(
+                src_ref=brick.at[source : source + 1, rows],
+                dst_ref=held.at[target : target + 1, rows],
+                send_sem=send_halo.at[index],
+                recv_sem=recv_halo.at[index],
+                device_id={"inl": me_x + step},
+                device_id_type=MESH,
+            )
+
+            @pl.when((me_x + step >= 0) & (me_x + step < count_x))
+            def _():
+                copy.start()
+
     gather_kernel(
         tokens_ref, weight_hbm, gains_ref, brick, weight, field, rows_in, send_rows, recv_rows, weight_sem, extra,
-        {done // 2: early},
+        {done // 2: early, "each": edge_rows},
     )
     loads[1].wait()
     block_kernel(True, done, brick, kernel_in, gains_ref, kernel_out, out_ref, *scratch[10:])

time: 38.1 us -> 37.3 us (0.979)
  Pallas kernels: 36.2 us -> 35.4 us
    pallas_call x1, Pallas kernels: 36.2 us -> 35.4 us  [decoder_block(): pl.pallas_call(whole_kernel, out_shape=jax.ShapeDtypeStruct((block, nx, n...]
where the time goes in v20:
time: 37.3 us; the launch traced here: 36.8 us
  Pallas kernels  35.4 us (95%)
  local copies, waits for them, and re-layouts  1.33 us (4%)
    pallas_call x1, Pallas kernels, decoder_block(): pl.pallas_call(whole_kernel, out_shape=jax.ShapeDtypeStruct((block, nx, n...  35.4 us
    unnamed x1, local copies, waits for them, and re-layouts  1.33 us

profile of v20, /device:TPU:3, one launch (start us, length us, event | category | flops | bytes accessed | tf_op | source)
XLA Modules:
  0.0 36.8 jit_solution(16182725419650154179)
XLA Ops:
  0.0 35.4 %shard_map.55 = bf16[8,4,256]{2,1,0:T(4,128)(2,1)} custom-call(bf16[128,1024]{1,0:T(8,128)(2,1)} %bitcast.7, bf16[1024,1024]{1,0:T(8,128)(2,1)} %bitcast.5, f32[2,128]{1,0:T(2,128)} %bitcast.9, bf16[27,128,128]{2,1,0:T(8,128)(2,1)} %bitcast.6, bf16[9,96,128]{2,1,0:T(8,128)(2,1)} %bitcast.8), custom_call_target="tpu_custom_call" | custom-call | tf_op jit(solution)/shard_map/pallas_call | solution.py:439
  35.4 1.3 %copy.7 = bf16[8,4,256]{2,1,0:T(4,128)(2,1)} copy(bf16[8,4,256]{2,1,0:T(4,128)(2,1)} %shard_map.55) | data formatting | bytes 32768

commit v21 on v20

--- a/solution.py
+++ b/solution.py
@@ -169,12 +169,13 @@
     return (me > 0).astype(jnp.int32) + (me < count - 1).astype(jnp.int32)
 
 
-def halo_start(field_ref, held, send_sem, recv_sem, start=True):
+def halo_start(field_ref, held, send_sem, recv_sem, start=True, steps=(-1, 1)):
     nx = field_ref.shape[0]
     count = lax.axis_size("inl")
     me = lax.axis_index("inl")
     copies = []
-    for index, step in enumerate((-1, 1)):
+    for step in steps:
+        index = 0 if step < 0 else 1
         source, target = (0, nx + 1) if step < 0 else (nx - 1, 0)
         copy = pltpu.make_async_remote_copy(
             src_ref=field_ref.at[source : source + 1],
@@ -290,10 +291,10 @@
 
     inner_taps, inner_rows = conv_in_rows(field_ref, kernel_in_ref, gains_ref, held, shifted, mixed)
 
-    def outer_rows(first, last):
+    def outer_rows(first, last, offsets_x=(0, 1, 2)):
         cells = (last - first) * ny_out * nz
         by_depth = jnp.zeros((cells, 3 * outch), jnp.float32)
-        for offset_x in range(3):
+        for offset_x in offsets_x:
             for offset_y in range(3):
                 window = held_out[first + offset_x : last + offset_x, offset_y : offset_y + ny_out].reshape(
                     cells, channels
@@ -316,7 +317,9 @@
         first_halo = halo_start(field_ref, held, send_sem, recv_sem)
     halo_finish(first_halo)
     inner_rows(0, 1, [a + b for a, b in zip(low, inner_taps(0, 1, (0,)))])
+    second_halo = halo_start(mixed, held_out, send_out, recv_out, steps=(-1,))
     inner_rows(nx - 1, nx, [a + b for a, b in zip(high, inner_taps(nx - 1, nx, (2,)))])
+    second_halo += halo_start(mixed, held_out, send_out, recv_out, steps=(1,))
 
     edge = jnp.zeros((nx * ny_out, 1, outch), jnp.float32)
     shifted_out[:, 0:1] = edge
@@ -359,13 +362,18 @@
             copy.wait_send()
         return result
 
-    copies = halo_start(mixed, held_out, send_out, recv_out)
     held_out[1 : nx + 1] = mixed[...]
     middle_sends = share(0, by_channel(outer_rows(1, nx - 1), nx - 2))
-    halo_finish(copies)
+    low_out = outer_rows(0, 1, (1, 2))
+    high_out = outer_rows(nx - 1, nx, (0, 1))
+    halo_finish(second_halo)
     row_cells = ny_out * nz
     ends = jnp.concatenate(
-        [by_channel(outer_rows(0, 1), 1), by_channel(outer_rows(nx - 1, nx), 1)], axis=1
+        [
+            by_channel(low_out + outer_rows(0, 1, (0,)), 1),
+            by_channel(high_out + outer_rows(nx - 1, nx, (2,)), 1),
+        ],
+        axis=1,
     )
     end_sends = share(1, ends)
     middle = gather(0, middle_sends)

time: 37.3 us -> 36.9 us (0.989)
  Pallas kernels: 35.4 us -> 34.9 us
    pallas_call x1, Pallas kernels: 35.4 us -> 34.9 us  [decoder_block(): pl.pallas_call(whole_kernel, out_shape=jax.ShapeDtypeStruct((block, nx, n...]
where the time goes in v21:
time: 36.9 us; the launch traced here: 36.2 us
  Pallas kernels  34.9 us (95%)
  local copies, waits for them, and re-layouts  1.33 us (4%)
    pallas_call x1, Pallas kernels, decoder_block(): pl.pallas_call(whole_kernel, out_shape=jax.ShapeDtypeStruct((block, nx, n...  34.9 us
    unnamed x1, local copies, waits for them, and re-layouts  1.33 us

profile of v21, /device:TPU:3, one launch (start us, length us, event | category | flops | bytes accessed | tf_op | source)
XLA Modules:
  0.0 36.2 jit_solution(3226359914278340102)
XLA Ops:
  0.0 34.9 %shard_map.55 = bf16[8,4,256]{2,1,0:T(4,128)(2,1)} custom-call(bf16[128,1024]{1,0:T(8,128)(2,1)} %bitcast.7, bf16[1024,1024]{1,0:T(8,128)(2,1)} %bitcast.5, f32[2,128]{1,0:T(2,128)} %bitcast.9, bf16[27,128,128]{2,1,0:T(8,128)(2,1)} %bitcast.6, bf16[9,96,128]{2,1,0:T(8,128)(2,1)} %bitcast.8), custom_call_target="tpu_custom_call" | custom-call | tf_op jit(solution)/shard_map/pallas_call | solution.py:447
  34.9 1.3 %copy.7 = bf16[8,4,256]{2,1,0:T(4,128)(2,1)} copy(bf16[8,4,256]{2,1,0:T(4,128)(2,1)} %shard_map.55) | data formatting | bytes 32768

commit v22 on v21

--- a/solution.py
+++ b/solution.py
@@ -394,16 +394,24 @@
     extra = entry_signals()
     held, shifted, mixed = scratch[10:13]
     nx, ny_in, nz, channels = brick.shape
-    done = ny_in // 2
+    ny = ny_in - 2
+    bounds = [2 * (ny // 6), 2 * (ny // 3)]
+    done = bounds[-1]
     inner_taps, inner_rows = conv_in_rows(brick, kernel_in, gains_ref, held, shifted, mixed)
 
-    def early():
-        loads[0].wait()
-        edge = jnp.zeros((shifted.shape[0], 1, channels), jnp.float32)
-        shifted[:, 0:1] = edge
-        shifted[:, nz + 1 : nz + 2] = edge
-        held[1 : nx + 1, 0 : done + 2] = brick[:, 0 : done + 2]
-        inner_rows(1, nx - 1, inner_taps(1, nx - 1, (0, 1, 2), 0, done), 0, done)
+    def chunk(low, high):
+        def run():
+            if low == 0:
+                loads[0].wait()
+                edge = jnp.zeros((shifted.shape[0], 1, channels), jnp.float32)
+                shifted[:, 0:1] = edge
+                shifted[:, nz + 1 : nz + 2] = edge
+                held[1 : nx + 1, 0 : high + 2] = brick[:, 0 : high + 2]
+            else:
+                held[1 : nx + 1, low + 2 : high + 2] = brick[:, low + 2 : high + 2]
+            inner_rows(1, nx - 1, inner_taps(1, nx - 1, (0, 1, 2), low, high), low, high)
+
+        return run
 
     send_halo, recv_halo = scratch[17], scratch[18]
     count_x = lax.axis_size("inl")
@@ -428,7 +436,7 @@
 
     gather_kernel(
         tokens_ref, weight_hbm, gains_ref, brick, weight, field, rows_in, send_rows, recv_rows, weight_sem, extra,
-        {done // 2: early, "each": edge_rows},
+        {bounds[0] // 2: chunk(0, bounds[0]), bounds[1] // 2: chunk(bounds[0], bounds[1]), "each": edge_rows},
     )
     loads[1].wait()
     block_kernel(True, done, brick, kernel_in, gains_ref, kernel_out, out_ref, *scratch[10:])

time: 36.9 us -> 37.3 us (1.011)
  the two profiles are of different devices: /device:TPU:3 before, /device:TPU:5 now
where the time goes in v22:
time: 37.3 us; the launch traced here: 37.1 us
  Pallas kernels  35.8 us (96%)
  local copies, waits for them, and re-layouts  1.33 us (4%)
    pallas_call x1, Pallas kernels, decoder_block(): pl.pallas_call(whole_kernel, out_shape=jax.ShapeDtypeStruct((block, nx, n...  35.8 us
    unnamed x1, local copies, waits for them, and re-layouts  1.33 us

profile of v22, /device:TPU:5, one launch (start us, length us, event | category | flops | bytes accessed | tf_op | source)
XLA Modules:
  0.0 37.1 jit_solution(10926975441516835011)
XLA Ops:
  0.0 35.8 %shard_map.55 = bf16[8,4,256]{2,1,0:T(4,128)(2,1)} custom-call(bf16[128,1024]{1,0:T(8,128)(2,1)} %bitcast.7, bf16[1024,1024]{1,0:T(8,128)(2,1)} %bitcast.5, f32[2,128]{1,0:T(2,128)} %bitcast.9, bf16[27,128,128]{2,1,0:T(8,128)(2,1)} %bitcast.6, bf16[9,96,128]{2,1,0:T(8,128)(2,1)} %bitcast.8), custom_call_target="tpu_custom_call" | custom-call | tf_op jit(solution)/shard_map/pallas_call | solution.py:455
  35.8 1.3 %copy.7 = bf16[8,4,256]{2,1,0:T(4,128)(2,1)} copy(bf16[8,4,256]{2,1,0:T(4,128)(2,1)} %shard_map.55) | data formatting | bytes 32768

commit v23 on v21

--- a/solution.py
+++ b/solution.py
@@ -362,7 +362,6 @@
             copy.wait_send()
         return result
 
-    held_out[1 : nx + 1] = mixed[...]
     middle_sends = share(0, by_channel(outer_rows(1, nx - 1), nx - 2))
     low_out = outer_rows(0, 1, (1, 2))
     high_out = outer_rows(nx - 1, nx, (0, 1))
@@ -392,7 +391,8 @@
     for load in loads:
         load.start()
     extra = entry_signals()
-    held, shifted, mixed = scratch[10:13]
+    held, shifted = scratch[10:12]
+    mixed = scratch[13].at[1 : brick.shape[0] + 1]
     nx, ny_in, nz, channels = brick.shape
     done = ny_in // 2
     inner_taps, inner_rows = conv_in_rows(brick, kernel_in, gains_ref, held, shifted, mixed)
@@ -431,7 +431,7 @@
         {done // 2: early, "each": edge_rows},
     )
     loads[1].wait()
-    block_kernel(True, done, brick, kernel_in, gains_ref, kernel_out, out_ref, *scratch[10:])
+    block_kernel(True, done, brick, kernel_in, gains_ref, kernel_out, out_ref, held, shifted, mixed, *scratch[13:])
 
 
 def decoder_block(tokens, weight, gains, kernel_in, kernel_out, collective):

time: 36.9 us -> 36.9 us (level)
  no operation moved by 1% of the time
where the time goes in v23:
time: 36.9 us; the launch traced here: 36.2 us
  Pallas kernels  34.9 us (95%)
  local copies, waits for them, and re-layouts  1.33 us (4%)
    pallas_call x1, Pallas kernels, decoder_block(): pl.pallas_call(whole_kernel, out_shape=jax.ShapeDtypeStruct((block, nx, n...  34.9 us
    unnamed x1, local copies, waits for them, and re-layouts  1.33 us

profile of v23, /device:TPU:3, one launch (start us, length us, event | category | flops | bytes accessed | tf_op | source)
XLA Modules:
  0.0 36.2 jit_solution(11766695430802852171)
XLA Ops:
  0.0 34.9 %shard_map.55 = bf16[8,4,256]{2,1,0:T(4,128)(2,1)} custom-call(bf16[128,1024]{1,0:T(8,128)(2,1)} %bitcast.7, bf16[1024,1024]{1,0:T(8,128)(2,1)} %bitcast.5, f32[2,128]{1,0:T(2,128)} %bitcast.9, bf16[27,128,128]{2,1,0:T(8,128)(2,1)} %bitcast.6, bf16[9,96,128]{2,1,0:T(8,128)(2,1)} %bitcast.8), custom_call_target="tpu_custom_call" | custom-call | tf_op jit(solution)/shard_map/pallas_call | solution.py:447
  34.9 1.3 %copy.7 = bf16[8,4,256]{2,1,0:T(4,128)(2,1)} copy(bf16[8,4,256]{2,1,0:T(4,128)(2,1)} %shard_map.55) | data formatting | bytes 32768

commit v24 on v21

--- a/solution.py
+++ b/solution.py
@@ -68,6 +68,8 @@
             pl.semaphore_signal(barrier, inc=1, device_id={"inl": source_x, "xln": source_y}, device_id_type=MESH)
 
     loading.wait()
+    if hooks and "loaded" in hooks:
+        hooks["loaded"]()
     upsampled = jnp.dot(tokens_ref[...], weight[...], preferred_element_type=jnp.float32)
     for group in range(upsampled.shape[1] // width):
         part = upsampled[:, group * width : (group + 1) * width]
@@ -389,9 +391,12 @@
         pltpu.make_async_copy(kernel_in_hbm, kernel_in, kernel_sem.at[0]),
         pltpu.make_async_copy(kernel_out_hbm, kernel_out, kernel_sem.at[1]),
     ]
-    for load in loads:
-        load.start()
     extra = entry_signals()
+
+    def start_loads():
+        for load in loads:
+            load.start()
+
     held, shifted, mixed = scratch[10:13]
     nx, ny_in, nz, channels = brick.shape
     done = ny_in // 2
@@ -428,7 +433,7 @@
 
     gather_kernel(
         tokens_ref, weight_hbm, gains_ref, brick, weight, field, rows_in, send_rows, recv_rows, weight_sem, extra,
-        {done // 2: early, "each": edge_rows},
+        {done // 2: early, "each": edge_rows, "loaded": start_loads},
     )
     loads[1].wait()
     block_kernel(True, done, brick, kernel_in, gains_ref, kernel_out, out_ref, *scratch[10:])

time: 36.9 us -> 36.9 us (level)
  no operation moved by 1% of the time
where the time goes in v24:
time: 36.9 us; the launch traced here: 36.2 us
  Pallas kernels  34.9 us (95%)
  local copies, waits for them, and re-layouts  1.33 us (4%)
    pallas_call x1, Pallas kernels, decoder_block(): pl.pallas_call(whole_kernel, out_shape=jax.ShapeDtypeStruct((block, nx, n...  34.9 us
    unnamed x1, local copies, waits for them, and re-layouts  1.33 us

profile of v24, /device:TPU:3, one launch (start us, length us, event | category | flops | bytes accessed | tf_op | source)
XLA Modules:
  0.0 36.2 jit_solution(12122367954536656679)
XLA Ops:
  0.0 34.9 %shard_map.55 = bf16[8,4,256]{2,1,0:T(4,128)(2,1)} custom-call(bf16[128,1024]{1,0:T(8,128)(2,1)} %bitcast.7, bf16[1024,1024]{1,0:T(8,128)(2,1)} %bitcast.5, f32[2,128]{1,0:T(2,128)} %bitcast.9, bf16[27,128,128]{2,1,0:T(8,128)(2,1)} %bitcast.6, bf16[9,96,128]{2,1,0:T(8,128)(2,1)} %bitcast.8), custom_call_target="tpu_custom_call" | custom-call | tf_op jit(solution)/shard_map/pallas_call | solution.py:452
  34.9 1.3 %copy.7 = bf16[8,4,256]{2,1,0:T(4,128)(2,1)} copy(bf16[8,4,256]{2,1,0:T(4,128)(2,1)} %shard_map.55) | data formatting | bytes 32768

commit v25 on v21

--- a/solution.py
+++ b/solution.py
@@ -446,7 +446,7 @@
     block = outch // count
     return pl.pallas_call(
         whole_kernel,
-        out_shape=jax.ShapeDtypeStruct((block, nx, ny_out * nz), jnp.bfloat16),
+        out_shape=jax.ShapeDtypeStruct((block, nx, ny_out * nz), jnp.float32),
         in_specs=[
             pl.BlockSpec(memory_space=pltpu.VMEM),
             pl.BlockSpec(memory_space=pl.ANY),
@@ -496,7 +496,7 @@
     assert tokens_here.shape[0] == inl_size * PXD * GZ
     taps, outch, channels_in = conv_out.shape[1:]
     out_weight = conv_out[0].reshape(taps // 3, 3 * outch, channels_in)
-    return decoder_block(tokens_here, weight, gains, conv_in[0], out_weight, 3)
+    return decoder_block(tokens_here, weight, gains, conv_in[0], out_weight, 3).astype(jnp.bfloat16)
 
 
 def solution(mesh):

time: 36.9 us -> 36.9 us (level)
  other arithmetic: 0 us -> 1.37 us
  local copies, waits for them, and re-layouts: 1.33 us -> 0 us
    convert_element_type x0 -> x1, other arithmetic: none -> 1.37 us  [local(): decoder_block(tokens_here, weight, gains, conv_in[0], out_weight, 3)]
    unnamed x1 -> x0, local copies, waits for them, and re-layouts: 1.33 us -> none
where the time goes in v25:
time: 36.9 us; the launch traced here: 36.2 us
  Pallas kernels  34.9 us (95%)
  other arithmetic  1.37 us (4%)
    pallas_call x1, Pallas kernels, decoder_block(): pl.pallas_call(whole_kernel, out_shape=jax.ShapeDtypeStruct((block, nx, n...  34.9 us
    convert_element_type x1, other arithmetic, local(): decoder_block(tokens_here, weight, gains, conv_in[0], out_weight, 3)  1.37 us

profile of v25, /device:TPU:3, one launch (start us, length us, event | category | flops | bytes accessed | tf_op | source)
XLA Modules:
  0.0 36.2 jit_solution(7239070441692595016)
XLA Ops:
  0.0 34.9 %shard_map.55 = f32[8,4,256]{2,1,0:T(4,128)} custom-call(bf16[128,1024]{1,0:T(8,128)(2,1)} %bitcast.7, bf16[1024,1024]{1,0:T(8,128)(2,1)} %bitcast.5, f32[2,128]{1,0:T(2,128)} %bitcast.9, bf16[27,128,128]{2,1,0:T(8,128)(2,1)} %bitcast.6, bf16[9,96,128]{2,1,0:T(8,128)(2,1)} %bitcast.8), custom_call_target="tpu_custom_call" | custom-call | tf_op jit(solution)/shard_map/pallas_call | solution.py:447
  34.9 1.4 %convert_element_type.3 = bf16[8,4,256]{2,1,0:T(4,128)(2,1)} convert(f32[8,4,256]{2,1,0:T(4,128)} %shard_map.55) | non-fusion elementwise | flops 8192 | bytes 49152 | tf_op jit(solution)/shard_map/convert_element_type | solution.py:499

commit v26 on v21

--- a/solution.py
+++ b/solution.py
@@ -86,13 +86,22 @@
     interleave = jnp.where(same, 1.0, 0.0).astype(jnp.bfloat16)
 
     def place(slot, block):
+        pairs = jnp.concatenate(
+            [
+                jnp.concatenate(
+                    [block[:, ((u * 2 + v) * 2 + w) * width : ((u * 2 + v) * 2 + w + 1) * width] for u in range(2) for v in range(2)],
+                    axis=1,
+                )
+                for w in range(2)
+            ],
+            axis=0,
+        )
+        cells = jnp.dot(interleave, pairs, preferred_element_type=jnp.float32).astype(out_ref.dtype)
         for u in range(2):
             for v in range(2):
-                first = ((u * 2 + v) * 2) * width
-                pair = jnp.concatenate([block[:, first : first + width], block[:, first + width : first + 2 * width]], axis=0)
-                cells = jnp.dot(interleave, pair, preferred_element_type=jnp.float32).astype(out_ref.dtype)
+                column = (u * 2 + v) * width
                 for ix in range(2):
-                    out_ref[2 * ix + u, 2 * slot + v] = cells[ix * depth : (ix + 1) * depth]
+                    out_ref[2 * ix + u, 2 * slot + v] = cells[ix * depth : (ix + 1) * depth, column : column + width]
 
     pl.semaphore_wait(barrier, expected + extra)
     copies = []

time: 36.9 us -> 36.9 us (level)
  no operation moved by 1% of the time
where the time goes in v26:
time: 36.9 us; the launch traced here: 36.2 us
  Pallas kernels  34.9 us (95%)
  local copies, waits for them, and re-layouts  1.33 us (4%)
    pallas_call x1, Pallas kernels, decoder_block(): pl.pallas_call(whole_kernel, out_shape=jax.ShapeDtypeStruct((block, nx, n...  34.9 us
    unnamed x1, local copies, waits for them, and re-layouts  1.33 us

profile of v26, /device:TPU:3, one launch (start us, length us, event | category | flops | bytes accessed | tf_op | source)
XLA Modules:
  0.0 36.2 jit_solution(5905413129182673362)
XLA Ops:
  0.0 34.9 %shard_map.55 = bf16[8,4,256]{2,1,0:T(4,128)(2,1)} custom-call(bf16[128,1024]{1,0:T(8,128)(2,1)} %bitcast.7, bf16[1024,1024]{1,0:T(8,128)(2,1)} %bitcast.5, f32[2,128]{1,0:T(2,128)} %bitcast.9, bf16[27,128,128]{2,1,0:T(8,128)(2,1)} %bitcast.6, bf16[9,96,128]{2,1,0:T(8,128)(2,1)} %bitcast.8), custom_call_target="tpu_custom_call" | custom-call | tf_op jit(solution)/shard_map/pallas_call | solution.py:456
  34.9 1.3 %copy.7 = bf16[8,4,256]{2,1,0:T(4,128)(2,1)} copy(bf16[8,4,256]{2,1,0:T(4,128)(2,1)} %shard_map.55) | data formatting | bytes 32768
